TPU v7x, 256 devices: a whole 4x4x8 slice. The times are simulated.
256 devices in a mesh: dp: 2 (over y_hi), ctx: 64 (over x, z, core), head: 2 (over y_lo).
Axes of the slice: x: 4, y: 4 (y_hi: 2, y_lo: 2; y = y_hi * 2 + y_lo), z: 8, core: 2. Of those that a mesh axis runs over, the one named last changes fastest.
Arguments:
- queries: bfloat16 [8192, 4, 1024], P('ctx', ('dp', 'head')), may hold values from -5 to 5
- keys: bfloat16 [8192, 4, 128], P(('ctx', 'head', 'dp')), may hold values from -5 to 5
- values: bfloat16 [8192, 4, 128], P(('ctx', 'head', 'dp')), may hold values from -6 to 6
- outputs: bfloat16 [8192, 4, 1024], P('ctx', ('dp', 'head')), may hold values from -3 to 3
- grad_out: bfloat16 [8192, 4, 1024], P('ctx', ('dp', 'head')), may hold values from -6 to 6
- doc_ids: int32 [8192], P('ctx'), may hold values from 0 to 3, never falling along the last dimension, each value on 1 to 4096 neighbouring positions
- owner: int32 [2048], P('ctx'), may hold values from 0 to 63, as said below
Outputs:
- grad_q_planned: bfloat16 [8192, 4, 1024], P('ctx', ('dp', 'head'))
- grad_k: bfloat16 [8192, 4, 128], P('ctx', ('dp', 'head'))
- grad_v: bfloat16 [8192, 4, 128], P('ctx', ('dp', 'head'))
Inputs may be any that keep to these rules, and one draw needn't show every extreme that they name: `owner`: blocks b with the same b // 32 have different owners, and blocks with the same b % 32 have different owners, so every index of ctx owns exactly 32 blocks, one for each value of b % 32.
All inputs are finite; a program needn't handle non-finite values.
Results may differ from a plain program's by a relative error of at most 0.0047.
The roundings to bfloat16 on the way count: a program that leaves them out, or rounds other values in their place, can miss the bound.
Values may be sent and summed in bfloat16 or wider, within the bound.
No kernel may reach another device: no remote copies, remote signals or barrier semaphores. Data moves between devices by JAX's collectives and lax.ppermute only.
A program may use at most 64 MiB of HBM per device.

v0:
```python
import jax
import jax.numpy as jnp
from jax import lax
from jax.sharding import PartitionSpec as P

NEG_FILL = -1e30


def as_heads(block, head_dim):
    return block.reshape(block.shape[0], block.shape[1], block.shape[2] // head_dim, head_dim)


def visible_mask(q_pos, q_doc, key_start, key_doc):
    key_pos = key_start + jnp.arange(key_doc.shape[0], dtype=jnp.int32)
    return (key_doc[None, :] == q_doc[:, None]) & (key_pos[None, :] <= q_pos[:, None])


def raw_scores(q_heads, key_block, scale_val):
    return (
        jnp.einsum("rgid,kgd->girk", q_heads, key_block, preferred_element_type=jnp.float32)
        * scale_val
    )


def softmax_totals(q_heads, all_keys, all_docs, q_pos, q_doc, scale_val, key_step):
    last_query = jnp.max(q_pos)
    shape = (q_heads.shape[1], q_heads.shape[2], q_heads.shape[0])

    def visit(block_index, state):
        key_start = block_index * key_step

        def work(inner):
            peak, total = inner
            key_block = lax.dynamic_slice_in_dim(all_keys, key_start, key_step, 0)
            key_doc = lax.dynamic_slice_in_dim(all_docs, key_start, key_step, 0)
            visible = visible_mask(q_pos, q_doc, key_start, key_doc)[None, None]
            scores = raw_scores(q_heads, key_block, scale_val)
            fresh = jnp.maximum(peak, jnp.max(jnp.where(visible, scores, NEG_FILL), axis=-1))
            weights = jnp.where(visible, jnp.exp(scores - fresh[..., None]), 0.0)
            return (fresh, total * jnp.exp(peak - fresh) + jnp.sum(weights, axis=-1))

        return lax.cond(key_start <= last_query, work, lambda inner: inner, state)

    start_state = (jnp.full(shape, NEG_FILL, jnp.float32), jnp.zeros(shape, jnp.float32))
    peak, total = lax.fori_loop(0, all_keys.shape[0] // key_step, visit, start_state)
    return peak + jnp.log(total)


def block_terms(
    q_heads,
    do_heads,
    key_block,
    value_block,
    key_start,
    key_doc,
    q_pos,
    q_doc,
    lse,
    delta,
    scale_val,
):
    visible = visible_mask(q_pos, q_doc, key_start, key_doc)[None, None]
    scores = raw_scores(q_heads, key_block, scale_val)
    probs = jnp.where(visible, jnp.exp(scores - lse[..., None]), 0.0)
    dprob = jnp.einsum("rgid,kgd->girk", do_heads, value_block, preferred_element_type=jnp.float32)
    dscore = (probs * (dprob - delta[..., None]) * scale_val).astype(jnp.bfloat16)
    return (probs.astype(jnp.bfloat16), dscore)


def body(queries, keys, values, outputs, grad_out, doc_ids, owner):
    head_dim = keys.shape[2]
    scale_val = head_dim ** (-0.5)
    row_count = queries.shape[0]
    peer_count = lax.axis_size("ctx")
    per_device = owner.shape[0]
    block_len = row_count // per_device
    near_keys, near_values = (
        lax.all_to_all(
            lax.all_to_all(keys, "dp", split_axis=1, concat_axis=0, tiled=True),
            "head",
            split_axis=1,
            concat_axis=0,
            tiled=True,
        ),
        lax.all_to_all(
            lax.all_to_all(values, "dp", split_axis=1, concat_axis=0, tiled=True),
            "head",
            split_axis=1,
            concat_axis=0,
            tiled=True,
        ),
    )
    all_keys, all_values, all_docs = (
        lax.all_gather(near_keys, "ctx", axis=0, tiled=True),
        lax.all_gather(near_values, "ctx", axis=0, tiled=True),
        lax.all_gather(doc_ids, "ctx", axis=0, tiled=True),
    )
    total_len = all_keys.shape[0]
    kv_local = all_keys.shape[1]
    key_step = min(512, total_len)
    slot_ids = jnp.arange(per_device, dtype=jnp.int32)
    peer_ids = jnp.arange(peer_count, dtype=jnp.int32)
    send_hot = owner[None, :] == peer_ids[:, None]
    send_tag = jnp.sum(jnp.where(send_hot, slot_ids[None, :] + 1, 0), axis=1, keepdims=True)
    send_mat = send_hot.astype(jnp.bfloat16)
    q_rows, do_rows, o_rows = (queries, grad_out, outputs)
    q_pos = lax.axis_index("ctx") * row_count + jnp.arange(row_count, dtype=jnp.int32)
    q_doc = jnp.take(all_docs, q_pos)
    q_heads = as_heads(q_rows, head_dim)
    do_heads = as_heads(do_rows, head_dim)
    o_heads = as_heads(o_rows, head_dim)
    delta = jnp.transpose(
        jnp.sum(do_heads.astype(jnp.float32) * o_heads.astype(jnp.float32), axis=-1), (1, 2, 0)
    )
    lse = softmax_totals(q_heads, all_keys, all_docs, q_pos, q_doc, scale_val, key_step)
    last_query = jnp.max(q_pos)

    def grads_at(key_start, size):
        key_block = lax.dynamic_slice_in_dim(all_keys, key_start, size, 0)
        value_block = lax.dynamic_slice_in_dim(all_values, key_start, size, 0)
        key_doc = lax.dynamic_slice_in_dim(all_docs, key_start, size, 0)
        probs_low, dscore = block_terms(
            q_heads,
            do_heads,
            key_block,
            value_block,
            key_start,
            key_doc,
            q_pos,
            q_doc,
            lse,
            delta,
            scale_val,
        )
        return (key_block, probs_low, dscore)

    def key_grads(probs_low, dscore):
        dk_block = jnp.einsum("girk,rgid->kgd", dscore, q_heads, preferred_element_type=jnp.float32)
        dv_block = jnp.einsum(
            "girk,rgid->kgd", probs_low, do_heads, preferred_element_type=jnp.float32
        )
        return jnp.concatenate([dk_block, dv_block], axis=-1)

    def query_grads(dscore, key_block):
        return jnp.einsum("girk,kgd->rgid", dscore, key_block, preferred_element_type=jnp.float32)

    dq_zero = jnp.zeros(q_heads.shape, jnp.float32)

    def visit_all(block_index, state):
        key_start = block_index * key_step

        def work(inner):
            dq_sum, key_sum = inner
            key_block, probs_low, dscore = grads_at(key_start, key_step)
            dq_sum = dq_sum + query_grads(dscore, key_block)
            key_sum = lax.dynamic_update_slice_in_dim(
                key_sum, key_grads(probs_low, dscore), key_start, 0
            )
            return (dq_sum, key_sum)

        return lax.cond(key_start <= last_query, work, lambda inner: inner, state)

    key_zero = jnp.zeros((total_len, kv_local, 2 * head_dim), jnp.float32)
    dq_sum, key_sum = lax.fori_loop(0, total_len // key_step, visit_all, (dq_zero, key_zero))
    combined = lax.psum_scatter(key_sum, "ctx", scatter_dimension=0, tiled=True)
    dq_low = dq_sum.reshape(row_count, kv_local, -1).astype(jnp.bfloat16)
    blocks = dq_low.reshape((per_device, block_len) + dq_low.shape[1:])
    dq_recv = lax.all_to_all(
        jnp.einsum("pj,jbgw->pbgw", send_mat, blocks, preferred_element_type=jnp.float32).astype(
            jnp.bfloat16
        ),
        "ctx",
        split_axis=0,
        concat_axis=0,
        tiled=True,
    )
    tag_recv = lax.all_to_all(send_tag, "ctx", split_axis=0, concat_axis=0, tiled=True)
    pick_hot = tag_recv[:, 0][None, :] == slot_ids[:, None] + 1
    pick_hot, pick_mat = (pick_hot, pick_hot.astype(jnp.bfloat16))
    placed = jnp.einsum(
        "jp,pbgw->jbgw", pick_mat, dq_recv, preferred_element_type=jnp.float32
    ).astype(jnp.bfloat16)
    dq_out = placed.reshape((row_count,) + dq_recv.shape[2:])
    grad_k = combined[..., :head_dim].astype(jnp.bfloat16)
    grad_v = combined[..., head_dim:].astype(jnp.bfloat16)
    return (dq_out, grad_k, grad_v)


def solution(mesh):
    placed = (
        P("ctx", ("dp", "head"), None),
        P(("ctx", "head", "dp"), None, None),
        P(("ctx", "head", "dp"), None, None),
        P("ctx", ("dp", "head"), None),
        P("ctx", ("dp", "head"), None),
        P("ctx"),
        P("ctx"),
    )
    return jax.shard_map(
        body,
        mesh=mesh,
        in_specs=placed,
        out_specs=(
            P("ctx", ("dp", "head"), None),
            P("ctx", ("dp", "head"), None),
            P("ctx", ("dp", "head"), None),
        ),
        check_vma=False,
    )
```

profile of v0, /device:TPU:2, one launch (start us, length us, event | category | flops | bytes accessed | tf_op | source)
XLA Modules:
  0.0 459.7 jit_solution(2822669787318124813)
XLA Ops:
  8.0 9.7 %all_to_all.86 = bf16[32,4,128]{2,0,1:T(8,128)(2,1)S(1)} all-to-all(bf16[32,4,128]{2,0,1:T(8,128)(2,1)S(1)} %copy.85), channel_id=1, replica_groups=mesh['dp'=2,'ctx'=64,'head'=2] {'dp'}, dimensions={1} | all-to-all | bytes 65536 | tf_op jit(solution)/shard_map/all_to_all | solution.py:79
  17.7 7.0 %all_to_all.87 = bf16[64,2,128]{2,0,1:T(8,128)(2,1)} all-to-all(bf16[64,2,128]{2,0,1:T(8,128)(2,1)S(1)} %bitcast.159), channel_id=1, replica_groups=mesh['dp'=2,'ctx'=64,'head'=2] {'head'}, dimensions={1} | all-to-all | bytes 65536 | tf_op jit(solution)/shard_map/all_to_all | solution.py:78
  25.5 7.8 %all_to_all.88 = bf16[32,4,128]{2,0,1:T(8,128)(2,1)S(1)} all-to-all(bf16[32,4,128]{2,0,1:T(8,128)(2,1)S(1)} %copy.89), channel_id=1, replica_groups=mesh['dp'=2,'ctx'=64,'head'=2] {'dp'}, dimensions={1} | all-to-all | bytes 65536 | tf_op jit(solution)/shard_map/all_to_all | solution.py:86
  33.3 7.0 %all_to_all.89 = bf16[64,2,128]{2,0,1:T(8,128)(2,1)} all-to-all(bf16[64,2,128]{2,0,1:T(8,128)(2,1)S(1)} %bitcast.161), channel_id=1, replica_groups=mesh['dp'=2,'ctx'=64,'head'=2] {'head'}, dimensions={1} | all-to-all | bytes 65536 | tf_op jit(solution)/shard_map/all_to_all | solution.py:85
  43.6 42.3 %all-gather = s32[64,1,128]{2,1,0:T(1,128)S(1)} all-gather(s32[1,1,128]{2,1,0:T(1,128)S(1)} %bitcast.163), channel_id=1, replica_groups=mesh['dp'=2,'ctx'=64,'head'=2] {'ctx'}, dimensions={0}, use_global_device_ids=true | all-gather | bytes 33280 | tf_op jit(solution)/shard_map/all_gather | solution.py:96
  87.2 14.4 %all-gather.4.cloned.1.call-done = bf16[8192,1,128]{2,0,1:T(8,128)(2,1)} async-done(((bf16[128,1,128]{2,0,1:T(8,128)(2,1)}), bf16[8192,1,128]{2,0,1:T(8,128)(2,1)}) %all-gather.4.cloned.1.call-update) | async-done | bytes 2097168 | tf_op jit(solution)/shard_map/all_gather | solution.py:94
  101.6 22.0 %while.32 = (s32[]{:T(128)}, f32[1,8,128]{2,1,0:T(8,128)S(1)}, f32[1,8,128]{2,1,0:T(8,128)S(1)}, s32[]{:T(128)}, s32[8192]{0:T(1024)S(1)}, /*index=5*/s32[128]{0...) while((s32[]{:T(128)}, f32[1,8,128]{2,1,0:T(8,128)S(1)}, ...), condition=%wide.region_7.8_spmd.clone, body=%wide.region_2.7_spmd.clone.sunk | while | flops 138087040 | bytes 4850481 | solution.py:45
  102.3 2.2 conditional.6
  105.1 2.2 conditional.6
  108.0 2.2 conditional.6
  110.9 2.2 conditional.6
  113.8 2.2 conditional.6
  114.1 1.4 fusion.4
  123.7 55.7 %all-gather.6.cloned.1.call-done = bf16[8192,1,128]{2,0,1:T(8,128)(2,1)} async-done(((bf16[128,1,128]{2,0,1:T(8,128)(2,1)}), bf16[8192,1,128]{2,0,1:T(8,128)(2,1)}) %all-gather.6.cloned.1.call-update) | async-done | bytes 2097168 | tf_op jit(solution)/shard_map/all_gather | solution.py:95
  179.4 4.2 broadcast_in_dim.77
  183.6 42.3 %while.33 = (s32[]{:T(128)}, f32[128,1,8,128]{0,3,2,1:T(8,128)S(1)}, f32[8192,1,256]{0,2,1:T(8,128)}, s32[]{:T(128)}, bf16[8192,1,128]{2,0,1:T(8,128)(2,1)}, /*i...) while((s32[]{:T(128)}, ...), condition=%wide.region_12.13_spmd.clone, body=%wide.region_9.12_spmd.clone.sunk | while | flops 675742336 | bytes 13652861 | solution.py:164
  184.3 6.3 %conditional.7 = ((f32[128,1,8,128]{0,3,2,1:T(8,128)S(1)}, f32[8192,1,256]{0,2,1:T(8,128)})) conditional(s32[]{:T(128)} %convert_element_type.101, (f32[128,1,8,128]{0,3,2,1:T(8,128)S(1)}, f32[8192,1,256]{0,2,1:T(8,128)}) %tuple.92, (s32[]{:T(128)}, bf16[8192,1,128]{2,0,1:T(8,128)(2,1)}, s32[8192]{0:T(1024)S(1)}, s32[128]{0:T(128)S(1)}, ...), branch_computations={%region_10.10_spmd, %region_11.11_spmd} | conditional | flops 675742336 | bytes 13652054 | solution.py:161
  184.6 1.5 fusion.17
  191.2 6.3 %conditional.7 = ((f32[128,1,8,128]{0,3,2,1:T(8,128)S(1)}, f32[8192,1,256]{0,2,1:T(8,128)})) conditional(s32[]{:T(128)} %convert_element_type.101, (f32[128,1,8,128]{0,3,2,1:T(8,128)S(1)}, f32[8192,1,256]{0,2,1:T(8,128)}) %tuple.92, (s32[]{:T(128)}, bf16[8192,1,128]{2,0,1:T(8,128)(2,1)}, s32[8192]{0:T(1024)S(1)}, s32[128]{0:T(128)S(1)}, ...), branch_computations={%region_10.10_spmd, %region_11.11_spmd} | conditional | flops 675742336 | bytes 13652054 | solution.py:161
  191.5 1.5 fusion.17
  198.1 6.2 %conditional.7 = ((f32[128,1,8,128]{0,3,2,1:T(8,128)S(1)}, f32[8192,1,256]{0,2,1:T(8,128)})) conditional(s32[]{:T(128)} %convert_element_type.101, (f32[128,1,8,128]{0,3,2,1:T(8,128)S(1)}, f32[8192,1,256]{0,2,1:T(8,128)}) %tuple.92, (s32[]{:T(128)}, bf16[8192,1,128]{2,0,1:T(8,128)(2,1)}, s32[8192]{0:T(1024)S(1)}, s32[128]{0:T(128)S(1)}, ...), branch_computations={%region_10.10_spmd, %region_11.11_spmd} | conditional | flops 675742336 | bytes 13652054 | solution.py:161
  198.5 1.5 fusion.17
  205.0 6.2 %conditional.7 = ((f32[128,1,8,128]{0,3,2,1:T(8,128)S(1)}, f32[8192,1,256]{0,2,1:T(8,128)})) conditional(s32[]{:T(128)} %convert_element_type.101, (f32[128,1,8,128]{0,3,2,1:T(8,128)S(1)}, f32[8192,1,256]{0,2,1:T(8,128)}) %tuple.92, (s32[]{:T(128)}, bf16[8192,1,128]{2,0,1:T(8,128)(2,1)}, s32[8192]{0:T(1024)S(1)}, s32[128]{0:T(128)S(1)}, ...), branch_computations={%region_10.10_spmd, %region_11.11_spmd} | conditional | flops 675742336 | bytes 13652054 | solution.py:161
  205.4 1.5 fusion.17
  211.9 6.2 %conditional.7 = ((f32[128,1,8,128]{0,3,2,1:T(8,128)S(1)}, f32[8192,1,256]{0,2,1:T(8,128)})) conditional(s32[]{:T(128)} %convert_element_type.101, (f32[128,1,8,128]{0,3,2,1:T(8,128)S(1)}, f32[8192,1,256]{0,2,1:T(8,128)}) %tuple.92, (s32[]{:T(128)}, bf16[8192,1,128]{2,0,1:T(8,128)(2,1)}, s32[8192]{0:T(1024)S(1)}, s32[128]{0:T(128)S(1)}, ...), branch_computations={%region_10.10_spmd, %region_11.11_spmd} | conditional | flops 675742336 | bytes 13652054 | solution.py:161
  212.3 1.5 fusion.17
  225.9 9.0 %copy.98 = f32[8192,1,256]{2,0,1:T(8,128)} copy(f32[8192,1,256]{0,2,1:T(8,128)} %get-tuple-element.456) | data formatting | bytes 16777216 | tf_op jit(solution)/shard_map/while | solution.py:164
  236.4 74.3 %all-to-all-start = ((s32[64,1,1]{2,1,0:T(1,128)}), s32[64,1,1]{2,1,0:T(1,128)S(1)}, u32[]{:S(2)}, u32[]{:S(2)}) async-start(s32[64,1,1]{2,1,0:T(1,128)} %copy.84), calls=%async_computation | async-start | bytes 65536 | tf_op jit(solution)/shard_map/all_to_all | solution.py:177
  312.6 6.6 %all-to-all-done = s32[64,1,1]{2,1,0:T(1,128)S(1)} async-done(((s32[64,1,1]{2,1,0:T(1,128)}), s32[64,1,1]{2,1,0:T(1,128)S(1)}, u32[]{:S(2)}, u32[]{:S(2)}) %all-to-all-start) | async-done | bytes 288 | tf_op jit(solution)/shard_map/all_to_all | solution.py:177
  319.2 5.5 %all-to-all-start.5 = ((bf16[64,4,1,1024]{3,1,2,0:T(4,128)(2,1)}), bf16[64,4,1,1024]{3,1,2,0:T(4,128)(2,1)S(1)}, u32[]{:S(2)}, u32[]{:S(2)}) async-start(bf16[64,4,1,1024]{3,1,2,0:T(4,128)(2,1)} %copy.95), calls=%async_computation.5 | async-start | bytes 1048576 | tf_op jit(solution)/shard_map/all_to_all | solution.py:168
  326.0 15.5 %all-to-all-done.5 = bf16[64,4,1,1024]{3,1,2,0:T(4,128)(2,1)S(1)} async-done(((bf16[64,4,1,1024]{3,1,2,0:T(4,128)(2,1)}), bf16[64,4,1,1024]{3,1,2,0:T(4,128)(2,1)S(1)}, u32[]{:S(2)}, u32[]{:S(2)}) %all-to-all-start.5) | async-done | bytes 524320 | tf_op jit(solution)/shard_map/all_to_all | solution.py:168
  342.9 108.8 %reduce-scatter.2.cloned.1.call-done = f32[128,1,256]{2,0,1:T(8,128)} async-done(((f32[8192,1,256]{2,0,1:T(8,128)}), f32[128,1,256]{2,0,1:T(8,128)}) %reduce-scatter.2.cloned.1.call-update) | async-done | bytes 131088 | tf_op jit(solution)/shard_map/reduce_scatter | solution.py:165
  (187 shorter events, 46.9 us)
Async XLA Ops:
  7.2 36.3 %copy-start = (bf16[128,1,1024]{2,0,1:T(8,128)(2,1)S(1)}, bf16[128,1,1024]{2,0,1:T(8,128)(2,1)}, u32[]{:S(2)}) copy-start(bf16[128,1,1024]{2,0,1:T(8,128)(2,1)} %param.18) | copy-start | bytes 786436
  7.2 36.4 %copy-start.1 = (s32[128]{0:T(128)S(1)}, s32[128]{0:T(128)}, u32[]{:S(2)}) copy-start(s32[128]{0:T(128)} %param.20) | copy-start | bytes 1540
  7.2 94.4 %all-gather.4.cloned.1.call-start = ((), (), s32[]{:S(2)}) async-start(), calls=%async_computation.7 | async-start | bytes 2129920 | tf_op jit(solution)/shard_map/all_gather | solution.py:94
  24.7 154.6 %all-gather.6.cloned.1.call-start = ((), (), s32[]{:S(2)}) async-start(), calls=%async_computation.8 | async-start | bytes 2129920 | tf_op jit(solution)/shard_map/all_gather | solution.py:95
  40.3 411.3 %reduce-scatter.2.cloned.1.call-start = ((), (), s32[]{:S(2)}) async-start(), calls=%async_computation.9 | async-start | bytes 8519680 | tf_op jit(solution)/shard_map/reduce_scatter | solution.py:165
  234.9 0.7 copy-start.2
  236.4 82.8 %all-to-all-start = ((s32[64,1,1]{2,1,0:T(1,128)}), s32[64,1,1]{2,1,0:T(1,128)S(1)}, u32[]{:S(2)}, u32[]{:S(2)}) async-start(s32[64,1,1]{2,1,0:T(1,128)} %copy.84), calls=%async_computation | async-start | bytes 65536 | tf_op jit(solution)/shard_map/all_to_all | solution.py:177
  319.2 22.2 %all-to-all-start.5 = ((bf16[64,4,1,1024]{3,1,2,0:T(4,128)(2,1)}), bf16[64,4,1,1024]{3,1,2,0:T(4,128)(2,1)S(1)}, u32[]{:S(2)}, u32[]{:S(2)}) async-start(bf16[64,4,1,1024]{3,1,2,0:T(4,128)(2,1)} %copy.95), calls=%async_computation.5 | async-start | bytes 1048576 | tf_op jit(solution)/shard_map/all_to_all | solution.py:168
Sparse Core Ops, SparseCore 0:
  24.8 76.7 all-gather.3
  104.4 74.9 all-gather.5
  235.1 216.5 reduce-scatter.1
where the time goes:
time: 463 us; the launch traced here: 460 us
  waiting for transfers between devices  201 us (43%)
  starting transfers between devices  79.9 us (17%)
  blocking collectives  73.8 us (16%)
  matrix products  32.7 us (7%)
  local copies, waits for them, and re-layouts  23.8 us (5%)
  loops' own time  22.9 us (5%)
  between operations  13.9 us (3%)
  other arithmetic  11.7 us (3%)
    reduce_scatter x1, waiting for transfers between devices, body(): combined = lax.psum_scatter(key_sum, 'ctx', scatter_dimension=0, tiled=True)  109 us
    all_to_all x1, starting transfers between devices, body(): lax.all_to_all(send_tag, 'ctx', split_axis=0, concat_axis=0, tiled=True)  74.3 us
    all_gather x1, waiting for transfers between devices, body(): lax.all_gather(near_values, 'ctx', axis=0, tiled=True)  55.7 us
    all_gather x1, blocking collectives, body(): lax.all_gather(doc_ids, 'ctx', axis=0, tiled=True)  42.3 us
    all_to_all x1, waiting for transfers between devices, body(): lax.all_to_all(jnp.einsum('pj,jbgw->pbgw', send_mat, blocks, preferred_el...  15.5 us
    all_gather x1, waiting for transfers between devices, body(): lax.all_gather(near_keys, 'ctx', axis=0, tiled=True)  14.4 us
    dot_general x10, matrix products, raw_scores(): jnp.einsum('rgid,kgd->girk', q_heads, key_block, preferred_element_type=j...  14.1 us
    another operation x1, loops' own time, softmax_totals(): lax.fori_loop(0, all_keys.shape[0] // key_step, visit, start_state)  10.9 us
  transfers between devices with their start and end apart: 5, of which 5 were waited for; matrix products, arithmetic and copies ran while one was open for 5% of the time, Pallas kernels for 0%

commit v1 on v0

v1 whole, which is shorter than its diff:
```python
import functools

import jax
import jax.numpy as jnp
from jax import lax
from jax.experimental import pallas as pl
from jax.experimental.pallas import tpu as pltpu
from jax.sharding import Mesh, PartitionSpec as P

NEG_FILL = -1e30
BF = jnp.bfloat16
F32 = jnp.float32
EXTRA = 8


def nt(a, b):
    return lax.dot_general(a, b, (((1,), (1,)), ((), ())), preferred_element_type=F32)


def nn(a, b):
    return lax.dot_general(a, b, (((1,), (0,)), ((), ())), preferred_element_type=F32)


def tn(a, b):
    return lax.dot_general(a, b, (((0,), (0,)), ((), ())), preferred_element_type=F32)


def attention_kernel(
    place_ref,
    q_ref,
    do_ref,
    o_ref,
    doc_ref,
    own_ref,
    other_ref,
    dq_ref,
    own_grad_ref,
    other_grad_ref,
    q_all,
    do_all,
    p_all,
    peaks,
    state,
    dq_sum,
    *,
    zs,
    slots,
    scale,
    tile,
):
    rows, width = q_ref.shape
    hd = own_ref.shape[2] // 2
    heads = width // hd
    total = heads * rows
    chips = slots * zs
    x, z, core = place_ref[0], place_ref[1], place_ref[2]
    base = place_ref[3]
    exist = place_ref[4]
    here = (slots - 1) * zs + z

    def add_counts(j, tot):
        return (
            tot
            + own_ref[j, rows : rows + EXTRA, :].astype(F32)
            + other_ref[j, rows : rows + EXTRA, :].astype(F32)
        )

    counts = lax.fori_loop(0, chips, add_counts, jnp.zeros((EXTRA, 2 * hd), F32))
    doc = doc_ref[...]
    first_row = jnp.zeros((1, rows), F32)
    for d in range(1, EXTRA):
        first_row = jnp.where(doc == d, counts[d : d + 1, :rows], first_row)
    first_row = first_row.astype(jnp.int32) + exist
    lo_key = jnp.min(first_row)
    lo = jnp.maximum((lo_key - base) // (2 * rows), 0)
    q_pos = base + (here * 2 + core) * rows + lax.broadcasted_iota(jnp.int32, (1, rows), 1)
    firsts = jnp.concatenate([first_row] * (tile // rows), axis=1)
    lasts = jnp.concatenate([q_pos] * (tile // rows), axis=1)

    deltas = []
    for n in range(heads):
        cols = slice(n * hd, (n + 1) * hd)
        q_all[n * rows : (n + 1) * rows, :] = q_ref[:, cols]
        do_all[n * rows : (n + 1) * rows, :] = do_ref[:, cols]
        prod = do_ref[:, cols].astype(F32) * o_ref[:, cols].astype(F32)
        state[2:3, n * rows : (n + 1) * rows] = jnp.sum(prod.T, axis=0, keepdims=True)
    state[0:1, :] = jnp.full((1, total), NEG_FILL, F32)
    state[1:2, :] = jnp.zeros((1, total), F32)
    dq_sum[...] = jnp.zeros_like(dq_sum)

    key_iota = lax.broadcasted_iota(jnp.int32, (rows, tile), 0)

    def see(j, c, s):
        key_pos = key_iota + (base + (j * 2 + c) * rows)
        return jnp.where((key_pos >= firsts) & (key_pos <= lasts), s, NEG_FILL)

    def first_pass(j, carry):
        slot = j - lo
        k_own = own_ref[j, :rows, :hd]
        k_other = other_ref[j, :rows, :hd]
        for t in range(total // tile):
            cols = slice(t * tile, (t + 1) * tile)
            q_t = q_all[cols, :]
            s_own = see(j, core, nt(k_own, q_t))
            s_other = see(j, 1 - core, nt(k_other, q_t))
            old = state[0:1, cols]
            peak = jnp.maximum(
                old,
                jnp.maximum(
                    jnp.max(s_own, axis=0, keepdims=True), jnp.max(s_other, axis=0, keepdims=True)
                ),
            )
            p_own = jnp.exp((s_own - peak) * scale)
            p_other = jnp.exp((s_other - peak) * scale)
            p_all[slot, :rows, cols] = p_own
            p_all[slot, rows:, cols] = p_other
            state[1:2, cols] = (
                state[1:2, cols] * jnp.exp((old - peak) * scale)
                + jnp.sum(p_own, axis=0, keepdims=True)
                + jnp.sum(p_other, axis=0, keepdims=True)
            )
            state[0:1, cols] = peak
            peaks[slot, 0:1, cols] = peak
        return carry

    lax.fori_loop(lo, here + 1, first_pass, 0)
    state[1:2, :] = 1.0 / state[1:2, :]

    def second_pass(j, carry):
        slot = j - lo
        k_own = own_ref[j, :rows, :hd]
        k_other = other_ref[j, :rows, :hd]
        kk = jnp.concatenate([k_own, k_other], axis=0)
        vv = jnp.concatenate([own_ref[j, :rows, hd:], other_ref[j, :rows, hd:]], axis=0)
        dk = jnp.zeros((2 * rows, hd), F32)
        dv = jnp.zeros((2 * rows, hd), F32)
        for t in range(total // tile):
            cols = slice(t * tile, (t + 1) * tile)
            do_t = do_all[cols, :]
            factor = jnp.exp((peaks[slot, 0:1, cols] - state[0:1, cols]) * scale) * state[1:2, cols]
            probs = p_all[slot, :, cols] * factor
            dprob = nt(vv, do_t)
            dscore = (probs * (dprob - state[2:3, cols]) * scale).astype(BF)
            dv = dv + nn(probs.astype(BF), do_t)
            dk = dk + nn(dscore, q_all[cols, :])
            dq_sum[:, cols] += tn(kk, dscore)
        own_grad_ref[j, :, :hd] = dk[:rows]
        own_grad_ref[j, :, hd:] = dv[:rows]
        other_grad_ref[j, :, :hd] = dk[rows:]
        other_grad_ref[j, :, hd:] = dv[rows:]
        return carry

    lax.fori_loop(lo, here + 1, second_pass, 0)

    def clear(j, carry):
        own_grad_ref[j] = jnp.zeros((rows, 2 * hd), F32)
        other_grad_ref[j] = jnp.zeros((rows, 2 * hd), F32)
        return carry

    lax.fori_loop(0, lo, clear, 0)
    lax.fori_loop(here + 1, chips, clear, 0)
    for n in range(heads):
        dq_ref[:, n * hd : (n + 1) * hd] = dq_sum[:, n * rows : (n + 1) * rows].T.astype(BF)


def attention(place, q, do, o, doc, own, other, zs, slots, scale):
    rows, width = q.shape
    hd = own.shape[2] // 2
    total = rows * (width // hd)
    chips = slots * zs
    reach = (slots - 1) * zs + 1
    vmem = pl.BlockSpec(memory_space=pltpu.VMEM)
    return pl.pallas_call(
        functools.partial(
            attention_kernel, zs=zs, slots=slots, scale=scale, tile=min(256, total)
        ),
        in_specs=[pl.BlockSpec(memory_space=pltpu.SMEM)] + [vmem] * 6,
        out_specs=[vmem] * 3,
        out_shape=[
            jax.ShapeDtypeStruct((rows, width), BF),
            jax.ShapeDtypeStruct((chips, rows, 2 * hd), F32),
            jax.ShapeDtypeStruct((chips, rows, 2 * hd), F32),
        ],
        scratch_shapes=[
            pltpu.VMEM((total, hd), BF),
            pltpu.VMEM((total, hd), BF),
            pltpu.VMEM((reach, 2 * rows, total), F32),
            pltpu.VMEM((reach, 8, total), F32),
            pltpu.VMEM((8, total), F32),
            pltpu.VMEM((hd, total), F32),
        ],
        compiler_params=pltpu.CompilerParams(vmem_limit_bytes=56 * 1024 * 1024),
        name="attention_backward",
    )(place, q, do, o, doc, own, other)


def body(queries, keys, values, outputs, grad_out, doc_ids, owner):
    hd = keys.shape[2]
    scale = hd**-0.5
    rows, _, width = queries.shape
    xs, zs = lax.axis_size("x"), lax.axis_size("z")
    x, z, core = lax.axis_index("x"), lax.axis_index("z"), lax.axis_index("core")
    peers = xs * zs * 2
    slots = xs // 2 + 1
    per_device = owner.shape[0]
    block_len = rows // per_device

    near = lax.all_to_all(
        jnp.concatenate([keys, values], axis=-1), ("dp", "head"), split_axis=1, concat_axis=0, tiled=True
    )
    part = keys.shape[0]
    near = near.reshape(2, 2, part, 2 * hd).transpose(1, 0, 2, 3).reshape(rows, 2 * hd)
    earlier = jnp.sum(
        (doc_ids[None, :] < jnp.arange(EXTRA, dtype=jnp.int32)[:, None]).astype(F32), axis=1, keepdims=True
    )
    near = jnp.concatenate([near, jnp.broadcast_to(earlier, (EXTRA, 2 * hd)).astype(BF)], axis=0)

    line = lax.all_gather(near, "z", axis=0, tiled=False)
    shifted = [
        lax.ppermute(line, "x", [(i, i + s) for i in range(xs - s)]) for s in range(slots - 1, 0, -1)
    ]
    own = jnp.concatenate(shifted + [line], axis=0)
    other = lax.ppermute(own, "core", [(0, 1), (1, 0)])

    base = (x - (slots - 1)) * (zs * 2 * rows)
    place = jnp.stack([x, z, core, base, jnp.maximum(base, 0)]).astype(jnp.int32)
    dq, own_grad, other_grad = attention(
        place,
        queries.reshape(rows, width),
        grad_out.reshape(rows, width),
        outputs.reshape(rows, width),
        doc_ids.reshape(1, rows),
        own,
        other,
        zs,
        slots,
        scale,
    )

    swapped = lax.ppermute(other_grad, "core", [(0, 1), (1, 0)])
    summed = (own_grad + swapped).reshape(slots, zs, rows, 2 * hd)
    mine = summed[slots - 1]
    for s in range(1, slots):
        mine = mine + lax.ppermute(
            summed[slots - 1 - s].astype(BF), "x", [(i, i - s) for i in range(s, xs)]
        ).astype(F32)
    spread = lax.all_to_all(mine.astype(BF), "z", split_axis=0, concat_axis=0, tiled=True)
    grads = jnp.sum(spread.astype(F32), axis=0).astype(BF)
    grad_k = grads[:, None, :hd]
    grad_v = grads[:, None, hd:]

    slot_ids = jnp.arange(per_device, dtype=jnp.int32)
    send_mat = (owner[None, :] == jnp.arange(peers, dtype=jnp.int32)[:, None]).astype(BF)
    tags = jnp.broadcast_to((slot_ids + 1)[:, None, None], (per_device, block_len, 128)).astype(BF)
    blocks = jnp.concatenate([dq.reshape(per_device, block_len, width), tags], axis=-1)
    packed = jnp.einsum("pj,jbw->pbw", send_mat, blocks, preferred_element_type=F32).astype(BF)
    arrived = lax.all_to_all(packed, ("x", "z", "core"), split_axis=0, concat_axis=0, tiled=True)
    tag = arrived[:, 0, width].astype(jnp.int32)
    pick = (tag[None, :] == slot_ids[:, None] + 1).astype(BF)
    placed = jnp.einsum(
        "jp,pbw->jbw", pick, arrived[:, :, :width], preferred_element_type=F32
    ).astype(BF)
    return (placed.reshape(rows, 1, width), grad_k, grad_v)


def solution(mesh):
    sizes = mesh.shape
    dp, ctx, head = sizes["dp"], sizes["ctx"], sizes["head"]
    xs = 4
    fine = Mesh(
        mesh.devices.reshape(dp, xs, ctx // (2 * xs), 2, head), ("dp", "x", "z", "core", "head")
    )
    ctx_axes = ("x", "z", "core")
    heads = P(ctx_axes, ("dp", "head"), None)
    tokens = P(ctx_axes + ("head", "dp"), None, None)
    return jax.shard_map(
        body,
        mesh=fine,
        in_specs=(heads, tokens, tokens, heads, heads, P(ctx_axes), P(ctx_axes)),
        out_specs=(heads, heads, heads),
        check_vma=False,
    )
```

time: 463 us -> 165 us (0.36)
  waiting for transfers between devices: 201 us -> 58 us
  blocking collectives: 73.8 us -> 29.1 us
  matrix products: 32.7 us -> 0.88 us
  starting transfers between devices: 79.9 us -> 48.5 us
  loops' own time: 22.9 us -> 0 us
  local copies, waits for them, and re-layouts: 23.8 us -> 8.97 us
  between operations: 13.9 us -> 0.8 us
  Pallas kernels: 0 us -> 9.09 us
    reduce_scatter x1 -> x0, waiting for transfers between devices: 109 us -> none  [body(): combined = lax.psum_scatter(key_sum, 'ctx', scatter_dimension=0, tiled=True)]
    all_gather x2 -> x0, waiting for transfers between devices: 70.1 us -> none  [the longest x1 55.7 us: body(): lax.all_gather(near_values, 'ctx', axis=0, tiled=True)]
    ppermute x0 -> x6, waiting for transfers between devices: none -> 40.7 us  [the longest x2 28.4 us: body(): lax.ppermute(summed[slots - 1 - s].astype(BF), 'x', [(i, i - s) for i in...]
    all_to_all x2 -> x3, starting transfers between devices: 79.8 us -> 39.3 us  [the longest x1 28.3 us: body(): lax.all_to_all(packed, ('x', 'z', 'core'), split_axis=0, concat_axis=0, t...]
    dot_general x32 -> x2, matrix products: 32.7 us -> 0.88 us  [the longest x1 0.45 us: body(): jnp.einsum('jp,pbw->jbw', pick, arrived[:, :, :width], preferred_element_...]
    all_to_all x4 -> x0, blocking collectives: 31.4 us -> none  [the longest x1 9.7 us: body(): lax.all_to_all(keys, 'dp', split_axis=1, concat_axis=0, tiled=True)]
    another operation x34 -> x0, loops' own time: 22.9 us -> none  [the longest x1 10.9 us: softmax_totals(): lax.fori_loop(0, all_keys.shape[0] // key_step, visit, start_state)]
    all_gather x1, blocking collectives: 42.3 us -> 29.1 us  [body(): line = lax.all_gather(near, 'z', axis=0, tiled=False)]
  transfers between devices with their start and end apart: 5 -> 9, of which waited for: 5 -> 6; matrix products, arithmetic and copies ran while one was open for 5% -> 8% of each run, Pallas kernels for 0% -> 0%
where the time goes in v1:
time: 165 us; the launch traced here: 163 us
  waiting for transfers between devices  58 us (35%)
  starting transfers between devices  48.5 us (29%)
  blocking collectives  29.1 us (18%)
  Pallas kernels  9.09 us (6%)
  local copies, waits for them, and re-layouts  8.97 us (5%)
  other arithmetic  7.29 us (4%)
    all_gather x1, blocking collectives, body(): line = lax.all_gather(near, 'z', axis=0, tiled=False)  29.1 us
    ppermute x2, waiting for transfers between devices, body(): lax.ppermute(summed[slots - 1 - s].astype(BF), 'x', [(i, i - s) for i in...  28.4 us
    all_to_all x1, starting transfers between devices, body(): lax.all_to_all(packed, ('x', 'z', 'core'), split_axis=0, concat_axis=0, t...  28.3 us
    all_to_all x1, waiting for transfers between devices, body(): lax.all_to_all(mine.astype(BF), 'z', split_axis=0, concat_axis=0, tiled=T...  12.5 us
    ppermute x2, waiting for transfers between devices, body(): lax.ppermute(line, 'x', [(i, i + s) for i in range(xs - s)])  9.48 us
    pallas_call x1, Pallas kernels, attention(): pl.pallas_call(functools.partial(attention_kernel, zs=zs, slots=slots, sc...  9.09 us
    all_to_all x1, starting transfers between devices, body(): lax.all_to_all(mine.astype(BF), 'z', split_axis=0, concat_axis=0, tiled=T...  6.46 us
    ppermute x2, starting transfers between devices, body(): lax.ppermute(line, 'x', [(i, i + s) for i in range(xs - s)])  5.34 us
  transfers between devices with their start and end apart: 9, of which 6 were waited for; matrix products, arithmetic and copies ran while one was open for 8% of the time, Pallas kernels for 0%

profile of v1, /device:TPU:2, one launch (start us, length us, event | category | flops | bytes accessed | tf_op | source)
XLA Modules:
  0.0 162.6 jit_solution(1490273039541031989)
XLA Ops:
  0.6 0.8 copy.22
  1.4 0.8 copy.23
  2.2 0.6 pad_maximum_fusion.2
  2.8 4.5 %all-to-all-start = ((bf16[32,4,256]{2,0,1:T(8,128)(2,1)}), bf16[32,4,256]{2,0,1:T(8,128)(2,1)S(1)}, u32[]{:S(2)}, u32[]{:S(2)}) async-start(bf16[32,4,256]{2,0,1:T(8,128)(2,1)} %pad_maximum_fusion.2), calls=%async_computation | async-start | bytes 131072 | tf_op jit(solution)/shard_map/all_to_all | solution.py:208
  7.3 0.8 convert_reduce_fusion
  8.0 4.8 %all-to-all-done = bf16[32,4,256]{2,0,1:T(8,128)(2,1)S(1)} async-done(((bf16[32,4,256]{2,0,1:T(8,128)(2,1)}), bf16[32,4,256]{2,0,1:T(8,128)(2,1)S(1)}, u32[]{:S(2)}, u32[]{:S(2)}) %all-to-all-start) | async-done | bytes 65568 | tf_op jit(solution)/shard_map/all_to_all | solution.py:208
  13.0 29.1 %all-gather = bf16[1088,256]{1,0:T(8,128)(2,1)S(1)} all-gather(bf16[136,256]{1,0:T(8,128)(2,1)S(1)} %pad_maximum_fusion.1), channel_id=2, replica_groups=mesh['dp'=2,'x'=4,'z'=8,'core'=2,'head'=2] {'z'}, dimensions={0}, use_global_device_ids=true | all-gather | bytes 626688 | tf_op jit(solution)/shard_map/all_gather | solution.py:218
  42.1 3.4 %collective-permute-start.1 = (bf16[8,136,256]{2,1,0:T(8,128)(2,1)S(1)}, bf16[8,136,256]{2,1,0:T(8,128)(2,1)S(1)}, u32[]{:S(2)}, u32[]{:S(2)}) collective-permute-start(bf16[8,136,256]{2,1,0:T(8,128)(2,1)S(1)} %bitcast.28), channel_id=1, source_target_pairs={{0,32},{32,64},{64,96},{1,33},{33,65},{65,97},{2,34},{34,66},{66,9... | collective-permute-start | bytes 1671176 | tf_op jit(solution)/shard_map/ppermute | solution.py:220
  45.5 2.0 %collective-permute-start = (bf16[8,136,256]{2,1,0:T(8,128)(2,1)S(1)}, bf16[8,136,256]{2,1,0:T(8,128)(2,1)S(1)}, u32[]{:S(2)}, u32[]{:S(2)}) collective-permute-start(bf16[8,136,256]{2,1,0:T(8,128)(2,1)S(1)} %bitcast.29), channel_id=1, source_target_pairs={{0,64},{32,96},{1,65},{33,97},{2,66},{34,98},{3,67},{35,99},{4,68}... | collective-permute-start | bytes 1671176 | tf_op jit(solution)/shard_map/ppermute | solution.py:220
  47.4 9.5 %collective-permute-done.1 = bf16[8,136,256]{2,1,0:T(8,128)(2,1)S(1)} collective-permute-done((bf16[8,136,256]{2,1,0:T(8,128)(2,1)S(1)}, bf16[8,136,256]{2,1,0:T(8,128)(2,1)S(1)}, u32[]{:S(2)}, u32[]{:S(2)}) %collective-permute-start.1) | collective-permute-done | bytes 557088 | tf_op jit(solution)/shard_map/ppermute | solution.py:220
  57.2 0.7 stack.23.place_ref
  58.0 2.8 %collective-permute-done.2.other_ref = bf16[24,136,256]{2,1,0:T(8,128)(2,1)S(1)} collective-permute-done((bf16[24,136,256]{2,1,0:T(8,128)(2,1)S(1)}, bf16[24,136,256]{2,1,0:T(8,128)(2,1)S(1)}, u32[]{:S(2)}, u32[]{:S(2)}) %collective-permute-start.2) | collective-permute-done | bytes 1671200 | tf_op jit(solution)/shard_map/ppermute | solution.py:223
  60.7 1.3 copy-done.2
  62.0 9.1 %attention_backward.1 = (bf16[128,1024]{1,0:T(8,128)(2,1)}, f32[24,128,256]{2,1,0:T(8,128)}, f32[24,128,256]{2,1,0:T(8,128)}) custom-call(s32[5]{0:T(128)} %stack.23.place_ref, bf16[128,1024]{1,0:T(8,128)(2,1)} %bitcast.31, bf16[128,1024]{1,0:T(8,128)(2,1)} %bitcast.32, bf16[128,1024]{1,0:T(8,128)(2,1)} %bitcast.33, s32[1,128]{1,0:T(1,128)} %bitcast.36, ...), custom_call_target="tpu_custom_call" | custom-call | tf_op jit(solution)/shard_map/attention_backward/pallas_call | solution.py:173
  71.2 1.1 reshape.63
  72.5 0.4 convolution_convert_fusion
  72.9 1.3 copy.26
  74.2 28.3 %all-to-all-start.1 = ((bf16[64,4,1152]{2,1,0:T(4,128)(2,1)}), bf16[64,4,1152]{2,1,0:T(4,128)(2,1)}, u32[]{:S(2)}, u32[]{:S(2)}) async-start(bf16[64,4,1152]{2,1,0:T(4,128)(2,1)} %copy.26), calls=%async_computation.1 | async-start | bytes 1179648 | tf_op jit(solution)/shard_map/all_to_all | solution.py:257
  102.5 2.5 %fusion.16 = (bf16[24,128,256]{2,1,0:T(8,128)(2,1)S(1)}, f32[24,128,256]{2,1,0:T(8,128)S(1)}) fusion(f32[24,128,256]{2,1,0:T(8,128)S(1)} %copy-done.1, f32[24,128,256]{2,1,0:T(8,128)} %collective-permute-done.3), kind=kLoop, calls=%fused_computation.28 | loop fusion | flops 1572864 | bytes 11010048 | tf_op jit(solution)/shard_map/convert.3
  105.1 2.4 %collective-permute-start.4 = (bf16[8,128,256]{2,1,0:T(8,128)(2,1)S(1)}, bf16[8,128,256]{2,1,0:T(8,128)(2,1)S(1)}, u32[]{:S(2)}, u32[]{:S(2)}) collective-permute-start(bf16[8,128,256]{2,1,0:T(8,128)(2,1)S(1)} %get-tuple-element.11), channel_id=1, source_target_pairs={{32,0},{64,32},{96,64},{33,1},{65,33},{97,65},{34,2},{66,34},{98,6... | collective-permute-start | bytes 1572872 | tf_op jit(solution)/shard_map/ppermute | solution.py:244
  107.5 1.3 collective-permute-start.5
  108.8 16.5 %collective-permute-done.4 = bf16[8,128,256]{2,1,0:T(8,128)(2,1)S(1)} collective-permute-done((bf16[8,128,256]{2,1,0:T(8,128)(2,1)S(1)}, bf16[8,128,256]{2,1,0:T(8,128)(2,1)S(1)}, u32[]{:S(2)}, u32[]{:S(2)}) %collective-permute-start.4) | collective-permute-done | bytes 524320 | tf_op jit(solution)/shard_map/ppermute | solution.py:244
  125.3 11.9 %collective-permute-done.5 = bf16[8,128,256]{2,1,0:T(8,128)(2,1)S(1)} collective-permute-done((bf16[8,128,256]{2,1,0:T(8,128)(2,1)S(1)}, bf16[8,128,256]{2,1,0:T(8,128)(2,1)S(1)}, u32[]{:S(2)}, u32[]{:S(2)}) %collective-permute-start.5) | collective-permute-done | bytes 524320 | tf_op jit(solution)/shard_map/ppermute | solution.py:244
  137.2 1.0 fusion.1
  138.3 6.5 %all-to-all-start.2 = ((bf16[8,128,256]{2,1,0:T(8,128)(2,1)}), bf16[8,128,256]{2,1,0:T(8,128)(2,1)S(1)}, u32[]{:S(2)}, u32[]{:S(2)}) async-start(bf16[8,128,256]{2,1,0:T(8,128)(2,1)} %fusion.1), calls=%async_computation.2 | async-start | bytes 1048576 | tf_op jit(solution)/shard_map/all_to_all | solution.py:247
  144.7 1.2 slice.34
  146.0 2.1 %fusion.6 = s32[64]{0:T(128)S(1)} fusion(bf16[64,4,1152]{2,1,0:T(4,128)(2,1)} %all-to-all-done.1), kind=kLoop, calls=%fused_computation.15 | loop fusion | flops 64 | bytes 384 | tf_op jit(solution)/shard_map/convert_element_type | solution.py:258
  148.0 0.5 convolution_convert_fusion.1
  148.5 0.2 copy.28
  148.7 0.8 reshape.64
  149.5 12.5 %all-to-all-done.2 = bf16[8,128,256]{2,1,0:T(8,128)(2,1)S(1)} async-done(((bf16[8,128,256]{2,1,0:T(8,128)(2,1)}), bf16[8,128,256]{2,1,0:T(8,128)(2,1)S(1)}, u32[]{:S(2)}, u32[]{:S(2)}) %all-to-all-start.2) | async-done | bytes 524320 | tf_op jit(solution)/shard_map/all_to_all | solution.py:247
  162.0 0.6 slice_bitcast_fusion
  (22 shorter events, 0.8 us)
Async XLA Ops:
  2.8 10.1 %all-to-all-start = ((bf16[32,4,256]{2,0,1:T(8,128)(2,1)}), bf16[32,4,256]{2,0,1:T(8,128)(2,1)S(1)}, u32[]{:S(2)}, u32[]{:S(2)}) async-start(bf16[32,4,256]{2,0,1:T(8,128)(2,1)} %pad_maximum_fusion.2), calls=%async_computation | async-start | bytes 131072 | tf_op jit(solution)/shard_map/all_to_all | solution.py:208
  42.1 14.8 %collective-permute-start.1 = (bf16[8,136,256]{2,1,0:T(8,128)(2,1)S(1)}, bf16[8,136,256]{2,1,0:T(8,128)(2,1)S(1)}, u32[]{:S(2)}, u32[]{:S(2)}) collective-permute-start(bf16[8,136,256]{2,1,0:T(8,128)(2,1)S(1)} %bitcast.28), channel_id=1, source_target_pairs={{0,32},{32,64},{64,96},{1,33},{33,65},{65,97},{2,34},{34,66},{66,9... | collective-permute-start | bytes 1671176 | tf_op jit(solution)/shard_map/ppermute | solution.py:220
  45.5 11.4 %collective-permute-start = (bf16[8,136,256]{2,1,0:T(8,128)(2,1)S(1)}, bf16[8,136,256]{2,1,0:T(8,128)(2,1)S(1)}, u32[]{:S(2)}, u32[]{:S(2)}) collective-permute-start(bf16[8,136,256]{2,1,0:T(8,128)(2,1)S(1)} %bitcast.29), channel_id=1, source_target_pairs={{0,64},{32,96},{1,65},{33,97},{2,66},{34,98},{3,67},{35,99},{4,68}... | collective-permute-start | bytes 1671176 | tf_op jit(solution)/shard_map/ppermute | solution.py:220
  57.1 3.7 %copy-start = (bf16[24,136,256]{2,1,0:T(8,128)(2,1)}, bf16[24,136,256]{2,1,0:T(8,128)(2,1)S(1)}, u32[]{:S(2)}) copy-start(bf16[24,136,256]{2,1,0:T(8,128)(2,1)S(1)} %pad_maximum_fusion.own_ref) | copy-start | bytes 5013508
  57.1 3.6 %collective-permute-start.2 = (bf16[24,136,256]{2,1,0:T(8,128)(2,1)S(1)}, bf16[24,136,256]{2,1,0:T(8,128)(2,1)S(1)}, u32[]{:S(2)}, u32[]{:S(2)}) collective-permute-start(bf16[24,136,256]{2,1,0:T(8,128)(2,1)S(1)} %pad_maximum_fusion.own_ref), channel_id=1, source_target_pairs={{0,2},{2,0},{1,3},{3,1},{4,6},{6,4},{5,7},{7,5},{8,10},{10,8},{9,1... | collective-permute-start | bytes 5013512 | tf_op jit(solution)/shard_map/ppermute | solution.py:223
  60.7 1.3 copy-start.2
  62.0 10.5 %copy-start.3 = (s32[32]{0:T(128)S(1)}, s32[32]{0:T(128)}, u32[]{:S(2)}) copy-start(s32[32]{0:T(128)} %param.13) | copy-start | bytes 388
  71.1 31.4 %collective-permute-start.3 = (f32[24,128,256]{2,1,0:T(8,128)}, f32[24,128,256]{2,1,0:T(8,128)}, u32[]{:S(2)}, u32[]{:S(2)}) collective-permute-start(f32[24,128,256]{2,1,0:T(8,128)} %get-tuple-element.8), channel_id=1, source_target_pairs={{0,2},{2,0},{1,3},{3,1},{4,6},{6,4},{5,7},{7,5},{8,10},{10,8},{9,1... | collective-permute-start | bytes 9437192 | tf_op jit(solution)/shard_map/ppermute | solution.py:240
  72.4 30.2 %copy-start.1 = (f32[24,128,256]{2,1,0:T(8,128)S(1)}, f32[24,128,256]{2,1,0:T(8,128)}, u32[]{:S(2)}) copy-start(f32[24,128,256]{2,1,0:T(8,128)} %get-tuple-element.7) | copy-start | bytes 9437188
  74.2 64.1 %all-to-all-start.1 = ((bf16[64,4,1152]{2,1,0:T(4,128)(2,1)}), bf16[64,4,1152]{2,1,0:T(4,128)(2,1)}, u32[]{:S(2)}, u32[]{:S(2)}) async-start(bf16[64,4,1152]{2,1,0:T(4,128)(2,1)} %copy.26), calls=%async_computation.1 | async-start | bytes 1179648 | tf_op jit(solution)/shard_map/all_to_all | solution.py:257
  105.1 20.2 %collective-permute-start.4 = (bf16[8,128,256]{2,1,0:T(8,128)(2,1)S(1)}, bf16[8,128,256]{2,1,0:T(8,128)(2,1)S(1)}, u32[]{:S(2)}, u32[]{:S(2)}) collective-permute-start(bf16[8,128,256]{2,1,0:T(8,128)(2,1)S(1)} %get-tuple-element.11), channel_id=1, source_target_pairs={{32,0},{64,32},{96,64},{33,1},{65,33},{97,65},{34,2},{66,34},{98,6... | collective-permute-start | bytes 1572872 | tf_op jit(solution)/shard_map/ppermute | solution.py:244
  107.5 29.7 %collective-permute-start.5 = (bf16[8,128,256]{2,1,0:T(8,128)(2,1)S(1)}, bf16[8,128,256]{2,1,0:T(8,128)(2,1)S(1)}, u32[]{:S(2)}, u32[]{:S(2)}) collective-permute-start(bf16[8,128,256]{2,1,0:T(8,128)(2,1)S(1)} %get-tuple-element.12), channel_id=1, source_target_pairs={{64,0},{96,32},{65,1},{97,33},{66,2},{98,34},{67,3},{99,35},{68,4}... | collective-permute-start | bytes 1572872 | tf_op jit(solution)/shard_map/ppermute | solution.py:244
  138.3 23.7 %all-to-all-start.2 = ((bf16[8,128,256]{2,1,0:T(8,128)(2,1)}), bf16[8,128,256]{2,1,0:T(8,128)(2,1)S(1)}, u32[]{:S(2)}, u32[]{:S(2)}) async-start(bf16[8,128,256]{2,1,0:T(8,128)(2,1)} %fusion.1), calls=%async_computation.2 | async-start | bytes 1048576 | tf_op jit(solution)/shard_map/all_to_all | solution.py:247

commit v2 on v1

v2 whole, which is shorter than its diff:
```python
import functools
import math

import jax
import jax.numpy as jnp
from jax import lax
from jax.experimental import pallas as pl
from jax.experimental.pallas import tpu as pltpu
from jax.sharding import Mesh, PartitionSpec as P


NEG_FILL = -1e30
BF = jnp.bfloat16
F32 = jnp.float32
EXTRA = 8


def nt(a, b):
    return lax.dot_general(a, b, (((1,), (1,)), ((), ())), preferred_element_type=F32)


def nn(a, b):
    return lax.dot_general(a, b, (((1,), (0,)), ((), ())), preferred_element_type=F32)


def stack_heads(dst, src):
    rows, width = src.shape
    hd = dst.shape[1]
    for n in range(width // hd):
        dst[n * rows : (n + 1) * rows, :] = src[:, n * hd : (n + 1) * hd]


def fill_window(win, own, other, far_own, far_other, z, zs):
    rows = win.shape[1] // 2
    for half, near, far in ((0, own, far_own), (1, other, far_other)):
        cut = pl.ds(half * rows, rows)
        for zz in range(zs):
            win[zs + zz, cut, :] = near[zz, 0, :rows, :]
            win[jnp.where(zz > z, zz, 2 * zs + zz), cut, :] = near[zz, 1, :rows, :]
        win[z, cut, :] = far


def out_index(j, z, zs):
    zz = lax.rem(j, zs)
    middle = (j >= zs) & (j < 2 * zs)
    return jnp.where(middle, 2 * zz, jnp.where(j == z, 2 * zs, 2 * zz + 1))


def softmax_kernel(
    place_ref,
    q_ref,
    do_ref,
    doc_ref,
    k_own,
    k_other,
    far_own,
    far_other,
    dv_own,
    dv_other,
    p_out,
    info_ref,
    q_all,
    do_all,
    k_win,
    p_all,
    peaks,
    state,
    sems,
    *,
    zs,
    scale,
    tile,
):
    rows, _ = q_ref.shape
    hd = q_all.shape[1]
    total = q_all.shape[0]
    x, z, core = place_ref[0], place_ref[1], place_ref[2]
    base, reach = place_ref[3], place_ref[4]
    here = 2 * zs + z
    unit = scale * math.log2(math.e)

    stack_heads(q_all, q_ref)
    stack_heads(do_all, do_ref)
    fill_window(k_win, k_own, k_other, far_own[:rows, :], far_other[:rows, :], z, zs)

    near_ok = (x >= 1).astype(F32)
    far_ok = (x >= 2).astype(F32)
    counts = (
        far_own[rows : rows + EXTRA, :].astype(F32) + far_other[rows : rows + EXTRA, :].astype(F32)
    ) * far_ok
    for zz in range(zs):
        both = k_own[zz, 0, rows : rows + EXTRA, :].astype(F32) + k_other[
            zz, 0, rows : rows + EXTRA, :
        ].astype(F32)
        counts = counts + both * near_ok
        both = k_own[zz, 1, rows : rows + EXTRA, :].astype(F32) + k_other[
            zz, 1, rows : rows + EXTRA, :
        ].astype(F32)
        counts = counts + both * jnp.where(zz > z, far_ok, 1.0)
    doc = doc_ref[...]
    first_row = jnp.zeros((1, rows), F32)
    for d in range(1, EXTRA):
        first_row = jnp.where(doc == d, counts[d : d + 1, :rows], first_row)
    first_row = first_row.astype(jnp.int32) + reach
    lo = (jnp.min(first_row) - base) // (2 * rows)
    edge = jnp.minimum((jnp.max(first_row) - base) // (2 * rows) + 1, here)
    info_ref[0] = lo
    q_pos = base + (here * 2 + core) * rows + lax.broadcasted_iota(jnp.int32, (1, rows), 1)
    firsts = jnp.concatenate([first_row] * (tile // rows), axis=1)
    lasts = jnp.concatenate([q_pos] * (tile // rows), axis=1)
    key_iota = lax.broadcasted_iota(jnp.int32, (rows, tile), 0)

    state[0:1, :] = jnp.full((1, total), NEG_FILL, F32)
    state[1:2, :] = jnp.zeros((1, total), F32)

    def visit(j, masked):
        slot = j - lo
        keys = k_win[j]
        for t in range(total // tile):
            cols = slice(t * tile, (t + 1) * tile)
            s = nt(keys, q_all[cols, :])
            if masked:
                pieces = []
                for half, c in ((0, core), (1, 1 - core)):
                    key_pos = key_iota + (base + (j * 2 + c) * rows)
                    pieces.append(
                        jnp.where(
                            (key_pos >= firsts) & (key_pos <= lasts),
                            s[half * rows : (half + 1) * rows],
                            NEG_FILL,
                        )
                    )
                s = jnp.concatenate(pieces, axis=0)
            old = state[0:1, cols]
            peak = jnp.maximum(old, jnp.max(s, axis=0, keepdims=True))
            p = jnp.exp2(s * unit - peak * unit)
            p_all[slot, :, cols] = p
            state[1:2, cols] = state[1:2, cols] * jnp.exp2((old - peak) * unit) + jnp.sum(
                p, axis=0, keepdims=True
            )
            state[0:1, cols] = peak
            peaks[slot, 0:1, cols] = peak

    def plain(j, carry):
        visit(j, False)
        return carry

    def edges(i, carry):
        visit(jnp.where(lo + i < edge, lo + i, here), True)
        return carry

    lax.fori_loop(0, edge - lo + 1, edges, 0)
    lax.fori_loop(edge, here, plain, 0)
    state[1:2, :] = 1.0 / state[1:2, :]

    def copy_out(slot):
        return pltpu.make_async_copy(p_all.at[slot], p_out.at[slot], sems.at[slot])

    def second(j, carry):
        slot = j - lo
        dv = jnp.zeros((2 * rows, hd), F32)
        for t in range(total // tile):
            cols = slice(t * tile, (t + 1) * tile)
            factor = jnp.exp2((peaks[slot, 0:1, cols] - state[0:1, cols]) * unit) * state[1:2, cols]
            probs = p_all[slot, :, cols] * factor
            p_all[slot, :, cols] = probs
            dv = dv + nn(probs.astype(BF), do_all[cols, :])
        copy_out(slot).start()
        at = out_index(j, z, zs)
        dv_own[at] = dv[:rows]
        dv_other[at] = dv[rows:]
        return carry

    lax.fori_loop(lo, here + 1, second, 0)

    def clear(j, carry):
        at = out_index(j, z, zs)
        dv_own[at] = jnp.zeros((rows, hd), F32)
        dv_other[at] = jnp.zeros((rows, hd), F32)
        return carry

    lax.fori_loop(z, lo, clear, 0)

    def finish(j, carry):
        copy_out(j - lo).wait()
        return carry

    lax.fori_loop(lo, here + 1, finish, 0)


def score_kernel(
    place_ref,
    info_ref,
    q_ref,
    do_ref,
    o_ref,
    k_own,
    k_other,
    far_own,
    far_other,
    v_own,
    v_other,
    far_v_own,
    far_v_other,
    p_in,
    dq_ref,
    dk_own,
    dk_other,
    q_all,
    do_all,
    k_win,
    v_win,
    p_all,
    delta,
    dq_sum,
    sems,
    *,
    zs,
    scale,
    tile,
):
    rows, width = q_ref.shape
    hd = q_all.shape[1]
    total = q_all.shape[0]
    z = place_ref[1]
    here = 2 * zs + z
    lo = info_ref[0]

    def copy_in(slot):
        return pltpu.make_async_copy(p_in.at[slot], p_all.at[slot], sems.at[slot])

    def begin(j, carry):
        copy_in(j - lo).start()
        return carry

    lax.fori_loop(lo, here + 1, begin, 0)
    stack_heads(q_all, q_ref)
    stack_heads(do_all, do_ref)
    fill_window(k_win, k_own, k_other, far_own[:rows, :], far_other[:rows, :], z, zs)
    fill_window(v_win, v_own, v_other, far_v_own[...], far_v_other[...], z, zs)
    for n in range(width // hd):
        cols = slice(n * hd, (n + 1) * hd)
        prod = do_ref[:, cols].astype(F32) * o_ref[:, cols].astype(F32)
        delta[0:1, n * rows : (n + 1) * rows] = jnp.sum(prod.T, axis=0, keepdims=True)
    dq_sum[...] = jnp.zeros_like(dq_sum)

    def clear(j, carry):
        at = out_index(j, z, zs)
        dk_own[at] = jnp.zeros((rows, hd), F32)
        dk_other[at] = jnp.zeros((rows, hd), F32)
        return carry

    lax.fori_loop(z, lo, clear, 0)

    def visit(j, carry):
        slot = j - lo
        copy_in(slot).wait()
        keys_t = k_win[j].T
        values = v_win[j]
        dk = jnp.zeros((2 * rows, hd), F32)
        for t in range(total // tile):
            cols = slice(t * tile, (t + 1) * tile)
            dprob = nt(values, do_all[cols, :])
            dscore = (p_all[slot, :, cols] * (dprob - delta[0:1, cols]) * scale).astype(BF)
            dk = dk + nn(dscore, q_all[cols, :])
            dq_sum[:, cols] += nn(keys_t, dscore)
        at = out_index(j, z, zs)
        dk_own[at] = dk[:rows]
        dk_other[at] = dk[rows:]
        return carry

    lax.fori_loop(lo, here + 1, visit, 0)
    for n in range(width // hd):
        dq_ref[:, n * hd : (n + 1) * hd] = dq_sum[:, n * rows : (n + 1) * rows].T.astype(BF)


def swap(value):
    return lax.ppermute(value, "core", [(0, 1), (1, 0)])


def reduce_blocks(own, other, zs, xs, z):
    rows, hd = own.shape[1:]
    both = own + swap(other)
    sent = both[: 2 * zs].astype(BF).reshape(zs, 2, rows, hd)
    came = lax.all_to_all(sent, "z", split_axis=0, concat_axis=0, tiled=True)
    came = came.astype(F32)
    later = (jnp.arange(zs) >= z)[:, None, None]
    mine = jnp.sum(jnp.where(later, came[:, 1], 0.0), axis=0)
    near = jnp.sum(came[:, 0], axis=0)
    far = jnp.sum(jnp.where(later, 0.0, came[:, 1]), axis=0) + both[2 * zs]
    from_next = lax.ppermute(near, "x", [(i, i - 1) for i in range(1, xs)])
    from_last = lax.ppermute(far, "x", [(i, i - 2) for i in range(2, xs)])
    return (mine + from_next + from_last).astype(BF)[:, None, :]


def program(queries, keys, values, outputs, grad_out, doc_ids, owner):
    hd = keys.shape[2]
    scale = hd**-0.5
    rows, _, width = queries.shape
    total = rows * (width // hd)
    tile = min(256, total)
    xs, zs = lax.axis_size("x"), lax.axis_size("z")
    x, z, core = lax.axis_index("x"), lax.axis_index("z"), lax.axis_index("core")
    peers = xs * zs * 2
    per_device = owner.shape[0]
    block_len = rows // per_device
    part = keys.shape[0]
    chips = 2 * zs + 1

    earlier = jnp.sum(
        (doc_ids[None, :] < jnp.arange(EXTRA, dtype=jnp.int32)[:, None]).astype(F32), axis=1, keepdims=True
    )
    earlier = jnp.broadcast_to(earlier[None], (4, EXTRA, 2 * hd)).astype(BF)
    mixed = jnp.transpose(jnp.concatenate([keys, values], axis=-1), (1, 0, 2))
    mixed = jnp.concatenate([mixed, earlier], axis=1)
    mixed = jnp.broadcast_to(mixed[:, None], (4, xs, part + EXTRA, 2 * hd))
    mixed = lax.all_to_all(
        mixed.reshape(4 * xs, part + EXTRA, 2 * hd),
        ("dp", "head", "x"),
        split_axis=0,
        concat_axis=0,
        tiled=True,
    ).reshape(2, 2, xs, part + EXTRA, 2 * hd)

    def piece(back):
        got = lax.dynamic_index_in_dim(mixed, lax.rem(x - back + xs, xs), 2, keepdims=False)
        tokens = jnp.transpose(got[:, :, :part], (1, 0, 2, 3)).reshape(rows, 2 * hd)
        return jnp.concatenate([tokens, got[0, 0, part:]], axis=0)

    last, near, far = piece(0), piece(1), piece(2)
    far_other = swap(far)

    def along_z(a, b, c):
        ahead = (jnp.arange(zs) >= z)[:, None, None]
        chosen = jnp.where(ahead, a[None], c[None])
        pair = jnp.stack([jnp.broadcast_to(b[None], chosen.shape), chosen], axis=1)
        return lax.all_to_all(pair, "z", split_axis=0, concat_axis=0, tiled=True)

    k_own = along_z(last[:, :hd], near[:, :hd], far[:, :hd])
    k_other = swap(k_own)
    v_own = along_z(last[:rows, hd:], near[:rows, hd:], far[:rows, hd:])

    base = (x - 2) * (zs * 2 * rows)
    place = jnp.stack([x, z, core, base, jnp.maximum(base + z * 2 * rows, 0)]).astype(jnp.int32)
    q = queries.reshape(rows, width)
    do = grad_out.reshape(rows, width)
    o = outputs.reshape(rows, width)
    vmem = pl.BlockSpec(memory_space=pltpu.VMEM)
    smem = pl.BlockSpec(memory_space=pltpu.SMEM)
    anywhere = pl.BlockSpec(memory_space=pl.ANY)
    grad_shape = jax.ShapeDtypeStruct((chips, rows, hd), F32)
    params = pltpu.CompilerParams(vmem_limit_bytes=48 * 1024 * 1024)
    dv_own, dv_other, probs, info = pl.pallas_call(
        functools.partial(softmax_kernel, zs=zs, scale=scale, tile=tile),
        in_specs=[smem] + [vmem] * 7,
        out_specs=[vmem, vmem, anywhere, smem],
        out_shape=[
            grad_shape,
            grad_shape,
            jax.ShapeDtypeStruct((chips, 2 * rows, total), F32),
            jax.ShapeDtypeStruct((1,), jnp.int32),
        ],
        scratch_shapes=[
            pltpu.VMEM((total, hd), BF),
            pltpu.VMEM((total, hd), BF),
            pltpu.VMEM((3 * zs, 2 * rows, hd), BF),
            pltpu.VMEM((chips, 2 * rows, total), F32),
            pltpu.VMEM((chips, 8, total), F32),
            pltpu.VMEM((8, total), F32),
            pltpu.SemaphoreType.DMA((chips,)),
        ],
        compiler_params=params,
        cost_estimate=pl.CostEstimate(
            flops=12_000_000_000, bytes_accessed=20_000_000, transcendentals=4_000_000
        ),
        name="softmax_and_value_gradient",
    )(
        place,
        q,
        do,
        doc_ids.reshape(1, rows),
        k_own,
        k_other,
        far[:, :hd],
        far_other[:, :hd],
    )
    v_other = swap(v_own)
    grad_v = reduce_blocks(dv_own, dv_other, zs, xs, z)
    dq, dk_own, dk_other = pl.pallas_call(
        functools.partial(score_kernel, zs=zs, scale=scale, tile=tile),
        in_specs=[smem, smem] + [vmem] * 11 + [anywhere],
        out_specs=[vmem] * 3,
        out_shape=[jax.ShapeDtypeStruct((rows, width), BF), grad_shape, grad_shape],
        scratch_shapes=[
            pltpu.VMEM((total, hd), BF),
            pltpu.VMEM((total, hd), BF),
            pltpu.VMEM((3 * zs, 2 * rows, hd), BF),
            pltpu.VMEM((3 * zs, 2 * rows, hd), BF),
            pltpu.VMEM((chips, 2 * rows, total), F32),
            pltpu.VMEM((8, total), F32),
            pltpu.VMEM((hd, total), F32),
            pltpu.SemaphoreType.DMA((chips,)),
        ],
        compiler_params=params,
        cost_estimate=pl.CostEstimate(
            flops=12_000_000_000, bytes_accessed=20_000_000, transcendentals=0
        ),
        name="score_gradient",
    )(
        place,
        info,
        q,
        do,
        o,
        k_own,
        k_other,
        far[:, :hd],
        far_other[:, :hd],
        v_own,
        v_other,
        far[:rows, hd:],
        far_other[:rows, hd:],
        probs,
    )
    grad_k = reduce_blocks(dk_own, dk_other, zs, xs, z)

    slot_ids = jnp.arange(per_device, dtype=jnp.int32)
    send_mat = (owner[None, :] == jnp.arange(peers, dtype=jnp.int32)[:, None]).astype(BF)
    tags = jnp.broadcast_to((slot_ids + 1)[:, None, None], (per_device, block_len, 128)).astype(BF)
    blocks = jnp.concatenate([dq.reshape(per_device, block_len, width), tags], axis=-1)
    packed = jnp.einsum("pj,jbw->pbw", send_mat, blocks, preferred_element_type=F32).astype(BF)
    arrived = lax.all_to_all(packed, ("x", "z", "core"), split_axis=0, concat_axis=0, tiled=True)
    tag = arrived[:, 0, width].astype(jnp.int32)
    pick = (tag[None, :] == slot_ids[:, None] + 1).astype(BF)
    placed = jnp.einsum(
        "jp,pbw->jbw", pick, arrived[:, :, :width], preferred_element_type=F32
    ).astype(BF)
    return (placed.reshape(rows, 1, width), grad_k, grad_v)


def solution(mesh):
    sizes = mesh.shape
    dp, ctx, head = sizes["dp"], sizes["ctx"], sizes["head"]
    xs = 4
    fine = Mesh(
        mesh.devices.reshape(dp, xs, ctx // (2 * xs), 2, head), ("dp", "x", "z", "core", "head")
    )
    ctx_axes = ("x", "z", "core")
    heads = P(ctx_axes, ("dp", "head"), None)
    tokens = P(ctx_axes + ("head", "dp"), None, None)
    return jax.shard_map(
        program,
        mesh=fine,
        in_specs=(heads, tokens, tokens, heads, heads, P(ctx_axes), P(ctx_axes)),
        out_specs=(heads, heads, heads),
        check_vma=False,
    )
```

time: 165 us -> 187 us (1.13)
  waiting for transfers between devices: 58 us -> 88.2 us
  blocking collectives: 29.1 us -> 0 us
  Pallas kernels: 9.09 us -> 19.9 us
  local copies, waits for them, and re-layouts: 8.97 us -> 15 us
  starting transfers between devices: 48.5 us -> 51.4 us
  other arithmetic: 7.29 us -> 9.8 us
    all_to_all x3 -> x6, waiting for transfers between devices: 17.3 us -> 79.7 us  [the longest x2 29.6 us: along_z(): return lax.all_to_all(pair, 'z', split_axis=0, concat_axis=0, tiled=True)]
    ppermute x6 -> x9, waiting for transfers between devices: 40.7 us -> 8.51 us  [the longest x5 3.82 us: swap(): return lax.ppermute(value, 'core', [(0, 1), (1, 0)])]
    all_gather x1 -> x0, blocking collectives: 29.1 us -> none  [body(): line = lax.all_gather(near, 'z', axis=0, tiled=False)]
    pallas_call x1 -> x2, Pallas kernels: 9.09 us -> 19.9 us  [the longest x1 10.8 us: program(): pl.pallas_call(functools.partial(score_kernel, zs=zs, scale=scale, tile=t...]
    unnamed x10 -> x30, local copies, waits for them, and re-layouts: 2.81 us -> 7.51 us
    all_to_all x3 -> x6, starting transfers between devices: 39.3 us -> 42.7 us  [the longest x1 16.2 us: program(): lax.all_to_all(packed, ('x', 'z', 'core'), split_axis=0, concat_axis=0, t...]
    add x1 -> x5, other arithmetic: 0.01 us -> 2.41 us  [the longest x2 1.55 us: reduce_blocks(): both = own + swap(other)]
    ppermute x6 -> x9, starting transfers between devices: 9.28 us -> 8.67 us  [the longest x2 4.83 us: reduce_blocks(): from_next = lax.ppermute(near, 'x', [(i, i - 1) for i in range(1, xs)])]
  transfers between devices with their start and end apart: 9 -> 15, of which waited for: 6 -> 12; matrix products, arithmetic and copies ran while one was open for 8% -> 5% of each run, Pallas kernels for 0% -> 5%
where the time goes in v2:
time: 187 us; the launch traced here: 186 us
  waiting for transfers between devices  88.2 us (47%)
  starting transfers between devices  51.4 us (27%)
  Pallas kernels  19.9 us (11%)
  local copies, waits for them, and re-layouts  15 us (8%)
  other arithmetic  9.8 us (5%)
    all_to_all x2, waiting for transfers between devices, along_z(): return lax.all_to_all(pair, 'z', split_axis=0, concat_axis=0, tiled=True)  29.6 us
    all_to_all x2, waiting for transfers between devices, reduce_blocks(): came = lax.all_to_all(sent, 'z', split_axis=0, concat_axis=0, tiled=True)  29.2 us
    all_to_all x1, starting transfers between devices, program(): lax.all_to_all(packed, ('x', 'z', 'core'), split_axis=0, concat_axis=0, t...  16.2 us
    all_to_all x1, waiting for transfers between devices, program(): lax.all_to_all(packed, ('x', 'z', 'core'), split_axis=0, concat_axis=0, t...  12.8 us
    all_to_all x2, starting transfers between devices, along_z(): return lax.all_to_all(pair, 'z', split_axis=0, concat_axis=0, tiled=True)  12 us
    pallas_call x1, Pallas kernels, program(): pl.pallas_call(functools.partial(score_kernel, zs=zs, scale=scale, tile=t...  10.8 us
    pallas_call x1, Pallas kernels, program(): pl.pallas_call(functools.partial(softmax_kernel, zs=zs, scale=scale, tile...  9.08 us
    all_to_all x1, waiting for transfers between devices, program(): lax.all_to_all(mixed.reshape(4 * xs, part + EXTRA, 2 * hd), ('dp', 'head'...  8.01 us
  transfers between devices with their start and end apart: 15, of which 12 were waited for; matrix products, arithmetic and copies ran while one was open for 5% of the time, Pallas kernels for 5%

profile of v2, /device:TPU:2, one launch (start us, length us, event | category | flops | bytes accessed | tf_op | source)
XLA Modules:
  0.0 186.3 jit_solution(5870897876492497689)
XLA Ops:
  3.2 7.5 %all-to-all-start = ((bf16[16,40,256]{2,1,0:T(8,128)(2,1)}), bf16[16,40,256]{2,1,0:T(8,128)(2,1)S(1)}, u32[]{:S(2)}, u32[]{:S(2)}) async-start(bf16[16,40,256]{2,1,0:T(8,128)(2,1)} %bitcast.10), calls=%async_computation | async-start | bytes 655360 | tf_op jit(solution)/shard_map/all_to_all | solution.py:317
  10.7 8.0 %all-to-all-done = bf16[16,40,256]{2,1,0:T(8,128)(2,1)S(1)} async-done(((bf16[16,40,256]{2,1,0:T(8,128)(2,1)}), bf16[16,40,256]{2,1,0:T(8,128)(2,1)S(1)}, u32[]{:S(2)}, u32[]{:S(2)}) %all-to-all-start) | async-done | bytes 327712 | tf_op jit(solution)/shard_map/all_to_all | solution.py:317
  19.8 8.5 %all-to-all-start.1 = ((bf16[8,2,136,128]{3,2,1,0:T(8,128)(2,1)}), bf16[8,2,136,128]{3,2,1,0:T(8,128)(2,1)S(1)}, u32[]{:S(2)}, u32[]{:S(2)}) async-start(bf16[8,2,136,128]{3,2,1,0:T(8,128)(2,1)} %pad_maximum_fusion), calls=%async_computation.1 | async-start | bytes 1114112 | tf_op jit(solution)/shard_map/all_to_all | solution.py:337
  29.3 16.1 %all-to-all-done.1.k_own = bf16[8,2,136,128]{3,2,1,0:T(8,128)(2,1)S(1)} async-done(((bf16[8,2,136,128]{3,2,1,0:T(8,128)(2,1)}), bf16[8,2,136,128]{3,2,1,0:T(8,128)(2,1)S(1)}, u32[]{:S(2)}, u32[]{:S(2)}) %all-to-all-start.1) | async-done | bytes 557088 | tf_op jit(solution)/shard_map/all_to_all | solution.py:337
  45.4 3.5 %all-to-all-start.2 = ((bf16[8,2,128,128]{3,2,1,0:T(8,128)(2,1)}), bf16[8,2,128,128]{3,2,1,0:T(8,128)(2,1)S(1)}, u32[]{:S(2)}, u32[]{:S(2)}) async-start(bf16[8,2,128,128]{3,2,1,0:T(8,128)(2,1)} %pad_maximum_fusion.1), calls=%async_computation.2 | async-start | bytes 1048576 | tf_op jit(solution)/shard_map/all_to_all | solution.py:337
  49.7 1.4 collective-permute-done.1
  51.1 13.6 %all-to-all-done.2.v_own = bf16[8,2,128,128]{3,2,1,0:T(8,128)(2,1)S(1)} async-done(((bf16[8,2,128,128]{3,2,1,0:T(8,128)(2,1)}), bf16[8,2,128,128]{3,2,1,0:T(8,128)(2,1)S(1)}, u32[]{:S(2)}, u32[]{:S(2)}) %all-to-all-start.2) | async-done | bytes 524320 | tf_op jit(solution)/shard_map/all_to_all | solution.py:337
  65.5 1.1 copy-done.5
  66.5 0.9 copy-done.7
  68.4 9.1 %softmax_and_value_gradient.1 = (f32[17,128,128]{2,1,0:T(8,128)S(1)}, f32[17,128,128]{2,1,0:T(8,128)S(1)}, f32[17,256,1024]{2,1,0:T(8,128)}, s32[1]{0:T(128)}) custom-call(s32[5]{0:T(128)S(1)} %stack.31.place_ref, bf16[128,1024]{1,0:T(8,128)(2,1)S(1)} %bitcast.66, bf16[128,1024]{1,0:T(8,128)(2,1)S(1)} %bitcast.68, s32[1,128]{1,0:T(1,128)S(1)} %bitcast.71, ...), custom_call_target="tpu_custom_call" | custom-call | flops 12000000000 | bytes 20000000 | tf_op jit(solution)/shard_map/softmax_and_value_gradient/pallas_call | solution.py:353
  77.5 1.0 copy-done.3
  78.6 10.8 %score_gradient.1 = (bf16[128,1024]{1,0:T(8,128)(2,1)S(1)}, f32[17,128,128]{2,1,0:T(8,128)S(1)}, f32[17,128,128]{2,1,0:T(8,128)S(1)}) custom-call(s32[5]{0:T(128)S(1)} %stack.31.place_ref, s32[1]{0:T(128)} %get-tuple-element.10.info_ref, bf16[128,1024]{1,0:T(8,128)(2,1)S(1)} %bitcast.67, bf16[128,1024]{1,0:T(8,128)(2,1)S(1)} %bitcast.69, ...), custom_call_target="tpu_custom_call" | custom-call | flops 12000000000 | bytes 20000000 | tf_op jit(solution)/shard_map/score_gradient/pallas_call | solution.py:389
  90.1 1.0 copy-done.1
  91.1 1.1 reshape.88
  92.8 1.3 copy.45
  94.0 16.2 %all-to-all-start.3 = ((bf16[64,4,1152]{2,1,0:T(4,128)(2,1)}), bf16[64,4,1152]{2,1,0:T(4,128)(2,1)}, u32[]{:S(2)}, u32[]{:S(2)}) async-start(bf16[64,4,1152]{2,1,0:T(4,128)(2,1)} %copy.45), calls=%async_computation.3 | async-start | bytes 1179648 | tf_op jit(solution)/shard_map/all_to_all | solution.py:432
  110.8 2.5 %collective-permute-done.6 = f32[17,128,128]{2,1,0:T(8,128)S(1)} collective-permute-done((f32[17,128,128]{2,1,0:T(8,128)}, f32[17,128,128]{2,1,0:T(8,128)S(1)}, u32[]{:S(2)}, u32[]{:S(2)}) %collective-permute-start.6) | collective-permute-done | bytes 1114144 | tf_op jit(solution)/shard_map/ppermute | solution.py:278
  113.4 1.0 copy-done.13
  115.3 12.8 %all-to-all-done.3 = bf16[64,4,1152]{2,1,0:T(4,128)(2,1)} async-done(((bf16[64,4,1152]{2,1,0:T(4,128)(2,1)}), bf16[64,4,1152]{2,1,0:T(4,128)(2,1)}, u32[]{:S(2)}, u32[]{:S(2)}) %all-to-all-start.3) | async-done | bytes 589856 | tf_op jit(solution)/shard_map/all_to_all | solution.py:432
  128.2 3.6 %all-to-all-start.5 = ((bf16[8,2,128,128]{3,2,1,0:T(8,128)(2,1)}), bf16[8,2,128,128]{3,2,1,0:T(8,128)(2,1)S(1)}, u32[]{:S(2)}, u32[]{:S(2)}) async-start(bf16[8,2,128,128]{3,2,1,0:T(8,128)(2,1)} %bitcast.30), calls=%async_computation.5 | async-start | bytes 1048576 | tf_op jit(solution)/shard_map/all_to_all | solution.py:285
  131.8 1.4 add.80
  134.1 16.2 %all-to-all-done.5 = bf16[8,2,128,128]{3,2,1,0:T(8,128)(2,1)S(1)} async-done(((bf16[8,2,128,128]{3,2,1,0:T(8,128)(2,1)}), bf16[8,2,128,128]{3,2,1,0:T(8,128)(2,1)S(1)}, u32[]{:S(2)}, u32[]{:S(2)}) %all-to-all-start.5) | async-done | bytes 524320 | tf_op jit(solution)/shard_map/all_to_all | solution.py:285
  150.2 3.5 %all-to-all-start.4 = ((bf16[8,2,128,128]{3,2,1,0:T(8,128)(2,1)}), bf16[8,2,128,128]{3,2,1,0:T(8,128)(2,1)S(1)}, u32[]{:S(2)}, u32[]{:S(2)}) async-start(bf16[8,2,128,128]{3,2,1,0:T(8,128)(2,1)} %bitcast.26), calls=%async_computation.4 | async-start | bytes 1048576 | tf_op jit(solution)/shard_map/all_to_all | solution.py:285
  153.8 1.2 slice.118
  155.0 2.1 %fusion.9 = s32[64]{0:T(128)S(1)} fusion(bf16[64,4,1152]{2,1,0:T(4,128)(2,1)} %all-to-all-done.3), kind=kLoop, calls=%fused_computation.44 | loop fusion | flops 64 | bytes 384 | tf_op jit(solution)/shard_map/convert_element_type | solution.py:433
  158.6 13.0 %all-to-all-done.4 = bf16[8,2,128,128]{3,2,1,0:T(8,128)(2,1)S(1)} async-done(((bf16[8,2,128,128]{3,2,1,0:T(8,128)(2,1)}), bf16[8,2,128,128]{3,2,1,0:T(8,128)(2,1)S(1)}, u32[]{:S(2)}, u32[]{:S(2)}) %all-to-all-start.4) | async-done | bytes 524320 | tf_op jit(solution)/shard_map/all_to_all | solution.py:285
  172.8 1.3 collective-permute-start.8
  174.1 2.9 %collective-permute-start.7 = (f32[128,128]{1,0:T(8,128)S(1)}, f32[128,128]{1,0:T(8,128)S(1)}, u32[]{:S(2)}, u32[]{:S(2)}) collective-permute-start(f32[128,128]{1,0:T(8,128)S(1)} %slice_reduce_fusion), channel_id=1, source_target_pairs={{32,0},{64,32},{96,64},{33,1},{65,33},{97,65},{34,2},{66,34},{98,6... | collective-permute-start | bytes 196616 | tf_op jit(solution)/shard_map/ppermute | solution.py:291
  177.1 1.3 collective-permute-start.5
  178.4 1.9 %collective-permute-start.4 = (f32[128,128]{1,0:T(8,128)S(1)}, f32[128,128]{1,0:T(8,128)S(1)}, u32[]{:S(2)}, u32[]{:S(2)}) collective-permute-start(f32[128,128]{1,0:T(8,128)S(1)} %slice_reduce_fusion.1), channel_id=1, source_target_pairs={{32,0},{64,32},{96,64},{33,1},{65,33},{97,65},{34,2},{66,34},{98,6... | collective-permute-start | bytes 196616 | tf_op jit(solution)/shard_map/ppermute | solution.py:291
  180.6 1.2 collective-permute-done.7
  182.4 2.9 %collective-permute-done.5 = f32[128,128]{1,0:T(8,128)S(1)} collective-permute-done((f32[128,128]{1,0:T(8,128)S(1)}, f32[128,128]{1,0:T(8,128)S(1)}, u32[]{:S(2)}, u32[]{:S(2)}) %collective-permute-start.5) | collective-permute-done | bytes 65568 | tf_op jit(solution)/shard_map/ppermute | solution.py:292
  (86 shorter events, 15.5 us)
Async XLA Ops:
  3.2 15.5 %all-to-all-start = ((bf16[16,40,256]{2,1,0:T(8,128)(2,1)}), bf16[16,40,256]{2,1,0:T(8,128)(2,1)S(1)}, u32[]{:S(2)}, u32[]{:S(2)}) async-start(bf16[16,40,256]{2,1,0:T(8,128)(2,1)} %bitcast.10), calls=%async_computation | async-start | bytes 655360 | tf_op jit(solution)/shard_map/all_to_all | solution.py:317
  19.8 25.6 %all-to-all-start.1 = ((bf16[8,2,136,128]{3,2,1,0:T(8,128)(2,1)}), bf16[8,2,136,128]{3,2,1,0:T(8,128)(2,1)S(1)}, u32[]{:S(2)}, u32[]{:S(2)}) async-start(bf16[8,2,136,128]{3,2,1,0:T(8,128)(2,1)} %pad_maximum_fusion), calls=%async_computation.1 | async-start | bytes 1114112 | tf_op jit(solution)/shard_map/all_to_all | solution.py:337
  28.5 37.0 %copy-start.12 = (s32[128]{0:T(128)S(1)}, s32[128]{0:T(128)}, u32[]{:S(2)}) copy-start(s32[128]{0:T(128)} %param.12) | copy-start | bytes 1540
  45.4 19.2 %all-to-all-start.2 = ((bf16[8,2,128,128]{3,2,1,0:T(8,128)(2,1)}), bf16[8,2,128,128]{3,2,1,0:T(8,128)(2,1)S(1)}, u32[]{:S(2)}, u32[]{:S(2)}) async-start(bf16[8,2,128,128]{3,2,1,0:T(8,128)(2,1)} %pad_maximum_fusion.1), calls=%async_computation.2 | async-start | bytes 1048576 | tf_op jit(solution)/shard_map/all_to_all | solution.py:337
  48.9 15.7 %collective-permute-start = (bf16[8,2,136,128]{3,2,1,0:T(8,128)(2,1)S(1)}, bf16[8,2,136,128]{3,2,1,0:T(8,128)(2,1)S(1)}, u32[]{:S(2)}, u32[]{:S(2)}) collective-permute-start(bf16[8,2,136,128]{3,2,1,0:T(8,128)(2,1)S(1)} %all-to-all-done.1.k_own), channel_id=1, source_target_pairs={{0,2},{2,0},{1,3},{3,1},{4,6},{6,4},{5,7},{7,5},{8,10},{10,8},{9,1... | collective-permute-start | bytes 1671176 | tf_op jit(solution)/shard_map/ppermute | solution.py:278
  49.1 1.9 %collective-permute-start.1 = (bf16[136,256]{1,0:T(8,128)(2,1)S(1)}, bf16[136,256]{1,0:T(8,128)(2,1)S(1)}, u32[]{:S(2)}, u32[]{:S(2)}) collective-permute-start(bf16[136,256]{1,0:T(8,128)(2,1)S(1)} %pad_maximum_fusion.2), channel_id=1, source_target_pairs={{0,2},{2,0},{1,3},{3,1},{4,6},{6,4},{5,7},{7,5},{8,10},{10,8},{9,1... | collective-permute-start | bytes 208904 | tf_op jit(solution)/shard_map/ppermute | solution.py:278
  64.6 13.9 %collective-permute-start.2 = (bf16[8,2,128,128]{3,2,1,0:T(8,128)(2,1)S(1)}, bf16[8,2,128,128]{3,2,1,0:T(8,128)(2,1)S(1)}, u32[]{:S(2)}, u32[]{:S(2)}) collective-permute-start(bf16[8,2,128,128]{3,2,1,0:T(8,128)(2,1)S(1)} %all-to-all-done.2.v_own), channel_id=1, source_target_pairs={{0,2},{2,0},{1,3},{3,1},{4,6},{6,4},{5,7},{7,5},{8,10},{10,8},{9,1... | collective-permute-start | bytes 1572872 | tf_op jit(solution)/shard_map/ppermute | solution.py:278
  64.6 0.8 copy-start.4
  65.5 1.1 copy-start.5
  66.5 0.9 copy-start.7
  67.5 0.9 copy-start.9
  68.4 10.1 %copy-start.6 = (bf16[8,2,136,128]{3,2,1,0:T(8,128)(2,1)S(1)}, bf16[8,2,136,128]{3,2,1,0:T(8,128)(2,1)}, u32[]{:S(2)}) copy-start(bf16[8,2,136,128]{3,2,1,0:T(8,128)(2,1)} %copy-done.4) | copy-start | bytes 1671172
  68.4 10.1 %copy-start.8 = (bf16[128,1,1024]{2,0,1:T(8,128)(2,1)S(1)}, bf16[128,1,1024]{2,0,1:T(8,128)(2,1)}, u32[]{:S(2)}) copy-start(bf16[128,1,1024]{2,0,1:T(8,128)(2,1)} %param.7) | copy-start | bytes 786436
  68.4 10.1 %copy-start.10 = (bf16[128,1,1024]{2,0,1:T(8,128)(2,1)S(1)}, bf16[128,1,1024]{2,0,1:T(8,128)(2,1)}, u32[]{:S(2)}) copy-start(bf16[128,1,1024]{2,0,1:T(8,128)(2,1)} %param.11) | copy-start | bytes 786436
  68.4 10.1 %copy-start.11 = (bf16[128,1,1024]{2,0,1:T(8,128)(2,1)S(1)}, bf16[128,1,1024]{2,0,1:T(8,128)(2,1)}, u32[]{:S(2)}) copy-start(bf16[128,1,1024]{2,0,1:T(8,128)(2,1)} %param.10) | copy-start | bytes 786436
  77.5 1.0 copy-start.3
  78.5 13.8 %copy-start.14 = (s32[32]{0:T(128)S(1)}, s32[32]{0:T(128)}, u32[]{:S(2)}) copy-start(s32[32]{0:T(128)} %param.13) | copy-start | bytes 388
  89.4 0.7 copy-start
  90.1 1.0 copy-start.1
  92.7 17.7 %copy-start.2 = (f32[17,128,128]{2,1,0:T(8,128)S(1)}, f32[17,128,128]{2,1,0:T(8,128)}, u32[]{:S(2)}) copy-start(f32[17,128,128]{2,1,0:T(8,128)} %copy-done.1) | copy-start | bytes 3342340
  94.0 34.1 %all-to-all-start.3 = ((bf16[64,4,1152]{2,1,0:T(4,128)(2,1)}), bf16[64,4,1152]{2,1,0:T(4,128)(2,1)}, u32[]{:S(2)}, u32[]{:S(2)}) async-start(bf16[64,4,1152]{2,1,0:T(4,128)(2,1)} %copy.45), calls=%async_computation.3 | async-start | bytes 1179648 | tf_op jit(solution)/shard_map/all_to_all | solution.py:432
  110.2 3.1 %collective-permute-start.6 = (f32[17,128,128]{2,1,0:T(8,128)}, f32[17,128,128]{2,1,0:T(8,128)S(1)}, u32[]{:S(2)}, u32[]{:S(2)}) collective-permute-start(f32[17,128,128]{2,1,0:T(8,128)} %copy-done.3), channel_id=1, source_target_pairs={{0,2},{2,0},{1,3},{3,1},{4,6},{6,4},{5,7},{7,5},{8,10},{10,8},{9,1... | collective-permute-start | bytes 3342344 | tf_op jit(solution)/shard_map/ppermute | solution.py:278
  110.4 21.4 %collective-permute-start.3 = (f32[17,128,128]{2,1,0:T(8,128)S(1)}, f32[17,128,128]{2,1,0:T(8,128)}, u32[]{:S(2)}, u32[]{:S(2)}) collective-permute-start(f32[17,128,128]{2,1,0:T(8,128)S(1)} %copy-done.2), channel_id=1, source_target_pairs={{0,2},{2,0},{1,3},{3,1},{4,6},{6,4},{5,7},{7,5},{8,10},{10,8},{9,1... | collective-permute-start | bytes 3342344 | tf_op jit(solution)/shard_map/ppermute | solution.py:278
  113.4 1.0 copy-start.13
  128.2 22.1 %all-to-all-start.5 = ((bf16[8,2,128,128]{3,2,1,0:T(8,128)(2,1)}), bf16[8,2,128,128]{3,2,1,0:T(8,128)(2,1)S(1)}, u32[]{:S(2)}, u32[]{:S(2)}) async-start(bf16[8,2,128,128]{3,2,1,0:T(8,128)(2,1)} %bitcast.30), calls=%async_computation.5 | async-start | bytes 1048576 | tf_op jit(solution)/shard_map/all_to_all | solution.py:285
  150.2 21.4 %all-to-all-start.4 = ((bf16[8,2,128,128]{3,2,1,0:T(8,128)(2,1)}), bf16[8,2,128,128]{3,2,1,0:T(8,128)(2,1)S(1)}, u32[]{:S(2)}, u32[]{:S(2)}) async-start(bf16[8,2,128,128]{3,2,1,0:T(8,128)(2,1)} %bitcast.26), calls=%async_computation.4 | async-start | bytes 1048576 | tf_op jit(solution)/shard_map/all_to_all | solution.py:285
  172.8 7.8 %collective-permute-start.8 = (f32[128,128]{1,0:T(8,128)S(1)}, f32[128,128]{1,0:T(8,128)S(1)}, u32[]{:S(2)}, u32[]{:S(2)}) collective-permute-start(f32[128,128]{1,0:T(8,128)S(1)} %fusion.4), channel_id=1, source_target_pairs={{64,0},{96,32},{65,1},{97,33},{66,2},{98,34},{67,3},{99,35},{68,4}... | collective-permute-start | bytes 196616 | tf_op jit(solution)/shard_map/ppermute | solution.py:292
  174.1 7.7 %collective-permute-start.7 = (f32[128,128]{1,0:T(8,128)S(1)}, f32[128,128]{1,0:T(8,128)S(1)}, u32[]{:S(2)}, u32[]{:S(2)}) collective-permute-start(f32[128,128]{1,0:T(8,128)S(1)} %slice_reduce_fusion), channel_id=1, source_target_pairs={{32,0},{64,32},{96,64},{33,1},{65,33},{97,65},{34,2},{66,34},{98,6... | collective-permute-start | bytes 196616 | tf_op jit(solution)/shard_map/ppermute | solution.py:291
  177.1 8.3 %collective-permute-start.5 = (f32[128,128]{1,0:T(8,128)S(1)}, f32[128,128]{1,0:T(8,128)S(1)}, u32[]{:S(2)}, u32[]{:S(2)}) collective-permute-start(f32[128,128]{1,0:T(8,128)S(1)} %fusion.5), channel_id=1, source_target_pairs={{64,0},{96,32},{65,1},{97,33},{66,2},{98,34},{67,3},{99,35},{68,4}... | collective-permute-start | bytes 196616 | tf_op jit(solution)/shard_map/ppermute | solution.py:292
  178.4 7.2 %collective-permute-start.4 = (f32[128,128]{1,0:T(8,128)S(1)}, f32[128,128]{1,0:T(8,128)S(1)}, u32[]{:S(2)}, u32[]{:S(2)}) collective-permute-start(f32[128,128]{1,0:T(8,128)S(1)} %slice_reduce_fusion.1), channel_id=1, source_target_pairs={{32,0},{64,32},{96,64},{33,1},{65,33},{97,65},{34,2},{66,34},{98,6... | collective-permute-start | bytes 196616 | tf_op jit(solution)/shard_map/ppermute | solution.py:291

commit v3 on v2

v3 whole, which is shorter than its diff:
```python
import functools
import math

import jax
import jax.numpy as jnp
from jax import lax
from jax.experimental import pallas as pl
from jax.experimental.pallas import tpu as pltpu
from jax.sharding import Mesh, PartitionSpec as P


NEG_FILL = -1e30
BF = jnp.bfloat16
F32 = jnp.float32
COUNTS = 4


def nt(a, b):
    return lax.dot_general(a, b, (((1,), (1,)), ((), ())), preferred_element_type=F32)


def nn(a, b):
    return lax.dot_general(a, b, (((1,), (0,)), ((), ())), preferred_element_type=F32)


def stack_heads(dst, src):
    rows, width = src.shape
    hd = dst.shape[1]
    for n in range(width // hd):
        dst[n * rows : (n + 1) * rows, :] = src[:, n * hd : (n + 1) * hd]


def fill_window(win, own, other, far_own, far_other, z, zs):
    rows = win.shape[1] // 2
    for half, near, far in ((0, own, far_own), (1, other, far_other)):
        cut = pl.ds(half * rows, rows)
        for zz in range(zs):
            win[zs + zz, cut, :] = near[zz, 0, :rows, :]
            win[jnp.where(zz > z, zz, 2 * zs + zz), cut, :] = near[zz, 1, :rows, :]
        win[z, cut, :] = far


def out_index(j, z, zs):
    zz = lax.rem(j, zs)
    middle = (j >= zs) & (j < 2 * zs)
    return jnp.where(middle, 2 * zz, jnp.where(j == z, 2 * zs, 2 * zz + 1))


def relative_index(j, z, zs):
    zz = lax.rem(lax.rem(j, zs) + zs - z, zs)
    middle = (j >= zs) & (j < 2 * zs)
    return jnp.where(middle, 2 * zz, jnp.where(j == z, 2 * zs, 2 * zz + 1))


def softmax_kernel(
    place_ref,
    q_ref,
    do_ref,
    doc_ref,
    k_own,
    k_other,
    far_own,
    far_other,
    dv_own,
    dv_other,
    p_out,
    info_ref,
    factors,
    q_all,
    do_all,
    k_win,
    p_all,
    raw,
    low,
    state,
    sems,
    *,
    zs,
    scale,
    tile,
    group,
):
    rows, _ = q_ref.shape
    hd = q_all.shape[1]
    total = q_all.shape[0]
    x, z, core = place_ref[0], place_ref[1], place_ref[2]
    base, reach = place_ref[3], place_ref[4]
    here = 2 * zs + z
    unit = scale * math.log2(math.e)

    stack_heads(q_all, q_ref)
    stack_heads(do_all, do_ref)
    fill_window(k_win, k_own, k_other, far_own[:rows, :], far_other[:rows, :], z, zs)

    near_ok = (x >= 1).astype(F32)
    far_ok = (x >= 2).astype(F32)
    counts = (
        far_own[rows : rows + COUNTS, :].astype(F32) + far_other[rows : rows + COUNTS, :].astype(F32)
    ) * far_ok
    for zz in range(zs):
        both = k_own[zz, 0, rows : rows + COUNTS, :].astype(F32) + k_other[
            zz, 0, rows : rows + COUNTS, :
        ].astype(F32)
        counts = counts + both * near_ok
        both = k_own[zz, 1, rows : rows + COUNTS, :].astype(F32) + k_other[
            zz, 1, rows : rows + COUNTS, :
        ].astype(F32)
        counts = counts + both * jnp.where(zz > z, far_ok, 1.0)
    doc = doc_ref[...]
    first_row = jnp.zeros((1, rows), F32)
    for d in range(1, COUNTS):
        first_row = jnp.where(doc == d, counts[d : d + 1, :rows], first_row)
    first_row = first_row.astype(jnp.int32) + reach
    lo = (jnp.min(first_row) - base) // (2 * rows)
    edge = jnp.minimum((jnp.max(first_row) - base) // (2 * rows) + 1, here)
    info_ref[0] = lo
    q_pos = base + (here * 2 + core) * rows + lax.broadcasted_iota(jnp.int32, (1, rows), 1)
    firsts = jnp.concatenate([first_row] * (tile // rows), axis=1)
    lasts = jnp.concatenate([q_pos] * (tile // rows), axis=1)
    key_iota = lax.broadcasted_iota(jnp.int32, (rows, tile), 0)

    state[0:1, :] = jnp.full((1, total), NEG_FILL, F32)
    state[1:2, :] = jnp.zeros((1, total), F32)

    def visit(j, masked):
        slot = j - lo
        for t in range(total // tile):
            cols = slice(t * tile, (t + 1) * tile)
            q_t = q_all[cols, :]
            peak = state[0:1, cols]
            for half in range(2):
                cut = slice(half * rows, (half + 1) * rows)
                s = nt(k_win[j, cut, :], q_t) * unit
                if masked:
                    key_pos = key_iota + (base + (j * 2 + (core if half == 0 else 1 - core)) * rows)
                    s = jnp.where((key_pos >= firsts) & (key_pos <= lasts), s, NEG_FILL)
                peak = jnp.maximum(peak, jnp.max(s, axis=0, keepdims=True))
                raw[cut, cols] = s
            factors[slot, 0:1, cols] = peak
        for t in range(total // tile):
            cols = slice(t * tile, (t + 1) * tile)
            old, peak = state[0:1, cols], factors[slot, 0:1, cols]
            seen = state[1:2, cols] * jnp.exp2(old - peak)
            for half in range(2):
                cut = slice(half * rows, (half + 1) * rows)
                p = jnp.exp2(raw[cut, cols] - peak)
                p_all[slot, cut, cols] = p
                seen = seen + jnp.sum(p, axis=0, keepdims=True)
            state[0:1, cols] = peak
            state[1:2, cols] = seen
        pltpu.make_async_copy(p_all.at[slot], p_out.at[slot], sems.at[slot]).start()

    def plain(j, carry):
        visit(j, False)
        return carry

    def edges(i, carry):
        visit(jnp.where(lo + i < edge, lo + i, here), True)
        return carry

    lax.fori_loop(0, edge - lo + 1, edges, 0)
    lax.fori_loop(edge, here, plain, 0)
    state[1:2, :] = 1.0 / state[1:2, :]

    def second(j, carry):
        slot = j - lo
        dv = jnp.zeros((2 * rows, hd), F32)
        for g in range(total // group):
            for t in range(g * group // tile, (g + 1) * group // tile):
                cols = slice(t * tile, (t + 1) * tile)
                factor = jnp.exp2(factors[slot, 0:1, cols] - state[0:1, cols]) * state[1:2, cols]
                factors[slot, 0:1, cols] = factor
                for half in range(2):
                    cut = slice(half * rows, (half + 1) * rows)
                    low[cut, cols] = (p_all[slot, cut, cols] * factor).astype(BF)
            span = slice(g * group, (g + 1) * group)
            dv = dv + nn(low[:, span], do_all[span, :])
        at = out_index(j, z, zs)
        dv_own[at] = dv[:rows]
        dv_other[at] = dv[rows:]
        return carry

    lax.fori_loop(lo, here + 1, second, 0)

    def clear(j, carry):
        at = out_index(j, z, zs)
        dv_own[at] = jnp.zeros((rows, hd), F32)
        dv_other[at] = jnp.zeros((rows, hd), F32)
        return carry

    lax.fori_loop(z, lo, clear, 0)

    def finish(j, carry):
        slot = j - lo
        pltpu.make_async_copy(p_all.at[slot], p_out.at[slot], sems.at[slot]).wait()
        return carry

    lax.fori_loop(lo, here + 1, finish, 0)


def score_kernel(
    place_ref,
    info_ref,
    q_ref,
    do_ref,
    o_ref,
    k_own,
    k_other,
    far_own,
    far_other,
    v_own,
    v_other,
    far_v_own,
    far_v_other,
    factors,
    owner_ref,
    p_in,
    packed_ref,
    dk_own,
    dk_other,
    q_all,
    do_all,
    k_win,
    v_win,
    p_all,
    low,
    delta,
    dq_sum,
    sems,
    *,
    zs,
    scale,
    tile,
    group,
    block,
):
    rows, width = q_ref.shape
    hd = q_all.shape[1]
    total = q_all.shape[0]
    z = place_ref[1]
    here = 2 * zs + z
    lo = info_ref[0]

    def copy_in(slot):
        return pltpu.make_async_copy(p_in.at[slot], p_all.at[slot], sems.at[slot])

    def begin(j, carry):
        copy_in(j - lo).start()
        return carry

    lax.fori_loop(lo, here + 1, begin, 0)
    stack_heads(q_all, q_ref)
    stack_heads(do_all, do_ref)
    fill_window(k_win, k_own, k_other, far_own[:rows, :], far_other[:rows, :], z, zs)
    fill_window(v_win, v_own, v_other, far_v_own[...], far_v_other[...], z, zs)
    for n in range(width // hd):
        cols = slice(n * hd, (n + 1) * hd)
        prod = do_ref[:, cols].astype(F32) * o_ref[:, cols].astype(F32)
        delta[0:1, n * rows : (n + 1) * rows] = jnp.sum(prod.T, axis=0, keepdims=True)
    dq_sum[...] = jnp.zeros_like(dq_sum)

    def clear(j, carry):
        at = relative_index(j, z, zs)
        dk_own[at] = jnp.zeros((rows, hd), F32)
        dk_other[at] = jnp.zeros((rows, hd), F32)
        return carry

    lax.fori_loop(z, lo, clear, 0)

    def visit(j, carry):
        slot = j - lo
        copy_in(slot).wait()
        keys_t = k_win[j].T
        dk = jnp.zeros((2 * rows, hd), F32)
        for g in range(total // group):
            for t in range(g * group // tile, (g + 1) * group // tile):
                cols = slice(t * tile, (t + 1) * tile)
                do_t = do_all[cols, :]
                for half in range(2):
                    cut = slice(half * rows, (half + 1) * rows)
                    dprob = nt(v_win[j, cut, :], do_t)
                    probs = p_all[slot, cut, cols] * factors[slot, 0:1, cols]
                    low[cut, cols] = (probs * (dprob - delta[0:1, cols]) * scale).astype(BF)
            span = slice(g * group, (g + 1) * group)
            dk = dk + nn(low[:, span], q_all[span, :])
            dq_sum[:, span] += nn(keys_t, low[:, span])
        at = relative_index(j, z, zs)
        dk_own[at] = dk[:rows]
        dk_other[at] = dk[rows:]
        return carry

    lax.fori_loop(lo, here + 1, visit, 0)
    half_width = width // 2
    half_heads = half_width // hd
    spots = packed_ref.shape[0]
    row = lax.broadcasted_iota(jnp.int32, (spots, rows), 0)
    token = lax.broadcasted_iota(jnp.int32, (spots, rows), 1)
    goes = (row // (2 * block) == owner_ref[...]) & (row % block == token % block)
    packed = jnp.zeros((spots, half_width), F32)
    for h in range(2):
        here_half = goes & (row // block % 2 == h)
        turned = [
            dq_sum[:, n * rows : (n + 1) * rows].T.astype(BF)
            for n in range(h * half_heads, (h + 1) * half_heads)
        ]
        packed = packed + nn(here_half.astype(F32).astype(BF), jnp.concatenate(turned, axis=1))
    packed_ref[...] = packed.astype(BF)


def swap(value):
    return lax.ppermute(value, "core", [(0, 1), (1, 0)])


def placement_kernel(place_ref, owners_ref, arrived_ref, out_ref, *, block):
    peers, per_device = owners_ref.shape
    rows, spots = out_ref.shape[0], arrived_ref.shape[0]
    half_width = arrived_ref.shape[1]
    hit = (owners_ref[...].astype(F32) == place_ref[5].astype(F32)).astype(F32).astype(BF)
    slot = lax.broadcasted_iota(jnp.int32, (rows, per_device), 0) // block
    to_rows = (slot == lax.broadcasted_iota(jnp.int32, (rows, per_device), 1)).astype(F32).astype(BF)
    peer = lax.broadcasted_iota(jnp.int32, (peers, spots), 1) // (2 * block)
    to_spots = (peer == lax.broadcasted_iota(jnp.int32, (peers, spots), 0)).astype(F32).astype(BF)
    pick = nn(nt(to_rows, hit).astype(BF), to_spots)
    row = lax.broadcasted_iota(jnp.int32, (rows, spots), 0)
    spot = lax.broadcasted_iota(jnp.int32, (rows, spots), 1)
    same = spot % block == row % block
    for h in range(2):
        chosen = jnp.where(same & (spot // block % 2 == h), pick, 0.0).astype(BF)
        out_ref[:, h * half_width : (h + 1) * half_width] = nn(chosen, arrived_ref[...]).astype(BF)


def along_x(mine, near, far, xs):
    from_next = lax.ppermute(near, "x", [(i, i - 1) for i in range(1, xs)])
    from_last = lax.ppermute(far, "x", [(i, i - 2) for i in range(2, xs)])
    return (mine + from_next + from_last).astype(BF)[:, None, :]


def reduce_at_once(own, other, zs, xs, z):
    rows, hd = own.shape[1:]
    swapped = swap(other)
    sent = (own[: 2 * zs] + swapped[: 2 * zs]).astype(BF).reshape(zs, 2, rows, hd)
    came = lax.all_to_all(sent, "z", split_axis=0, concat_axis=0, tiled=True)
    came = came.astype(F32)
    later = (jnp.arange(zs) >= z)[:, None, None]
    mine = jnp.sum(jnp.where(later, came[:, 1], 0.0), axis=0)
    near = jnp.sum(came[:, 0], axis=0)
    far = jnp.sum(jnp.where(later, 0.0, came[:, 1]), axis=0) + own[2 * zs] + swapped[2 * zs]
    return along_x(mine, near, far, xs)


def reduce_by_shifts(own, other, zs, xs, z):
    swapped = swap(other)
    came = []
    for k in range(1, zs):
        sent = (own[2 * k : 2 * k + 2] + swapped[2 * k : 2 * k + 2]).astype(BF)
        came.append(lax.ppermute(sent, "z", [(i, (i + k) % zs) for i in range(zs)]))
    mine = own[1] + swapped[1]
    near = own[0] + swapped[0]
    far = own[2 * zs] + swapped[2 * zs]
    for k, got in enumerate(came, 1):
        near = near + got[0].astype(F32)
        mine = mine + jnp.where(z < k, got[1].astype(F32), 0.0)
        far = far + jnp.where(z < k, 0.0, got[1].astype(F32))
    return along_x(mine, near, far, xs)


def program(queries, keys, values, outputs, grad_out, doc_ids, owner):
    hd = keys.shape[2]
    scale = hd**-0.5
    rows, _, width = queries.shape
    total = rows * (width // hd)
    tile = min(256, total)
    group = min(512, total)
    xs, zs = lax.axis_size("x"), lax.axis_size("z")
    x, z, core = lax.axis_index("x"), lax.axis_index("z"), lax.axis_index("core")
    peers = xs * zs * 2
    per_device = owner.shape[0]
    block_len = rows // per_device
    part = keys.shape[0]
    chips = 2 * zs + 1

    extra = COUNTS + xs
    earlier = jnp.sum(
        (doc_ids[None, :] < jnp.arange(COUNTS, dtype=jnp.int32)[:, None]).astype(F32), axis=1, keepdims=True
    )
    notes = jnp.concatenate(
        [
            jnp.broadcast_to(earlier, (COUNTS, 2 * hd)),
            jnp.broadcast_to(jnp.pad(owner.astype(F32), (0, 2 * hd - per_device)), (xs, 2 * hd)),
        ],
        axis=0,
    ).astype(BF)
    mixed = jnp.transpose(jnp.concatenate([keys, values], axis=-1), (1, 0, 2))
    mixed = jnp.concatenate([mixed, jnp.broadcast_to(notes[None], (4, extra, 2 * hd))], axis=1)
    mixed = jnp.broadcast_to(mixed[:, None], (4, xs, part + extra, 2 * hd))
    mixed = lax.all_to_all(
        mixed.reshape(4 * xs, part + extra, 2 * hd),
        ("dp", "head", "x"),
        split_axis=0,
        concat_axis=0,
        tiled=True,
    ).reshape(2, 2, xs, part + extra, 2 * hd)

    def piece(back):
        got = lax.dynamic_index_in_dim(mixed, lax.rem(x - back + xs, xs), 2, keepdims=False)
        tokens = jnp.transpose(got[:, :, :part], (1, 0, 2, 3)).reshape(rows, 2 * hd)
        return jnp.concatenate([tokens, got[0, 0, part:]], axis=0)

    last, near, far = piece(0), piece(1), piece(2)
    far_other = swap(far)

    def along_z(a, b, c):
        ahead = (jnp.arange(zs) >= z)[:, None, None]
        chosen = jnp.where(ahead, a[None], c[None])
        pair = jnp.stack([jnp.broadcast_to(b[None], chosen.shape), chosen], axis=1)
        return lax.all_to_all(pair, "z", split_axis=0, concat_axis=0, tiled=True)

    held = mixed[0, 0, :, part + COUNTS, :hd]
    near_keys = jnp.concatenate([near[: rows + COUNTS, :hd], held], axis=0)
    k_own = along_z(last[:, :hd], near_keys, far[:, :hd])
    k_other = swap(k_own)
    v_own = along_z(last[:rows, hd:], near[:rows, hd:], far[:rows, hd:])

    base = (x - 2) * (zs * 2 * rows)
    me = (x * zs + z) * 2 + core
    place = jnp.stack([x, z, core, base, jnp.maximum(base + z * 2 * rows, 0), me]).astype(jnp.int32)
    q = queries.reshape(rows, width)
    do = grad_out.reshape(rows, width)
    o = outputs.reshape(rows, width)
    vmem = pl.BlockSpec(memory_space=pltpu.VMEM)
    smem = pl.BlockSpec(memory_space=pltpu.SMEM)
    anywhere = pl.BlockSpec(memory_space=pl.ANY)
    grad_shape = jax.ShapeDtypeStruct((chips, rows, hd), F32)
    params = pltpu.CompilerParams(vmem_limit_bytes=48 * 1024 * 1024)
    dv_own, dv_other, probs, info, factors = pl.pallas_call(
        functools.partial(softmax_kernel, zs=zs, scale=scale, tile=tile, group=group),
        in_specs=[smem] + [vmem] * 7,
        out_specs=[vmem, vmem, anywhere, smem, vmem],
        out_shape=[
            grad_shape,
            grad_shape,
            jax.ShapeDtypeStruct((chips, 2 * rows, total), F32),
            jax.ShapeDtypeStruct((1,), jnp.int32),
            jax.ShapeDtypeStruct((chips, 8, total), F32),
        ],
        scratch_shapes=[
            pltpu.VMEM((total, hd), BF),
            pltpu.VMEM((total, hd), BF),
            pltpu.VMEM((3 * zs, 2 * rows, hd), BF),
            pltpu.VMEM((chips, 2 * rows, total), F32),
            pltpu.VMEM((2 * rows, total), F32),
            pltpu.VMEM((2 * rows, total), BF),
            pltpu.VMEM((8, total), F32),
            pltpu.SemaphoreType.DMA((chips,)),
        ],
        compiler_params=params,
        cost_estimate=pl.CostEstimate(
            flops=12_000_000_000, bytes_accessed=20_000_000, transcendentals=4_000_000
        ),
        name="softmax_and_value_gradient",
    )(
        place,
        q,
        do,
        doc_ids.reshape(1, rows),
        k_own,
        k_other,
        far[:, :hd],
        far_other[:, :hd],
    )
    v_other = swap(v_own)
    grad_v = reduce_at_once(dv_own, dv_other, zs, xs, z)
    packed, dk_own, dk_other = pl.pallas_call(
        functools.partial(
            score_kernel, zs=zs, scale=scale, tile=tile, group=group, block=block_len
        ),
        in_specs=[smem, smem] + [vmem] * 13 + [anywhere],
        out_specs=[vmem] * 3,
        out_shape=[
            jax.ShapeDtypeStruct((peers * 2 * block_len, width // 2), BF),
            grad_shape,
            grad_shape,
        ],
        scratch_shapes=[
            pltpu.VMEM((total, hd), BF),
            pltpu.VMEM((total, hd), BF),
            pltpu.VMEM((3 * zs, 2 * rows, hd), BF),
            pltpu.VMEM((3 * zs, 2 * rows, hd), BF),
            pltpu.VMEM((chips, 2 * rows, total), F32),
            pltpu.VMEM((2 * rows, total), BF),
            pltpu.VMEM((8, total), F32),
            pltpu.VMEM((hd, total), F32),
            pltpu.SemaphoreType.DMA((chips,)),
        ],
        compiler_params=params,
        cost_estimate=pl.CostEstimate(
            flops=12_000_000_000, bytes_accessed=20_000_000, transcendentals=0
        ),
        name="score_gradient",
    )(
        place,
        info,
        q,
        do,
        o,
        k_own,
        k_other,
        far[:, :hd],
        far_other[:, :hd],
        v_own,
        v_other,
        far[:rows, hd:],
        far_other[:rows, hd:],
        factors,
        jnp.repeat(owner, block_len)[None],
        probs,
    )
    grad_k = reduce_by_shifts(dk_own, dk_other, zs, xs, z)

    seen = [k[:, 0, rows + COUNTS :, :per_device] for k in (k_own, k_other)]
    even = jnp.where(core == 0, seen[0], seen[1])
    odd = jnp.where(core == 0, seen[1], seen[0])
    owners = jnp.transpose(jnp.stack([even, odd], axis=2), (1, 0, 2, 3)).reshape(peers, per_device)
    arrived = lax.all_to_all(
        packed.reshape(peers, 2 * block_len, width // 2),
        ("x", "z", "core"),
        split_axis=0,
        concat_axis=0,
        tiled=True,
    )
    placed = pl.pallas_call(
        functools.partial(placement_kernel, block=block_len),
        in_specs=[smem, vmem, vmem],
        out_specs=vmem,
        out_shape=jax.ShapeDtypeStruct((rows, width), BF),
        name="query_gradient_placement",
    )(place, owners, arrived.reshape(packed.shape))
    return (placed.reshape(rows, 1, width), grad_k, grad_v)


def solution(mesh):
    sizes = mesh.shape
    dp, ctx, head = sizes["dp"], sizes["ctx"], sizes["head"]
    xs = 4
    fine = Mesh(
        mesh.devices.reshape(dp, xs, ctx // (2 * xs), 2, head), ("dp", "x", "z", "core", "head")
    )
    ctx_axes = ("x", "z", "core")
    heads = P(ctx_axes, ("dp", "head"), None)
    tokens = P(ctx_axes + ("head", "dp"), None, None)
    return jax.shard_map(
        program,
        mesh=fine,
        in_specs=(heads, tokens, tokens, heads, heads, P(ctx_axes), P(ctx_axes)),
        out_specs=(heads, heads, heads),
        check_vma=False,
    )
```

time: 187 us -> 171 us (0.914)
  waiting for transfers between devices: 88.2 us -> 60.6 us
  starting transfers between devices: 51.4 us -> 65.2 us
  local copies, waits for them, and re-layouts: 15 us -> 7.18 us
  other arithmetic: 9.8 us -> 15.6 us
    all_to_all x4 -> x3, waiting for transfers between devices: 50 us -> 21.8 us  [the longest x1 13.8 us: program(): lax.all_to_all(packed.reshape(peers, 2 * block_len, width // 2), ('x', 'z...]
    ppermute x4 -> x11, starting transfers between devices: 7.41 us -> 27.7 us  [the longest x7 18 us: reduce_by_shifts(): came.append(lax.ppermute(sent, 'z', [(i, (i + k) % zs) for i in range(zs)]))]
    all_to_all x4 -> x3, starting transfers between devices: 30.8 us -> 24.3 us  [the longest x1 13.3 us: program(): lax.all_to_all(packed.reshape(peers, 2 * block_len, width // 2), ('x', 'z...]
    ppermute x4 -> x11, waiting for transfers between devices: 4.68 us -> 7.88 us  [the longest x7 4.48 us: reduce_by_shifts(): came.append(lax.ppermute(sent, 'z', [(i, (i + k) % zs) for i in range(zs)]))]
    slice x3 -> x1, local copies, waits for them, and re-layouts: 3 us -> 0.01 us  [program(): held = mixed[0, 0, :, part + COUNTS, :hd]]
    convert_element_type x4, other arithmetic: 2.26 us -> 4.9 us  [the longest x1 2.12 us: reduce_at_once(): sent = (own[:2 * zs] + swapped[:2 * zs]).astype(BF).reshape(zs, 2, rows, hd)]
    ppermute x5, waiting for transfers between devices: 3.82 us -> 1.28 us  [swap(): return lax.ppermute(value, 'core', [(0, 1), (1, 0)])]
    pallas_call x0 -> x1, Pallas kernels: none -> 2.34 us  [program(): pl.pallas_call(functools.partial(placement_kernel, block=block_len), in_s...]
  transfers between devices with their start and end apart: 15 -> 21, of which waited for: 12 -> 11; matrix products, arithmetic and copies ran while one was open for 5% -> 7% of each run, Pallas kernels for 5% -> 12%
where the time goes in v3:
time: 171 us; the launch traced here: 169 us
  starting transfers between devices  65.2 us (38%)
  waiting for transfers between devices  60.6 us (35%)
  Pallas kernels  19.9 us (12%)
  other arithmetic  15.6 us (9%)
  local copies, waits for them, and re-layouts  7.18 us (4%)
    all_to_all x2, waiting for transfers between devices, along_z(): return lax.all_to_all(pair, 'z', split_axis=0, concat_axis=0, tiled=True)  29.6 us
    ppermute x7, starting transfers between devices, reduce_by_shifts(): came.append(lax.ppermute(sent, 'z', [(i, (i + k) % zs) for i in range(zs)]))  18 us
    all_to_all x1, waiting for transfers between devices, program(): lax.all_to_all(packed.reshape(peers, 2 * block_len, width // 2), ('x', 'z...  13.8 us
    all_to_all x1, starting transfers between devices, program(): lax.all_to_all(packed.reshape(peers, 2 * block_len, width // 2), ('x', 'z...  13.3 us
    all_to_all x2, starting transfers between devices, along_z(): return lax.all_to_all(pair, 'z', split_axis=0, concat_axis=0, tiled=True)  12 us
    pallas_call x1, Pallas kernels, program(): pl.pallas_call(functools.partial(score_kernel, zs=zs, scale=scale, tile=t...  9.33 us
    pallas_call x1, Pallas kernels, program(): pl.pallas_call(functools.partial(softmax_kernel, zs=zs, scale=scale, tile...  8.23 us
    all_to_all x1, waiting for transfers between devices, program(): lax.all_to_all(mixed.reshape(4 * xs, part + extra, 2 * hd), ('dp', 'head'...  8.01 us
  transfers between devices with their start and end apart: 21, of which 11 were waited for; matrix products, arithmetic and copies ran while one was open for 7% of the time, Pallas kernels for 12%

profile of v3, /device:TPU:2, one launch (start us, length us, event | category | flops | bytes accessed | tf_op | source)
XLA Modules:
  0.0 169.5 jit_solution(11674104896536425035)
XLA Ops:
  3.8 7.5 %all-to-all-start = ((bf16[16,40,256]{2,1,0:T(8,128)(2,1)}), bf16[16,40,256]{2,1,0:T(8,128)(2,1)S(1)}, u32[]{:S(2)}, u32[]{:S(2)}) async-start(bf16[16,40,256]{2,1,0:T(8,128)(2,1)} %bitcast.7), calls=%async_computation | async-start | bytes 655360 | tf_op jit(solution)/shard_map/all_to_all | solution.py:396
  11.3 8.0 %all-to-all-done = bf16[16,40,256]{2,1,0:T(8,128)(2,1)S(1)} async-done(((bf16[16,40,256]{2,1,0:T(8,128)(2,1)}), bf16[16,40,256]{2,1,0:T(8,128)(2,1)S(1)}, u32[]{:S(2)}, u32[]{:S(2)}) %all-to-all-start) | async-done | bytes 327712 | tf_op jit(solution)/shard_map/all_to_all | solution.py:396
  20.5 8.5 %all-to-all-start.1 = ((bf16[8,2,136,128]{3,2,1,0:T(8,128)(2,1)}), bf16[8,2,136,128]{3,2,1,0:T(8,128)(2,1)S(1)}, u32[]{:S(2)}, u32[]{:S(2)}) async-start(bf16[8,2,136,128]{3,2,1,0:T(8,128)(2,1)} %pad_maximum_fusion), calls=%async_computation.1 | async-start | bytes 1114112 | tf_op jit(solution)/shard_map/all_to_all | solution.py:416
  30.0 16.0 %all-to-all-done.1.k_own = bf16[8,2,136,128]{3,2,1,0:T(8,128)(2,1)S(1)} async-done(((bf16[8,2,136,128]{3,2,1,0:T(8,128)(2,1)}), bf16[8,2,136,128]{3,2,1,0:T(8,128)(2,1)S(1)}, u32[]{:S(2)}, u32[]{:S(2)}) %all-to-all-start.1) | async-done | bytes 557088 | tf_op jit(solution)/shard_map/all_to_all | solution.py:416
  46.1 3.5 %all-to-all-start.2 = ((bf16[8,2,128,128]{3,2,1,0:T(8,128)(2,1)}), bf16[8,2,128,128]{3,2,1,0:T(8,128)(2,1)S(1)}, u32[]{:S(2)}, u32[]{:S(2)}) async-start(bf16[8,2,128,128]{3,2,1,0:T(8,128)(2,1)} %pad_maximum_fusion.1), calls=%async_computation.2 | async-start | bytes 1048576 | tf_op jit(solution)/shard_map/all_to_all | solution.py:416
  50.4 1.3 collective-permute-done.1
  51.7 13.6 %all-to-all-done.2.v_own = bf16[8,2,128,128]{3,2,1,0:T(8,128)(2,1)S(1)} async-done(((bf16[8,2,128,128]{3,2,1,0:T(8,128)(2,1)}), bf16[8,2,128,128]{3,2,1,0:T(8,128)(2,1)S(1)}, u32[]{:S(2)}, u32[]{:S(2)}) %all-to-all-start.2) | async-done | bytes 524320 | tf_op jit(solution)/shard_map/all_to_all | solution.py:416
  66.1 1.1 copy-done.3
  67.2 0.9 copy-done.4
  68.1 0.9 copy-done.5
  69.1 8.2 %softmax_and_value_gradient.1 = (f32[17,128,128]{2,1,0:T(8,128)S(1)}, f32[17,128,128]{2,1,0:T(8,128)}, f32[17,256,1024]{2,1,0:T(8,128)}, s32[1]{0:T(128)}, f32[17,8,1024]{2,1,0:T(8,128)S(1)}) custom-call(s32[6]{0:T(128)S(1)} %stack.40.place_ref, bf16[128,1024]{1,0:T(8,128)(2,1)S(1)} %bitcast.94, bf16[128,1024]{1,0:T(8,128)(2,1)S(1)} %bitcast.96, ...), custom_call_target="tpu_custom_call" | custom-call | flops 12000000000 | bytes 20000000 | tf_op jit(solution)/shard_map/softmax_and_value_gradient/pallas_call | solution.py:435
  77.9 9.3 %score_gradient.1 = (bf16[512,512]{1,0:T(8,128)(2,1)S(1)}, f32[17,128,128]{2,1,0:T(8,128)S(1)}, f32[17,128,128]{2,1,0:T(8,128)}) custom-call(s32[6]{0:T(128)S(1)} %stack.40.place_ref, s32[1]{0:T(128)} %get-tuple-element.11.info_ref, bf16[128,1024]{1,0:T(8,128)(2,1)S(1)} %bitcast.95, bf16[128,1024]{1,0:T(8,128)(2,1)S(1)} %bitcast.97, ...), custom_call_target="tpu_custom_call" | custom-call | flops 12000000000 | bytes 20000000 | tf_op jit(solution)/shard_map/score_gradient/pallas_call | solution.py:473
  88.1 13.3 %all-to-all-start.3 = ((bf16[64,8,512]{2,1,0:T(8,128)(2,1)}), bf16[64,8,512]{2,1,0:T(8,128)(2,1)S(1)}, u32[]{:S(2)}, u32[]{:S(2)}) async-start(bf16[64,8,512]{2,1,0:T(8,128)(2,1)} %bitcast.93), calls=%async_computation.3 | async-start | bytes 1048576 | tf_op jit(solution)/shard_map/all_to_all | solution.py:524
  102.1 2.1 %fusion = bf16[16,128,128]{2,1,0:T(8,128)(2,1)} fusion(f32[17,128,128]{2,1,0:T(8,128)} %collective-permute-done.13, f32[17,128,128]{2,1,0:T(8,128)S(1)} %get-tuple-element.17), kind=kLoop, calls=%fused_computation.1 | loop fusion | flops 524288 | bytes 2621440 | tf_op jit(solution)/shard_map/convert_element_type | solution.py:341
  104.3 13.8 %all-to-all-done.3 = bf16[64,8,512]{2,1,0:T(8,128)(2,1)S(1)} async-done(((bf16[64,8,512]{2,1,0:T(8,128)(2,1)}), bf16[64,8,512]{2,1,0:T(8,128)(2,1)S(1)}, u32[]{:S(2)}, u32[]{:S(2)}) %all-to-all-start.3) | async-done | bytes 524320 | tf_op jit(solution)/shard_map/all_to_all | solution.py:524
  118.8 3.6 %all-to-all-start.4 = ((bf16[8,2,128,128]{3,2,1,0:T(8,128)(2,1)}), bf16[8,2,128,128]{3,2,1,0:T(8,128)(2,1)S(1)}, u32[]{:S(2)}, u32[]{:S(2)}) async-start(bf16[8,2,128,128]{3,2,1,0:T(8,128)(2,1)} %bitcast.39), calls=%async_computation.4 | async-start | bytes 1048576 | tf_op jit(solution)/shard_map/all_to_all | solution.py:342
  122.4 2.0 %fusion.7 = (bf16[2,128,128]{2,1,0:T(8,128)(2,1)S(1)}, bf16[2,128,128]{2,1,0:T(8,128)(2,1)S(1)}, bf16[2,128,128]{2,1,0:T(8,128)(2,1)S(1)}, bf16[2,128,128]{2,1,0...) fusion(f32[17,128,128]{2,1,0:T(8,128)} %collective-permute-done.3, ...), kind=kLoop, calls=%fused_computation.23 | loop fusion | flops 458752 | bytes 2293760 | tf_op jit(solution)/shard_map/convert_element_type | solution.py:355
  124.4 3.2 %collective-permute-start.10 = (bf16[2,128,128]{2,1,0:T(8,128)(2,1)S(1)}, bf16[2,128,128]{2,1,0:T(8,128)(2,1)S(1)}, u32[]{:S(2)}, u32[]{:S(2)}) collective-permute-start(bf16[2,128,128]{2,1,0:T(8,128)(2,1)S(1)} %get-tuple-element.22), channel_id=1, source_target_pairs={{0,28},{4,0},{8,4},{12,8},{16,12},{20,16},{24,20},{28,24},{1,29},{... | collective-permute-start | bytes 196616 | tf_op jit(solution)/shard_map/ppermute | solution.py:356
  128.4 1.8 %collective-permute-start.5 = (bf16[2,128,128]{2,1,0:T(8,128)(2,1)}, bf16[2,128,128]{2,1,0:T(8,128)(2,1)S(1)}, u32[]{:S(2)}, u32[]{:S(2)}) collective-permute-start(bf16[2,128,128]{2,1,0:T(8,128)(2,1)} %get-tuple-element.27), channel_id=1, source_target_pairs={{0,8},{4,12},{8,16},{12,20},{16,24},{20,28},{24,0},{28,4},{1,9},{5... | collective-permute-start | bytes 196616 | tf_op jit(solution)/shard_map/ppermute | solution.py:356
  130.2 3.6 %collective-permute-start.6 = (bf16[2,128,128]{2,1,0:T(8,128)(2,1)}, bf16[2,128,128]{2,1,0:T(8,128)(2,1)S(1)}, u32[]{:S(2)}, u32[]{:S(2)}) collective-permute-start(bf16[2,128,128]{2,1,0:T(8,128)(2,1)} %get-tuple-element.26), channel_id=1, source_target_pairs={{0,12},{4,16},{8,20},{12,24},{16,28},{20,0},{24,4},{28,8},{1,13},{... | collective-permute-start | bytes 196616 | tf_op jit(solution)/shard_map/ppermute | solution.py:356
  133.7 1.5 collective-permute-start.7
  135.2 3.6 %collective-permute-done.10 = bf16[2,128,128]{2,1,0:T(8,128)(2,1)S(1)} collective-permute-done((bf16[2,128,128]{2,1,0:T(8,128)(2,1)S(1)}, bf16[2,128,128]{2,1,0:T(8,128)(2,1)S(1)}, u32[]{:S(2)}, u32[]{:S(2)}) %collective-permute-start.10) | collective-permute-done | bytes 65568 | tf_op jit(solution)/shard_map/ppermute | solution.py:356
  138.8 3.7 %collective-permute-start.8 = (bf16[2,128,128]{2,1,0:T(8,128)(2,1)}, bf16[2,128,128]{2,1,0:T(8,128)(2,1)S(1)}, u32[]{:S(2)}, u32[]{:S(2)}) collective-permute-start(bf16[2,128,128]{2,1,0:T(8,128)(2,1)} %get-tuple-element.24), channel_id=1, source_target_pairs={{0,20},{4,24},{8,28},{12,0},{16,4},{20,8},{24,12},{28,16},{1,21},{... | collective-permute-start | bytes 196616 | tf_op jit(solution)/shard_map/ppermute | solution.py:356
  142.5 4.2 %collective-permute-start.9 = (bf16[2,128,128]{2,1,0:T(8,128)(2,1)S(1)}, bf16[2,128,128]{2,1,0:T(8,128)(2,1)S(1)}, u32[]{:S(2)}, u32[]{:S(2)}) collective-permute-start(bf16[2,128,128]{2,1,0:T(8,128)(2,1)S(1)} %get-tuple-element.23), channel_id=1, source_target_pairs={{0,24},{4,28},{8,0},{12,4},{16,8},{20,12},{24,16},{28,20},{1,25},{... | collective-permute-start | bytes 196616 | tf_op jit(solution)/shard_map/ppermute | solution.py:356
  147.4 2.3 %query_gradient_placement.1 = bf16[128,1024]{1,0:T(8,128)(2,1)} custom-call(s32[6]{0:T(128)} %copy-done.1, bf16[64,32]{1,0:T(8,128)(2,1)} %bitcast.111, bf16[512,512]{1,0:T(8,128)(2,1)} %bitcast.100), custom_call_target="tpu_custom_call" | custom-call | tf_op jit(solution)/shard_map/query_gradient_placement/pallas_call | solution.py:531
  151.5 5.2 %collective-permute-start.11 = (f32[128,128]{1,0:T(8,128)S(1)}, f32[128,128]{1,0:T(8,128)S(1)}, u32[]{:S(2)}, u32[]{:S(2)}) collective-permute-start(f32[128,128]{1,0:T(8,128)S(1)} %fusion.36), channel_id=1, source_target_pairs={{32,0},{64,32},{96,64},{33,1},{65,33},{97,65},{34,2},{66,34},{98,6... | collective-permute-start | bytes 196616 | tf_op jit(solution)/shard_map/ppermute | solution.py:333
  156.7 1.5 fusion.27
  158.2 1.3 collective-permute-start.12
  160.7 1.3 collective-permute-start.15
  162.0 1.9 %collective-permute-start.14 = (f32[128,128]{1,0:T(8,128)S(1)}, f32[128,128]{1,0:T(8,128)S(1)}, u32[]{:S(2)}, u32[]{:S(2)}) collective-permute-start(f32[128,128]{1,0:T(8,128)S(1)} %slice_reduce_fusion), channel_id=1, source_target_pairs={{32,0},{64,32},{96,64},{33,1},{65,33},{97,65},{34,2},{66,34},{98,6... | collective-permute-start | bytes 196616 | tf_op jit(solution)/shard_map/ppermute | solution.py:333
  163.9 2.6 %collective-permute-done.12 = f32[128,128]{1,0:T(8,128)S(1)} collective-permute-done((f32[128,128]{1,0:T(8,128)}, f32[128,128]{1,0:T(8,128)S(1)}, u32[]{:S(2)}, u32[]{:S(2)}) %collective-permute-start.12) | collective-permute-done | bytes 65568 | tf_op jit(solution)/shard_map/ppermute | solution.py:334
  166.5 1.5 fusion.41
  (87 shorter events, 15.6 us)
Async XLA Ops:
  3.8 15.5 %all-to-all-start = ((bf16[16,40,256]{2,1,0:T(8,128)(2,1)}), bf16[16,40,256]{2,1,0:T(8,128)(2,1)S(1)}, u32[]{:S(2)}, u32[]{:S(2)}) async-start(bf16[16,40,256]{2,1,0:T(8,128)(2,1)} %bitcast.7), calls=%async_computation | async-start | bytes 655360 | tf_op jit(solution)/shard_map/all_to_all | solution.py:396
  20.5 25.6 %all-to-all-start.1 = ((bf16[8,2,136,128]{3,2,1,0:T(8,128)(2,1)}), bf16[8,2,136,128]{3,2,1,0:T(8,128)(2,1)S(1)}, u32[]{:S(2)}, u32[]{:S(2)}) async-start(bf16[8,2,136,128]{3,2,1,0:T(8,128)(2,1)} %pad_maximum_fusion), calls=%async_computation.1 | async-start | bytes 1114112 | tf_op jit(solution)/shard_map/all_to_all | solution.py:416
  29.1 21.0 %copy-start.9 = (s32[32]{0:T(128)S(1)}, s32[32]{0:T(128)}, u32[]{:S(2)}) copy-start(s32[32]{0:T(128)} %param.13) | copy-start | bytes 388
  29.2 37.0 %copy-start.7 = (s32[128]{0:T(128)S(1)}, s32[128]{0:T(128)}, u32[]{:S(2)}) copy-start(s32[128]{0:T(128)} %param.12) | copy-start | bytes 1540
  46.1 19.2 %all-to-all-start.2 = ((bf16[8,2,128,128]{3,2,1,0:T(8,128)(2,1)}), bf16[8,2,128,128]{3,2,1,0:T(8,128)(2,1)S(1)}, u32[]{:S(2)}, u32[]{:S(2)}) async-start(bf16[8,2,128,128]{3,2,1,0:T(8,128)(2,1)} %pad_maximum_fusion.1), calls=%async_computation.2 | async-start | bytes 1048576 | tf_op jit(solution)/shard_map/all_to_all | solution.py:416
  49.6 15.7 %collective-permute-start = (bf16[8,2,136,128]{3,2,1,0:T(8,128)(2,1)S(1)}, bf16[8,2,136,128]{3,2,1,0:T(8,128)(2,1)S(1)}, u32[]{:S(2)}, u32[]{:S(2)}) collective-permute-start(bf16[8,2,136,128]{3,2,1,0:T(8,128)(2,1)S(1)} %all-to-all-done.1.k_own), channel_id=1, source_target_pairs={{0,2},{2,0},{1,3},{3,1},{4,6},{6,4},{5,7},{7,5},{8,10},{10,8},{9,1... | collective-permute-start | bytes 1671176 | tf_op jit(solution)/shard_map/ppermute | solution.py:311
  49.7 2.0 %collective-permute-start.1 = (bf16[136,256]{1,0:T(8,128)(2,1)S(1)}, bf16[136,256]{1,0:T(8,128)(2,1)S(1)}, u32[]{:S(2)}, u32[]{:S(2)}) collective-permute-start(bf16[136,256]{1,0:T(8,128)(2,1)S(1)} %pad_maximum_fusion.2), channel_id=1, source_target_pairs={{0,2},{2,0},{1,3},{3,1},{4,6},{6,4},{5,7},{7,5},{8,10},{10,8},{9,1... | collective-permute-start | bytes 208904 | tf_op jit(solution)/shard_map/ppermute | solution.py:311
  50.4 27.5 %copy-start.1 = (s32[6]{0:T(128)}, s32[6]{0:T(128)S(1)}, u32[]{:S(2)}) copy-start(s32[6]{0:T(128)S(1)} %stack.40.place_ref) | copy-start | bytes 76
  65.3 12.6 %collective-permute-start.2 = (bf16[8,2,128,128]{3,2,1,0:T(8,128)(2,1)S(1)}, bf16[8,2,128,128]{3,2,1,0:T(8,128)(2,1)S(1)}, u32[]{:S(2)}, u32[]{:S(2)}) collective-permute-start(bf16[8,2,128,128]{3,2,1,0:T(8,128)(2,1)S(1)} %all-to-all-done.2.v_own), channel_id=1, source_target_pairs={{0,2},{2,0},{1,3},{3,1},{4,6},{6,4},{5,7},{7,5},{8,10},{10,8},{9,1... | collective-permute-start | bytes 1572872 | tf_op jit(solution)/shard_map/ppermute | solution.py:311
  65.3 0.8 copy-start.2
  66.1 1.1 copy-start.3
  67.2 0.9 copy-start.4
  68.1 0.9 copy-start.5
  69.1 8.8 %copy-start.6 = (bf16[128,1,1024]{2,0,1:T(8,128)(2,1)S(1)}, bf16[128,1,1024]{2,0,1:T(8,128)(2,1)}, u32[]{:S(2)}) copy-start(bf16[128,1,1024]{2,0,1:T(8,128)(2,1)} %param.10) | copy-start | bytes 786436
  77.3 24.8 %collective-permute-start.13 = (f32[17,128,128]{2,1,0:T(8,128)}, f32[17,128,128]{2,1,0:T(8,128)}, u32[]{:S(2)}, u32[]{:S(2)}) collective-permute-start(f32[17,128,128]{2,1,0:T(8,128)} %get-tuple-element.18), channel_id=1, source_target_pairs={{0,2},{2,0},{1,3},{3,1},{4,6},{6,4},{5,7},{7,5},{8,10},{10,8},{9,1... | collective-permute-start | bytes 3342344 | tf_op jit(solution)/shard_map/ppermute | solution.py:311
  87.2 0.8 copy-start
  88.0 34.4 %collective-permute-start.3 = (f32[17,128,128]{2,1,0:T(8,128)}, f32[17,128,128]{2,1,0:T(8,128)}, u32[]{:S(2)}, u32[]{:S(2)}) collective-permute-start(f32[17,128,128]{2,1,0:T(8,128)} %get-tuple-element.16), channel_id=1, source_target_pairs={{0,2},{2,0},{1,3},{3,1},{4,6},{6,4},{5,7},{7,5},{8,10},{10,8},{9,1... | collective-permute-start | bytes 3342344 | tf_op jit(solution)/shard_map/ppermute | solution.py:311
  88.1 29.9 %all-to-all-start.3 = ((bf16[64,8,512]{2,1,0:T(8,128)(2,1)}), bf16[64,8,512]{2,1,0:T(8,128)(2,1)S(1)}, u32[]{:S(2)}, u32[]{:S(2)}) async-start(bf16[64,8,512]{2,1,0:T(8,128)(2,1)} %bitcast.93), calls=%async_computation.3 | async-start | bytes 1048576 | tf_op jit(solution)/shard_map/all_to_all | solution.py:524
  118.0 0.8 copy-start.8
  118.8 40.7 %all-to-all-start.4 = ((bf16[8,2,128,128]{3,2,1,0:T(8,128)(2,1)}), bf16[8,2,128,128]{3,2,1,0:T(8,128)(2,1)S(1)}, u32[]{:S(2)}, u32[]{:S(2)}) async-start(bf16[8,2,128,128]{3,2,1,0:T(8,128)(2,1)} %bitcast.39), calls=%async_computation.4 | async-start | bytes 1048576 | tf_op jit(solution)/shard_map/all_to_all | solution.py:342
  124.4 14.4 %collective-permute-start.10 = (bf16[2,128,128]{2,1,0:T(8,128)(2,1)S(1)}, bf16[2,128,128]{2,1,0:T(8,128)(2,1)S(1)}, u32[]{:S(2)}, u32[]{:S(2)}) collective-permute-start(bf16[2,128,128]{2,1,0:T(8,128)(2,1)S(1)} %get-tuple-element.22), channel_id=1, source_target_pairs={{0,28},{4,0},{8,4},{12,8},{16,12},{20,16},{24,20},{28,24},{1,29},{... | collective-permute-start | bytes 196616 | tf_op jit(solution)/shard_map/ppermute | solution.py:356
  127.6 14.8 %collective-permute-start.4 = (bf16[2,128,128]{2,1,0:T(8,128)(2,1)S(1)}, bf16[2,128,128]{2,1,0:T(8,128)(2,1)S(1)}, u32[]{:S(2)}, u32[]{:S(2)}) collective-permute-start(bf16[2,128,128]{2,1,0:T(8,128)(2,1)S(1)} %get-tuple-element.21), channel_id=1, source_target_pairs={{0,4},{4,8},{8,12},{12,16},{16,20},{20,24},{24,28},{28,0},{1,5},{5... | collective-permute-start | bytes 196616 | tf_op jit(solution)/shard_map/ppermute | solution.py:356
  128.4 21.3 %collective-permute-start.5 = (bf16[2,128,128]{2,1,0:T(8,128)(2,1)}, bf16[2,128,128]{2,1,0:T(8,128)(2,1)S(1)}, u32[]{:S(2)}, u32[]{:S(2)}) collective-permute-start(bf16[2,128,128]{2,1,0:T(8,128)(2,1)} %get-tuple-element.27), channel_id=1, source_target_pairs={{0,8},{4,12},{8,16},{12,20},{16,24},{20,28},{24,0},{28,4},{1,9},{5... | collective-permute-start | bytes 196616 | tf_op jit(solution)/shard_map/ppermute | solution.py:356
  130.2 19.5 %collective-permute-start.6 = (bf16[2,128,128]{2,1,0:T(8,128)(2,1)}, bf16[2,128,128]{2,1,0:T(8,128)(2,1)S(1)}, u32[]{:S(2)}, u32[]{:S(2)}) collective-permute-start(bf16[2,128,128]{2,1,0:T(8,128)(2,1)} %get-tuple-element.26), channel_id=1, source_target_pairs={{0,12},{4,16},{8,20},{12,24},{16,28},{20,0},{24,4},{28,8},{1,13},{... | collective-permute-start | bytes 196616 | tf_op jit(solution)/shard_map/ppermute | solution.py:356
  133.7 16.3 %collective-permute-start.7 = (bf16[2,128,128]{2,1,0:T(8,128)(2,1)}, bf16[2,128,128]{2,1,0:T(8,128)(2,1)S(1)}, u32[]{:S(2)}, u32[]{:S(2)}) collective-permute-start(bf16[2,128,128]{2,1,0:T(8,128)(2,1)} %get-tuple-element.25), channel_id=1, source_target_pairs={{0,16},{4,20},{8,24},{12,28},{16,0},{20,4},{24,8},{28,12},{1,17},{... | collective-permute-start | bytes 196616 | tf_op jit(solution)/shard_map/ppermute | solution.py:356
  138.8 11.3 %collective-permute-start.8 = (bf16[2,128,128]{2,1,0:T(8,128)(2,1)}, bf16[2,128,128]{2,1,0:T(8,128)(2,1)S(1)}, u32[]{:S(2)}, u32[]{:S(2)}) collective-permute-start(bf16[2,128,128]{2,1,0:T(8,128)(2,1)} %get-tuple-element.24), channel_id=1, source_target_pairs={{0,20},{4,24},{8,28},{12,0},{16,4},{20,8},{24,12},{28,16},{1,21},{... | collective-permute-start | bytes 196616 | tf_op jit(solution)/shard_map/ppermute | solution.py:356
  142.5 8.1 %collective-permute-start.9 = (bf16[2,128,128]{2,1,0:T(8,128)(2,1)S(1)}, bf16[2,128,128]{2,1,0:T(8,128)(2,1)S(1)}, u32[]{:S(2)}, u32[]{:S(2)}) collective-permute-start(bf16[2,128,128]{2,1,0:T(8,128)(2,1)S(1)} %get-tuple-element.23), channel_id=1, source_target_pairs={{0,24},{4,28},{8,0},{12,4},{16,8},{20,12},{24,16},{28,20},{1,25},{... | collective-permute-start | bytes 196616 | tf_op jit(solution)/shard_map/ppermute | solution.py:356
  151.5 12.4 %collective-permute-start.11 = (f32[128,128]{1,0:T(8,128)S(1)}, f32[128,128]{1,0:T(8,128)S(1)}, u32[]{:S(2)}, u32[]{:S(2)}) collective-permute-start(f32[128,128]{1,0:T(8,128)S(1)} %fusion.36), channel_id=1, source_target_pairs={{32,0},{64,32},{96,64},{33,1},{65,33},{97,65},{34,2},{66,34},{98,6... | collective-permute-start | bytes 196616 | tf_op jit(solution)/shard_map/ppermute | solution.py:333
  158.2 8.3 %collective-permute-start.12 = (f32[128,128]{1,0:T(8,128)}, f32[128,128]{1,0:T(8,128)S(1)}, u32[]{:S(2)}, u32[]{:S(2)}) collective-permute-start(f32[128,128]{1,0:T(8,128)} %fusion.27), channel_id=1, source_target_pairs={{64,0},{96,32},{65,1},{97,33},{66,2},{98,34},{67,3},{99,35},{68,4}... | collective-permute-start | bytes 196616 | tf_op jit(solution)/shard_map/ppermute | solution.py:334
  160.7 7.8 %collective-permute-start.15 = (f32[128,128]{1,0:T(8,128)S(1)}, f32[128,128]{1,0:T(8,128)S(1)}, u32[]{:S(2)}, u32[]{:S(2)}) collective-permute-start(f32[128,128]{1,0:T(8,128)S(1)} %fusion.28), channel_id=1, source_target_pairs={{64,0},{96,32},{65,1},{97,33},{66,2},{98,34},{67,3},{99,35},{68,4}... | collective-permute-start | bytes 196616 | tf_op jit(solution)/shard_map/ppermute | solution.py:334
  162.0 6.9 %collective-permute-start.14 = (f32[128,128]{1,0:T(8,128)S(1)}, f32[128,128]{1,0:T(8,128)S(1)}, u32[]{:S(2)}, u32[]{:S(2)}) collective-permute-start(f32[128,128]{1,0:T(8,128)S(1)} %slice_reduce_fusion), channel_id=1, source_target_pairs={{32,0},{64,32},{96,64},{33,1},{65,33},{97,65},{34,2},{66,34},{98,6... | collective-permute-start | bytes 196616 | tf_op jit(solution)/shard_map/ppermute | solution.py:333

commit v4 on v3

--- a/solution.py
+++ b/solution.py
@@ -10,6 +10,7 @@
 
 
 NEG_FILL = -1e30
+VMEM_BYTES = 60 * 1024 * 1024
 BF = jnp.bfloat16
 F32 = jnp.float32
 COUNTS = 4
@@ -311,31 +312,67 @@
     return lax.ppermute(value, "core", [(0, 1), (1, 0)])
 
 
-def placement_kernel(place_ref, owners_ref, arrived_ref, out_ref, *, block):
-    peers, per_device = owners_ref.shape
-    rows, spots = out_ref.shape[0], arrived_ref.shape[0]
-    half_width = arrived_ref.shape[1]
-    hit = (owners_ref[...].astype(F32) == place_ref[5].astype(F32)).astype(F32).astype(BF)
-    slot = lax.broadcasted_iota(jnp.int32, (rows, per_device), 0) // block
-    to_rows = (slot == lax.broadcasted_iota(jnp.int32, (rows, per_device), 1)).astype(F32).astype(BF)
-    peer = lax.broadcasted_iota(jnp.int32, (peers, spots), 1) // (2 * block)
-    to_spots = (peer == lax.broadcasted_iota(jnp.int32, (peers, spots), 0)).astype(F32).astype(BF)
-    pick = nn(nt(to_rows, hit).astype(BF), to_spots)
+def first_payload_kernel(keys_ref, values_ref, doc_ref, owner_ref, out_ref, notes, *, xs):
+    part, groups, hd = keys_ref.shape
+    extra, width = notes.shape
+    per_device = owner_ref.shape[1]
+    row = lax.broadcasted_iota(jnp.int32, (extra, doc_ref.shape[1]), 0)
+    earlier = jnp.sum((doc_ref[...] < row).astype(F32), axis=1, keepdims=True)
+    notes[...] = jnp.broadcast_to(earlier, (extra, width))
+    notes[COUNTS:, :per_device] = jnp.broadcast_to(
+        owner_ref[...].astype(F32), (extra - COUNTS, per_device)
+    )
+    low = notes[...].astype(BF)
+    for g in range(groups):
+        k, v = keys_ref[:, g, :], values_ref[:, g, :]
+        for at in range(g * xs, (g + 1) * xs):
+            out_ref[at, :part, :hd] = k
+            out_ref[at, :part, hd:] = v
+            out_ref[at, part:, :] = low
+
+
+def pick_kernel(place_ref, k_own, k_other, pick_ref, *, block, per_device, xs):
+    zs, _, tall, hd = k_own.shape
+    extra = COUNTS + xs
+    first = tall - extra
+    rows, spots = pick_ref.shape[1:]
+    core, me = place_ref[2], place_ref[5]
+    slot = lax.broadcasted_iota(jnp.int32, (rows, hd), 0) // block
+    to_rows = (slot == lax.broadcasted_iota(jnp.int32, (rows, hd), 1)).astype(F32).astype(BF)
+    held = lax.broadcasted_iota(jnp.int32, (zs * extra, hd), 0) % extra >= COUNTS
+    held = held & (lax.broadcasted_iota(jnp.int32, (zs * extra, hd), 1) < per_device)
+    line = lax.broadcasted_iota(jnp.int32, (zs * extra, spots), 0)
+    peer = lax.broadcasted_iota(jnp.int32, (zs * extra, spots), 1) // (2 * block)
+    pick = jnp.zeros((rows, spots), F32)
+    for notes, c in ((k_own, core), (k_other, 1 - core)):
+        owners = jnp.concatenate([notes[zz, 0, first:, :].astype(F32) for zz in range(zs)], axis=0)
+        hit = (held & (owners == me.astype(F32))).astype(F32).astype(BF)
+        source = ((line % extra - COUNTS) * zs + line // extra) * 2 + c
+        to_spots = ((source == peer) & (line % extra >= COUNTS)).astype(F32).astype(BF)
+        pick = pick + nn(nt(to_rows, hit).astype(BF), to_spots)
     row = lax.broadcasted_iota(jnp.int32, (rows, spots), 0)
     spot = lax.broadcasted_iota(jnp.int32, (rows, spots), 1)
     same = spot % block == row % block
     for h in range(2):
-        chosen = jnp.where(same & (spot // block % 2 == h), pick, 0.0).astype(BF)
-        out_ref[:, h * half_width : (h + 1) * half_width] = nn(chosen, arrived_ref[...]).astype(BF)
-
-
-def along_x(mine, near, far, xs):
+        pick_ref[h] = jnp.where(same & (spot // block % 2 == h), pick, 0.0).astype(BF)
+
+
+def placement_kernel(pick_ref, arrived_ref, out_ref):
+    half_width = arrived_ref.shape[1]
+    for h in range(2):
+        out_ref[:, h * half_width : (h + 1) * half_width] = nn(
+            pick_ref[h], arrived_ref[...]
+        ).astype(BF)
+
+
+def along_x(parts, xs):
+    mine, near, far = parts
     from_next = lax.ppermute(near, "x", [(i, i - 1) for i in range(1, xs)])
     from_last = lax.ppermute(far, "x", [(i, i - 2) for i in range(2, xs)])
-    return (mine + from_next + from_last).astype(BF)[:, None, :]
-
-
-def reduce_at_once(own, other, zs, xs, z):
+    return (mine + from_next + from_last).astype(BF)
+
+
+def reduce_at_once(own, other, zs, z):
     rows, hd = own.shape[1:]
     swapped = swap(other)
     sent = (own[: 2 * zs] + swapped[: 2 * zs]).astype(BF).reshape(zs, 2, rows, hd)
@@ -345,10 +382,10 @@
     mine = jnp.sum(jnp.where(later, came[:, 1], 0.0), axis=0)
     near = jnp.sum(came[:, 0], axis=0)
     far = jnp.sum(jnp.where(later, 0.0, came[:, 1]), axis=0) + own[2 * zs] + swapped[2 * zs]
-    return along_x(mine, near, far, xs)
-
-
-def reduce_by_shifts(own, other, zs, xs, z):
+    return mine, near, far
+
+
+def reduce_by_shifts(own, other, zs, z):
     swapped = swap(other)
     came = []
     for k in range(1, zs):
@@ -361,7 +398,7 @@
         near = near + got[0].astype(F32)
         mine = mine + jnp.where(z < k, got[1].astype(F32), 0.0)
         far = far + jnp.where(z < k, 0.0, got[1].astype(F32))
-    return along_x(mine, near, far, xs)
+    return mine, near, far
 
 
 def program(queries, keys, values, outputs, grad_out, doc_ids, owner):
@@ -380,21 +417,19 @@
     chips = 2 * zs + 1
 
     extra = COUNTS + xs
-    earlier = jnp.sum(
-        (doc_ids[None, :] < jnp.arange(COUNTS, dtype=jnp.int32)[:, None]).astype(F32), axis=1, keepdims=True
-    )
-    notes = jnp.concatenate(
-        [
-            jnp.broadcast_to(earlier, (COUNTS, 2 * hd)),
-            jnp.broadcast_to(jnp.pad(owner.astype(F32), (0, 2 * hd - per_device)), (xs, 2 * hd)),
-        ],
-        axis=0,
-    ).astype(BF)
-    mixed = jnp.transpose(jnp.concatenate([keys, values], axis=-1), (1, 0, 2))
-    mixed = jnp.concatenate([mixed, jnp.broadcast_to(notes[None], (4, extra, 2 * hd))], axis=1)
-    mixed = jnp.broadcast_to(mixed[:, None], (4, xs, part + extra, 2 * hd))
+    vmem = pl.BlockSpec(memory_space=pltpu.VMEM)
+    smem = pl.BlockSpec(memory_space=pltpu.SMEM)
+    anywhere = pl.BlockSpec(memory_space=pl.ANY)
+    mixed = pl.pallas_call(
+        functools.partial(first_payload_kernel, xs=xs),
+        in_specs=[vmem] * 4,
+        out_specs=vmem,
+        out_shape=jax.ShapeDtypeStruct((4 * xs, part + extra, 2 * hd), BF),
+        scratch_shapes=[pltpu.VMEM((extra, 2 * hd), F32)],
+        name="first_payload",
+    )(keys, values, doc_ids[None], owner[None])
     mixed = lax.all_to_all(
-        mixed.reshape(4 * xs, part + extra, 2 * hd),
+        mixed,
         ("dp", "head", "x"),
         split_axis=0,
         concat_axis=0,
@@ -427,11 +462,8 @@
     q = queries.reshape(rows, width)
     do = grad_out.reshape(rows, width)
     o = outputs.reshape(rows, width)
-    vmem = pl.BlockSpec(memory_space=pltpu.VMEM)
-    smem = pl.BlockSpec(memory_space=pltpu.SMEM)
-    anywhere = pl.BlockSpec(memory_space=pl.ANY)
     grad_shape = jax.ShapeDtypeStruct((chips, rows, hd), F32)
-    params = pltpu.CompilerParams(vmem_limit_bytes=48 * 1024 * 1024)
+    params = pltpu.CompilerParams(vmem_limit_bytes=VMEM_BYTES)
     dv_own, dv_other, probs, info, factors = pl.pallas_call(
         functools.partial(softmax_kernel, zs=zs, scale=scale, tile=tile, group=group),
         in_specs=[smem] + [vmem] * 7,
@@ -469,7 +501,7 @@
         far_other[:, :hd],
     )
     v_other = swap(v_own)
-    grad_v = reduce_at_once(dv_own, dv_other, zs, xs, z)
+    parts_v = reduce_at_once(dv_own, dv_other, zs, z)
     packed, dk_own, dk_other = pl.pallas_call(
         functools.partial(
             score_kernel, zs=zs, scale=scale, tile=tile, group=group, block=block_len
@@ -515,12 +547,18 @@
         jnp.repeat(owner, block_len)[None],
         probs,
     )
-    grad_k = reduce_by_shifts(dk_own, dk_other, zs, xs, z)
-
-    seen = [k[:, 0, rows + COUNTS :, :per_device] for k in (k_own, k_other)]
-    even = jnp.where(core == 0, seen[0], seen[1])
-    odd = jnp.where(core == 0, seen[1], seen[0])
-    owners = jnp.transpose(jnp.stack([even, odd], axis=2), (1, 0, 2, 3)).reshape(peers, per_device)
+    parts_k = reduce_by_shifts(dk_own, dk_other, zs, z)
+    grads = along_x([jnp.concatenate(pair, axis=1) for pair in zip(parts_k, parts_v)], xs)
+    grad_k, grad_v = grads[:, None, :hd], grads[:, None, hd:]
+
+    pick = pl.pallas_call(
+        functools.partial(pick_kernel, block=block_len, per_device=per_device, xs=xs),
+        in_specs=[smem, vmem, vmem],
+        out_specs=vmem,
+        out_shape=jax.ShapeDtypeStruct((2, rows, peers * 2 * block_len), BF),
+        cost_estimate=pl.CostEstimate(flops=100_000_000, bytes_accessed=1_000_000, transcendentals=0),
+        name="placement_choice",
+    )(place, k_own, k_other)
     arrived = lax.all_to_all(
         packed.reshape(peers, 2 * block_len, width // 2),
         ("x", "z", "core"),
@@ -529,12 +567,13 @@
         tiled=True,
     )
     placed = pl.pallas_call(
-        functools.partial(placement_kernel, block=block_len),
-        in_specs=[smem, vmem, vmem],
+        placement_kernel,
+        in_specs=[vmem, vmem],
         out_specs=vmem,
         out_shape=jax.ShapeDtypeStruct((rows, width), BF),
+        compiler_params=params,
         name="query_gradient_placement",
-    )(place, owners, arrived.reshape(packed.shape))
+    )(pick, arrived.reshape(packed.shape))
     return (placed.reshape(rows, 1, width), grad_k, grad_v)
 
 

time: 171 us -> 168 us (0.982)
  other arithmetic: 15.6 us -> 6.61 us
  Pallas kernels: 19.9 us -> 27.1 us
  waiting for transfers between devices: 60.6 us -> 62.8 us
  starting transfers between devices: 65.2 us -> 63.3 us
    pallas_call x1 -> x3, Pallas kernels: 2.34 us -> 6.11 us  [the longest x1 2.3 us: program(): pl.pallas_call(functools.partial(pick_kernel, block=block_len, per_device...]
    ppermute x2 -> x1, waiting for transfers between devices: 3.01 us -> 6.48 us  [along_x(): from_last = lax.ppermute(far, 'x', [(i, i - 2) for i in range(2, xs)])]
    unnamed x21, local copies, waits for them, and re-layouts: 5.36 us -> 2.7 us
    ppermute x2 -> x1, starting transfers between devices: 7.15 us -> 4.57 us  [along_x(): from_next = lax.ppermute(near, 'x', [(i, i - 1) for i in range(1, xs)])]
    broadcast_in_dim x2 -> x0, other arithmetic: 2.14 us -> none  [along_x(): return (mine + from_next + from_last).astype(BF)[:, None, :]]
    pallas_call x1, Pallas kernels: 9.33 us -> 11.3 us  [program(): pl.pallas_call(functools.partial(score_kernel, zs=zs, scale=scale, tile=t...]
    ppermute x7, starting transfers between devices: 18 us -> 19.8 us  [reduce_by_shifts(): came.append(lax.ppermute(sent, 'z', [(i, (i + k) % zs) for i in range(zs)]))]
  transfers between devices with their start and end apart: 21 -> 19, of which waited for: 11 -> 8; matrix products, arithmetic and copies ran while one was open for 7% -> 5% of each run, Pallas kernels for 12% -> 15%
where the time goes in v4:
time: 168 us; the launch traced here: 167 us
  starting transfers between devices  63.3 us (38%)
  waiting for transfers between devices  62.8 us (37%)
  Pallas kernels  27.1 us (16%)
  other arithmetic  6.61 us (4%)
  local copies, waits for them, and re-layouts  6.11 us (4%)
    all_to_all x2, waiting for transfers between devices, along_z(): return lax.all_to_all(pair, 'z', split_axis=0, concat_axis=0, tiled=True)  28.4 us
    ppermute x7, starting transfers between devices, reduce_by_shifts(): came.append(lax.ppermute(sent, 'z', [(i, (i + k) % zs) for i in range(zs)]))  19.8 us
    all_to_all x1, starting transfers between devices, program(): lax.all_to_all(packed.reshape(peers, 2 * block_len, width // 2), ('x', 'z...  13.4 us
    all_to_all x1, waiting for transfers between devices, program(): lax.all_to_all(packed.reshape(peers, 2 * block_len, width // 2), ('x', 'z...  13.1 us
    all_to_all x2, starting transfers between devices, along_z(): return lax.all_to_all(pair, 'z', split_axis=0, concat_axis=0, tiled=True)  12 us
    pallas_call x1, Pallas kernels, program(): pl.pallas_call(functools.partial(score_kernel, zs=zs, scale=scale, tile=t...  11.3 us
    pallas_call x1, Pallas kernels, program(): pl.pallas_call(functools.partial(softmax_kernel, zs=zs, scale=scale, tile...  9.72 us
    all_to_all x1, waiting for transfers between devices, program(): lax.all_to_all(mixed, ('dp', 'head', 'x'), split_axis=0, concat_axis=0, t...  8.01 us
  transfers between devices with their start and end apart: 19, of which 8 were waited for; matrix products, arithmetic and copies ran while one was open for 5% of the time, Pallas kernels for 15%

profile of v4, /device:TPU:2, one launch (start us, length us, event | category | flops | bytes accessed | tf_op | source)
XLA Modules:
  0.0 166.9 jit_solution(8824986271548899681)
XLA Ops:
  0.6 1.7 first_payload.1
  2.3 7.5 %all-to-all-start = ((bf16[16,40,256]{2,1,0:T(8,128)(2,1)}), bf16[16,40,256]{2,1,0:T(8,128)(2,1)S(1)}, u32[]{:S(2)}, u32[]{:S(2)}) async-start(bf16[16,40,256]{2,1,0:T(8,128)(2,1)} %first_payload.1), calls=%async_computation | async-start | bytes 655360 | tf_op jit(solution)/shard_map/all_to_all | solution.py:431
  9.8 8.0 %all-to-all-done = bf16[16,40,256]{2,1,0:T(8,128)(2,1)S(1)} async-done(((bf16[16,40,256]{2,1,0:T(8,128)(2,1)}), bf16[16,40,256]{2,1,0:T(8,128)(2,1)S(1)}, u32[]{:S(2)}, u32[]{:S(2)}) %all-to-all-start) | async-done | bytes 327712 | tf_op jit(solution)/shard_map/all_to_all | solution.py:431
  18.1 0.8 pad_maximum_fusion
  19.0 8.5 %all-to-all-start.1 = ((bf16[8,2,136,128]{3,2,1,0:T(8,128)(2,1)}), bf16[8,2,136,128]{3,2,1,0:T(8,128)(2,1)S(1)}, u32[]{:S(2)}, u32[]{:S(2)}) async-start(bf16[8,2,136,128]{3,2,1,0:T(8,128)(2,1)} %pad_maximum_fusion), calls=%async_computation.1 | async-start | bytes 1114112 | tf_op jit(solution)/shard_map/all_to_all | solution.py:451
  27.7 0.9 pad_maximum_fusion.1
  28.5 16.0 %all-to-all-done.1.k_own = bf16[8,2,136,128]{3,2,1,0:T(8,128)(2,1)S(1)} async-done(((bf16[8,2,136,128]{3,2,1,0:T(8,128)(2,1)}), bf16[8,2,136,128]{3,2,1,0:T(8,128)(2,1)S(1)}, u32[]{:S(2)}, u32[]{:S(2)}) %all-to-all-start.1) | async-done | bytes 557088 | tf_op jit(solution)/shard_map/all_to_all | solution.py:451
  44.6 3.5 %all-to-all-start.2 = ((bf16[8,2,128,128]{3,2,1,0:T(8,128)(2,1)}), bf16[8,2,128,128]{3,2,1,0:T(8,128)(2,1)S(1)}, u32[]{:S(2)}, u32[]{:S(2)}) async-start(bf16[8,2,128,128]{3,2,1,0:T(8,128)(2,1)} %pad_maximum_fusion.1), calls=%async_computation.2 | async-start | bytes 1048576 | tf_op jit(solution)/shard_map/all_to_all | solution.py:451
  51.4 12.4 %all-to-all-done.2.v_own = bf16[8,2,128,128]{3,2,1,0:T(8,128)(2,1)S(1)} async-done(((bf16[8,2,128,128]{3,2,1,0:T(8,128)(2,1)}), bf16[8,2,128,128]{3,2,1,0:T(8,128)(2,1)S(1)}, u32[]{:S(2)}, u32[]{:S(2)}) %all-to-all-start.2) | async-done | bytes 524320 | tf_op jit(solution)/shard_map/all_to_all | solution.py:451
  63.8 0.8 copy-done.4
  64.6 9.7 %softmax_and_value_gradient.1 = (f32[17,128,128]{2,1,0:T(8,128)}, f32[17,128,128]{2,1,0:T(8,128)}, f32[17,256,1024]{2,1,0:T(8,128)}, s32[1]{0:T(128)}, f32[17,8,1024]{2,1,0:T(8,128)}) custom-call(s32[6]{0:T(128)} %stack.35.place_ref, bf16[128,1024]{1,0:T(8,128)(2,1)} %bitcast.82, bf16[128,1024]{1,0:T(8,128)(2,1)} %bitcast.84, s32[1,128]{1,0:T(1,128)} %bitcast.81, ...), custom_call_target="tpu_custom_call" | custom-call | flops 12000000000 | bytes 20000000 | tf_op jit(solution)/shard_map/softmax_and_value_gradient/pallas_call | solution.py:467
  75.0 0.8 copy-done.9
  75.8 11.3 %score_gradient.1 = (bf16[512,512]{1,0:T(8,128)(2,1)}, f32[17,128,128]{2,1,0:T(8,128)}, f32[17,128,128]{2,1,0:T(8,128)}) custom-call(s32[6]{0:T(128)} %stack.35.place_ref, s32[1]{0:T(128)} %get-tuple-element.11.info_ref, bf16[128,1024]{1,0:T(8,128)(2,1)} %bitcast.83, bf16[128,1024]{1,0:T(8,128)(2,1)} %bitcast.85, bf16[128,1024]{1,0:T(8,128)(2,1)} %bitcast.86, ...), custom_call_target="tpu_custom_call" | custom-call | flops 12000000000 | bytes 20000000 | tf_op jit(solution)/shard_map/score_gradient/pallas_call | solution.py:505
  87.3 13.4 %all-to-all-start.3 = ((bf16[64,8,512]{2,1,0:T(8,128)(2,1)}), bf16[64,8,512]{2,1,0:T(8,128)(2,1)S(1)}, u32[]{:S(2)}, u32[]{:S(2)}) async-start(bf16[64,8,512]{2,1,0:T(8,128)(2,1)} %bitcast.72), calls=%async_computation.3 | async-start | bytes 1048576 | tf_op jit(solution)/shard_map/all_to_all | solution.py:562
  100.6 1.0 copy-done.3
  101.6 2.6 %fusion = bf16[16,128,128]{2,1,0:T(8,128)(2,1)} fusion(f32[17,128,128]{2,1,0:T(8,128)} %copy-done.3, f32[17,128,128]{2,1,0:T(8,128)} %get-tuple-element.17), kind=kLoop, calls=%fused_computation.1 | loop fusion | flops 524288 | bytes 2621440 | tf_op jit(solution)/shard_map/convert_element_type | solution.py:378
  104.2 13.1 %all-to-all-done.3 = bf16[64,8,512]{2,1,0:T(8,128)(2,1)S(1)} async-done(((bf16[64,8,512]{2,1,0:T(8,128)(2,1)}), bf16[64,8,512]{2,1,0:T(8,128)(2,1)S(1)}, u32[]{:S(2)}, u32[]{:S(2)}) %all-to-all-start.3) | async-done | bytes 524320 | tf_op jit(solution)/shard_map/all_to_all | solution.py:562
  117.3 3.6 %all-to-all-start.4 = ((bf16[8,2,128,128]{3,2,1,0:T(8,128)(2,1)}), bf16[8,2,128,128]{3,2,1,0:T(8,128)(2,1)S(1)}, u32[]{:S(2)}, u32[]{:S(2)}) async-start(bf16[8,2,128,128]{3,2,1,0:T(8,128)(2,1)} %bitcast.29), calls=%async_computation.4 | async-start | bytes 1048576 | tf_op jit(solution)/shard_map/all_to_all | solution.py:379
  120.9 0.8 fusion.7
  121.6 3.2 %collective-permute-start.10 = (bf16[2,128,128]{2,1,0:T(8,128)(2,1)S(1)}, bf16[2,128,128]{2,1,0:T(8,128)(2,1)S(1)}, u32[]{:S(2)}, u32[]{:S(2)}) collective-permute-start(bf16[2,128,128]{2,1,0:T(8,128)(2,1)S(1)} %get-tuple-element.22), channel_id=1, source_target_pairs={{0,28},{4,0},{8,4},{12,8},{16,12},{20,16},{24,20},{28,24},{1,29},{... | collective-permute-start | bytes 196616 | tf_op jit(solution)/shard_map/ppermute | solution.py:393
  124.9 1.7 %collective-permute-start.5 = (bf16[2,128,128]{2,1,0:T(8,128)(2,1)}, bf16[2,128,128]{2,1,0:T(8,128)(2,1)S(1)}, u32[]{:S(2)}, u32[]{:S(2)}) collective-permute-start(bf16[2,128,128]{2,1,0:T(8,128)(2,1)} %get-tuple-element.27), channel_id=1, source_target_pairs={{0,8},{4,12},{8,16},{12,20},{16,24},{20,28},{24,0},{28,4},{1,9},{5... | collective-permute-start | bytes 196616 | tf_op jit(solution)/shard_map/ppermute | solution.py:393
  126.6 3.6 %collective-permute-start.6 = (bf16[2,128,128]{2,1,0:T(8,128)(2,1)}, bf16[2,128,128]{2,1,0:T(8,128)(2,1)S(1)}, u32[]{:S(2)}, u32[]{:S(2)}) collective-permute-start(bf16[2,128,128]{2,1,0:T(8,128)(2,1)} %get-tuple-element.26), channel_id=1, source_target_pairs={{0,12},{4,16},{8,20},{12,24},{16,28},{20,0},{24,4},{28,8},{1,13},{... | collective-permute-start | bytes 196616 | tf_op jit(solution)/shard_map/ppermute | solution.py:393
  130.2 1.5 collective-permute-start.7
  131.6 6.1 %collective-permute-done.10 = bf16[2,128,128]{2,1,0:T(8,128)(2,1)S(1)} collective-permute-done((bf16[2,128,128]{2,1,0:T(8,128)(2,1)S(1)}, bf16[2,128,128]{2,1,0:T(8,128)(2,1)S(1)}, u32[]{:S(2)}, u32[]{:S(2)}) %collective-permute-start.10) | collective-permute-done | bytes 65568 | tf_op jit(solution)/shard_map/ppermute | solution.py:393
  137.7 3.2 %collective-permute-start.8 = (bf16[2,128,128]{2,1,0:T(8,128)(2,1)S(1)}, bf16[2,128,128]{2,1,0:T(8,128)(2,1)S(1)}, u32[]{:S(2)}, u32[]{:S(2)}) collective-permute-start(bf16[2,128,128]{2,1,0:T(8,128)(2,1)S(1)} %get-tuple-element.24), channel_id=1, source_target_pairs={{0,20},{4,24},{8,28},{12,0},{16,4},{20,8},{24,12},{28,16},{1,21},{... | collective-permute-start | bytes 196616 | tf_op jit(solution)/shard_map/ppermute | solution.py:393
  140.9 6.6 %collective-permute-start.9 = (bf16[2,128,128]{2,1,0:T(8,128)(2,1)S(1)}, bf16[2,128,128]{2,1,0:T(8,128)(2,1)S(1)}, u32[]{:S(2)}, u32[]{:S(2)}) collective-permute-start(bf16[2,128,128]{2,1,0:T(8,128)(2,1)S(1)} %get-tuple-element.23), channel_id=1, source_target_pairs={{0,24},{4,28},{8,0},{12,4},{16,8},{20,12},{24,16},{28,20},{1,25},{... | collective-permute-start | bytes 196616 | tf_op jit(solution)/shard_map/ppermute | solution.py:393
  147.5 2.3 %placement_choice.1.pick_ref = bf16[2,128,512]{2,1,0:T(8,128)(2,1)} custom-call(s32[6]{0:T(128)} %stack.35.place_ref, bf16[8,2,136,128]{3,2,1,0:T(8,128)(2,1)} %copy-done, bf16[8,2,136,128]{3,2,1,0:T(8,128)(2,1)} %copy-done.4), custom_call_target="tpu_custom_call" | custom-call | flops 100000000 | bytes 1000000 | tf_op jit(solution)/shard_map/placement_choice/pallas_call | solution.py:554
  149.8 2.1 %query_gradient_placement.1 = bf16[128,1024]{1,0:T(8,128)(2,1)} custom-call(bf16[2,128,512]{2,1,0:T(8,128)(2,1)} %placement_choice.1.pick_ref, bf16[512,512]{1,0:T(8,128)(2,1)} %bitcast.66), custom_call_target="tpu_custom_call" | custom-call | tf_op jit(solution)/shard_map/query_gradient_placement/pallas_call | solution.py:569
  152.4 4.6 %collective-permute-start.12 = (f32[128,256]{1,0:T(8,128)S(1)}, f32[128,256]{1,0:T(8,128)S(1)}, u32[]{:S(2)}, u32[]{:S(2)}) collective-permute-start(f32[128,256]{1,0:T(8,128)S(1)} %pad_maximum_fusion.2), channel_id=1, source_target_pairs={{32,0},{64,32},{96,64},{33,1},{65,33},{97,65},{34,2},{66,34},{98,6... | collective-permute-start | bytes 393224 | tf_op jit(solution)/shard_map/ppermute | solution.py:370
  157.0 0.9 fusion.27
  157.9 1.3 collective-permute-start.13
  159.8 6.5 %collective-permute-done.13 = f32[128,256]{1,0:T(8,128)S(1)} collective-permute-done((f32[128,256]{1,0:T(8,128)S(1)}, f32[128,256]{1,0:T(8,128)S(1)}, u32[]{:S(2)}, u32[]{:S(2)}) %collective-permute-start.13) | collective-permute-done | bytes 131104 | tf_op jit(solution)/shard_map/ppermute | solution.py:371
  (73 shorter events, 6.1 us)
Async XLA Ops:
  2.3 15.5 %all-to-all-start = ((bf16[16,40,256]{2,1,0:T(8,128)(2,1)}), bf16[16,40,256]{2,1,0:T(8,128)(2,1)S(1)}, u32[]{:S(2)}, u32[]{:S(2)}) async-start(bf16[16,40,256]{2,1,0:T(8,128)(2,1)} %first_payload.1), calls=%async_computation | async-start | bytes 655360 | tf_op jit(solution)/shard_map/all_to_all | solution.py:431
  18.0 1.0 copy-start.6
  19.0 25.6 %all-to-all-start.1 = ((bf16[8,2,136,128]{3,2,1,0:T(8,128)(2,1)}), bf16[8,2,136,128]{3,2,1,0:T(8,128)(2,1)S(1)}, u32[]{:S(2)}, u32[]{:S(2)}) async-start(bf16[8,2,136,128]{3,2,1,0:T(8,128)(2,1)} %pad_maximum_fusion), calls=%async_computation.1 | async-start | bytes 1114112 | tf_op jit(solution)/shard_map/all_to_all | solution.py:451
  27.5 17.1 %copy-start.7 = (bf16[128,128]{1,0:T(8,128)(2,1)}, bf16[128,128]{1,0:T(8,128)(2,1)S(1)}, u32[]{:S(2)}) copy-start(bf16[128,128]{1,0:T(8,128)(2,1)S(1)} %slice.252.far_v_own) | copy-start | bytes 98308
  27.6 21.0 %copy-start.8 = (s32[32]{0:T(128)S(1)}, s32[32]{0:T(128)}, u32[]{:S(2)}) copy-start(s32[32]{0:T(128)} %param.13) | copy-start | bytes 388
  44.6 19.3 %copy-start = (bf16[8,2,136,128]{3,2,1,0:T(8,128)(2,1)}, bf16[8,2,136,128]{3,2,1,0:T(8,128)(2,1)S(1)}, u32[]{:S(2)}) copy-start(bf16[8,2,136,128]{3,2,1,0:T(8,128)(2,1)S(1)} %all-to-all-done.1.k_own) | copy-start | bytes 1671172
  44.6 19.2 %all-to-all-start.2 = ((bf16[8,2,128,128]{3,2,1,0:T(8,128)(2,1)}), bf16[8,2,128,128]{3,2,1,0:T(8,128)(2,1)S(1)}, u32[]{:S(2)}, u32[]{:S(2)}) async-start(bf16[8,2,128,128]{3,2,1,0:T(8,128)(2,1)} %pad_maximum_fusion.1), calls=%async_computation.2 | async-start | bytes 1048576 | tf_op jit(solution)/shard_map/all_to_all | solution.py:451
  48.1 15.7 %collective-permute-start = (bf16[8,2,136,128]{3,2,1,0:T(8,128)(2,1)S(1)}, bf16[8,2,136,128]{3,2,1,0:T(8,128)(2,1)S(1)}, u32[]{:S(2)}, u32[]{:S(2)}) collective-permute-start(bf16[8,2,136,128]{3,2,1,0:T(8,128)(2,1)S(1)} %all-to-all-done.1.k_own), channel_id=1, source_target_pairs={{0,2},{2,0},{1,3},{3,1},{4,6},{6,4},{5,7},{7,5},{8,10},{10,8},{9,1... | collective-permute-start | bytes 1671176 | tf_op jit(solution)/shard_map/ppermute | solution.py:312
  48.2 2.0 %collective-permute-start.1 = (bf16[136,256]{1,0:T(8,128)(2,1)S(1)}, bf16[136,256]{1,0:T(8,128)(2,1)S(1)}, u32[]{:S(2)}, u32[]{:S(2)}) collective-permute-start(bf16[136,256]{1,0:T(8,128)(2,1)S(1)} %pad_maximum_fusion.4), channel_id=1, source_target_pairs={{0,2},{2,0},{1,3},{3,1},{4,6},{6,4},{5,7},{7,5},{8,10},{10,8},{9,1... | collective-permute-start | bytes 208904 | tf_op jit(solution)/shard_map/ppermute | solution.py:312
  63.8 10.6 %copy-start.5 = (bf16[8,2,128,128]{3,2,1,0:T(8,128)(2,1)}, bf16[8,2,128,128]{3,2,1,0:T(8,128)(2,1)S(1)}, u32[]{:S(2)}) copy-start(bf16[8,2,128,128]{3,2,1,0:T(8,128)(2,1)S(1)} %all-to-all-done.2.v_own) | copy-start | bytes 1572868
  63.8 11.2 %collective-permute-start.2 = (bf16[8,2,128,128]{3,2,1,0:T(8,128)(2,1)S(1)}, bf16[8,2,128,128]{3,2,1,0:T(8,128)(2,1)S(1)}, u32[]{:S(2)}, u32[]{:S(2)}) collective-permute-start(bf16[8,2,128,128]{3,2,1,0:T(8,128)(2,1)S(1)} %all-to-all-done.2.v_own), channel_id=1, source_target_pairs={{0,2},{2,0},{1,3},{3,1},{4,6},{6,4},{5,7},{7,5},{8,10},{10,8},{9,1... | collective-permute-start | bytes 1572872 | tf_op jit(solution)/shard_map/ppermute | solution.py:312
  63.8 0.8 copy-start.4
  74.4 26.3 %collective-permute-start.11 = (f32[17,128,128]{2,1,0:T(8,128)}, f32[17,128,128]{2,1,0:T(8,128)S(1)}, u32[]{:S(2)}, u32[]{:S(2)}) collective-permute-start(f32[17,128,128]{2,1,0:T(8,128)} %get-tuple-element.18), channel_id=1, source_target_pairs={{0,2},{2,0},{1,3},{3,1},{4,6},{6,4},{5,7},{7,5},{8,10},{10,8},{9,1... | collective-permute-start | bytes 3342344 | tf_op jit(solution)/shard_map/ppermute | solution.py:312
  75.0 0.9 copy-start.9
  87.1 33.7 %collective-permute-start.3 = (f32[17,128,128]{2,1,0:T(8,128)}, f32[17,128,128]{2,1,0:T(8,128)S(1)}, u32[]{:S(2)}, u32[]{:S(2)}) collective-permute-start(f32[17,128,128]{2,1,0:T(8,128)} %get-tuple-element.16), channel_id=1, source_target_pairs={{0,2},{2,0},{1,3},{3,1},{4,6},{6,4},{5,7},{7,5},{8,10},{10,8},{9,1... | collective-permute-start | bytes 3342344 | tf_op jit(solution)/shard_map/ppermute | solution.py:312
  87.3 30.0 %all-to-all-start.3 = ((bf16[64,8,512]{2,1,0:T(8,128)(2,1)}), bf16[64,8,512]{2,1,0:T(8,128)(2,1)S(1)}, u32[]{:S(2)}, u32[]{:S(2)}) async-start(bf16[64,8,512]{2,1,0:T(8,128)(2,1)} %bitcast.72), calls=%async_computation.3 | async-start | bytes 1048576 | tf_op jit(solution)/shard_map/all_to_all | solution.py:562
  100.6 1.0 copy-start.3
  101.6 19.2 %copy-start.2 = (f32[17,128,128]{2,1,0:T(8,128)S(1)}, f32[17,128,128]{2,1,0:T(8,128)}, u32[]{:S(2)}) copy-start(f32[17,128,128]{2,1,0:T(8,128)} %get-tuple-element.15) | copy-start | bytes 3342340
  117.3 4.4 %copy-start.1 = (bf16[64,8,512]{2,1,0:T(8,128)(2,1)}, bf16[64,8,512]{2,1,0:T(8,128)(2,1)S(1)}, u32[]{:S(2)}) copy-start(bf16[64,8,512]{2,1,0:T(8,128)(2,1)S(1)} %all-to-all-done.3) | copy-start | bytes 1572868
  117.3 34.8 %all-to-all-start.4 = ((bf16[8,2,128,128]{3,2,1,0:T(8,128)(2,1)}), bf16[8,2,128,128]{3,2,1,0:T(8,128)(2,1)S(1)}, u32[]{:S(2)}, u32[]{:S(2)}) async-start(bf16[8,2,128,128]{3,2,1,0:T(8,128)(2,1)} %bitcast.29), calls=%async_computation.4 | async-start | bytes 1048576 | tf_op jit(solution)/shard_map/all_to_all | solution.py:379
  121.6 16.1 %collective-permute-start.10 = (bf16[2,128,128]{2,1,0:T(8,128)(2,1)S(1)}, bf16[2,128,128]{2,1,0:T(8,128)(2,1)S(1)}, u32[]{:S(2)}, u32[]{:S(2)}) collective-permute-start(bf16[2,128,128]{2,1,0:T(8,128)(2,1)S(1)} %get-tuple-element.22), channel_id=1, source_target_pairs={{0,28},{4,0},{8,4},{12,8},{16,12},{20,16},{24,20},{28,24},{1,29},{... | collective-permute-start | bytes 196616 | tf_op jit(solution)/shard_map/ppermute | solution.py:393
  124.9 16.1 %collective-permute-start.4 = (bf16[2,128,128]{2,1,0:T(8,128)(2,1)S(1)}, bf16[2,128,128]{2,1,0:T(8,128)(2,1)S(1)}, u32[]{:S(2)}, u32[]{:S(2)}) collective-permute-start(bf16[2,128,128]{2,1,0:T(8,128)(2,1)S(1)} %get-tuple-element.21), channel_id=1, source_target_pairs={{0,4},{4,8},{8,12},{12,16},{16,20},{20,24},{24,28},{28,0},{1,5},{5... | collective-permute-start | bytes 196616 | tf_op jit(solution)/shard_map/ppermute | solution.py:393
  124.9 27.1 %collective-permute-start.5 = (bf16[2,128,128]{2,1,0:T(8,128)(2,1)}, bf16[2,128,128]{2,1,0:T(8,128)(2,1)S(1)}, u32[]{:S(2)}, u32[]{:S(2)}) collective-permute-start(bf16[2,128,128]{2,1,0:T(8,128)(2,1)} %get-tuple-element.27), channel_id=1, source_target_pairs={{0,8},{4,12},{8,16},{12,20},{16,24},{20,28},{24,0},{28,4},{1,9},{5... | collective-permute-start | bytes 196616 | tf_op jit(solution)/shard_map/ppermute | solution.py:393
  126.6 25.4 %collective-permute-start.6 = (bf16[2,128,128]{2,1,0:T(8,128)(2,1)}, bf16[2,128,128]{2,1,0:T(8,128)(2,1)S(1)}, u32[]{:S(2)}, u32[]{:S(2)}) collective-permute-start(bf16[2,128,128]{2,1,0:T(8,128)(2,1)} %get-tuple-element.26), channel_id=1, source_target_pairs={{0,12},{4,16},{8,20},{12,24},{16,28},{20,0},{24,4},{28,8},{1,13},{... | collective-permute-start | bytes 196616 | tf_op jit(solution)/shard_map/ppermute | solution.py:393
  130.2 21.8 %collective-permute-start.7 = (bf16[2,128,128]{2,1,0:T(8,128)(2,1)S(1)}, bf16[2,128,128]{2,1,0:T(8,128)(2,1)S(1)}, u32[]{:S(2)}, u32[]{:S(2)}) collective-permute-start(bf16[2,128,128]{2,1,0:T(8,128)(2,1)S(1)} %get-tuple-element.25), channel_id=1, source_target_pairs={{0,16},{4,20},{8,24},{12,28},{16,0},{20,4},{24,8},{28,12},{1,17},{... | collective-permute-start | bytes 196616 | tf_op jit(solution)/shard_map/ppermute | solution.py:393
  137.7 14.3 %collective-permute-start.8 = (bf16[2,128,128]{2,1,0:T(8,128)(2,1)S(1)}, bf16[2,128,128]{2,1,0:T(8,128)(2,1)S(1)}, u32[]{:S(2)}, u32[]{:S(2)}) collective-permute-start(bf16[2,128,128]{2,1,0:T(8,128)(2,1)S(1)} %get-tuple-element.24), channel_id=1, source_target_pairs={{0,20},{4,24},{8,28},{12,0},{16,4},{20,8},{24,12},{28,16},{1,21},{... | collective-permute-start | bytes 196616 | tf_op jit(solution)/shard_map/ppermute | solution.py:393
  140.9 11.0 %collective-permute-start.9 = (bf16[2,128,128]{2,1,0:T(8,128)(2,1)S(1)}, bf16[2,128,128]{2,1,0:T(8,128)(2,1)S(1)}, u32[]{:S(2)}, u32[]{:S(2)}) collective-permute-start(bf16[2,128,128]{2,1,0:T(8,128)(2,1)S(1)} %get-tuple-element.23), channel_id=1, source_target_pairs={{0,24},{4,28},{8,0},{12,4},{16,8},{20,12},{24,16},{28,20},{1,25},{... | collective-permute-start | bytes 196616 | tf_op jit(solution)/shard_map/ppermute | solution.py:393
  152.4 7.4 %collective-permute-start.12 = (f32[128,256]{1,0:T(8,128)S(1)}, f32[128,256]{1,0:T(8,128)S(1)}, u32[]{:S(2)}, u32[]{:S(2)}) collective-permute-start(f32[128,256]{1,0:T(8,128)S(1)} %pad_maximum_fusion.2), channel_id=1, source_target_pairs={{32,0},{64,32},{96,64},{33,1},{65,33},{97,65},{34,2},{66,34},{98,6... | collective-permute-start | bytes 393224 | tf_op jit(solution)/shard_map/ppermute | solution.py:370
  157.9 8.4 %collective-permute-start.13 = (f32[128,256]{1,0:T(8,128)S(1)}, f32[128,256]{1,0:T(8,128)S(1)}, u32[]{:S(2)}, u32[]{:S(2)}) collective-permute-start(f32[128,256]{1,0:T(8,128)S(1)} %pad_maximum_fusion.3), channel_id=1, source_target_pairs={{64,0},{96,32},{65,1},{97,33},{66,2},{98,34},{67,3},{99,35},{68,4}... | collective-permute-start | bytes 393224 | tf_op jit(solution)/shard_map/ppermute | solution.py:371

commit v5 on v4

--- a/solution.py
+++ b/solution.py
@@ -31,14 +31,19 @@
         dst[n * rows : (n + 1) * rows, :] = src[:, n * hd : (n + 1) * hd]
 
 
-def fill_window(win, own, other, far_own, far_other, z, zs):
-    rows = win.shape[1] // 2
+def fill_window(win, own, other, far_own, far_other, z, zs, cols, rows):
+    hd = win.shape[1]
+
+    def at(j, half):
+        start = (j + 1) * 2 * rows + half * rows
+        return pl.ds(start if isinstance(start, int) else pl.multiple_of(start, rows), rows)
+
     for half, near, far in ((0, own, far_own), (1, other, far_other)):
-        cut = pl.ds(half * rows, rows)
         for zz in range(zs):
-            win[zs + zz, cut, :] = near[zz, 0, :rows, :]
-            win[jnp.where(zz > z, zz, 2 * zs + zz), cut, :] = near[zz, 1, :rows, :]
-        win[z, cut, :] = far
+            win[at(zs + zz, half), :] = near[zz, 0, :rows, :]
+            win[at(jnp.where(zz > z, zz, 2 * zs + zz), half), :] = near[zz, 1, :rows, :]
+        win[at(z, half), :] = far[:rows, cols]
+        win[at(z - 1, half), :] = jnp.zeros((rows, hd), BF)
 
 
 def out_index(j, z, zs):
@@ -51,6 +56,18 @@
     zz = lax.rem(lax.rem(j, zs) + zs - z, zs)
     middle = (j >= zs) & (j < 2 * zs)
     return jnp.where(middle, 2 * zz, jnp.where(j == z, 2 * zs, 2 * zz + 1))
+
+
+def store_pair(j, value, own, other, z, index):
+    rows = own.shape[1]
+
+    @pl.when(j >= z)
+    def _():
+        own[index(j)] = value[:rows]
+        other[index(j)] = value[rows : 2 * rows]
+
+    own[index(j + 1)] = value[2 * rows : 3 * rows]
+    other[index(j + 1)] = value[3 * rows :]
 
 
 def softmax_kernel(
@@ -91,12 +108,13 @@
 
     stack_heads(q_all, q_ref)
     stack_heads(do_all, do_ref)
-    fill_window(k_win, k_own, k_other, far_own[:rows, :], far_other[:rows, :], z, zs)
+    fill_window(k_win, k_own, k_other, far_own, far_other, z, zs, slice(0, hd), rows)
 
     near_ok = (x >= 1).astype(F32)
     far_ok = (x >= 2).astype(F32)
     counts = (
-        far_own[rows : rows + COUNTS, :].astype(F32) + far_other[rows : rows + COUNTS, :].astype(F32)
+        far_own[rows : rows + COUNTS, :hd].astype(F32)
+        + far_other[rows : rows + COUNTS, :hd].astype(F32)
     ) * far_ok
     for zz in range(zs):
         both = k_own[zz, 0, rows : rows + COUNTS, :].astype(F32) + k_other[
@@ -115,6 +133,9 @@
     lo = (jnp.min(first_row) - base) // (2 * rows)
     edge = jnp.minimum((jnp.max(first_row) - base) // (2 * rows) + 1, here)
     info_ref[0] = lo
+    pairs = (here - lo + 2) // 2
+    start = here + 1 - 2 * pairs
+    inner = jnp.minimum((edge - start + 1) // 2, pairs - 1)
     q_pos = base + (here * 2 + core) * rows + lax.broadcasted_iota(jnp.int32, (1, rows), 1)
     firsts = jnp.concatenate([first_row] * (tile // rows), axis=1)
     lasts = jnp.concatenate([q_pos] * (tile // rows), axis=1)
@@ -123,65 +144,67 @@
     state[0:1, :] = jnp.full((1, total), NEG_FILL, F32)
     state[1:2, :] = jnp.zeros((1, total), F32)
 
-    def visit(j, masked):
-        slot = j - lo
+    def pair_rows(i):
+        return pl.ds(pl.multiple_of((start + 2 * i + 1) * 2 * rows, 2 * rows), 4 * rows)
+
+    def visit(i, masked):
+        keys = k_win[pair_rows(i), :]
         for t in range(total // tile):
             cols = slice(t * tile, (t + 1) * tile)
             q_t = q_all[cols, :]
             peak = state[0:1, cols]
-            for half in range(2):
-                cut = slice(half * rows, (half + 1) * rows)
-                s = nt(k_win[j, cut, :], q_t) * unit
+            for c in range(4):
+                cut = slice(c * rows, (c + 1) * rows)
+                s = nt(keys[cut], q_t) * unit
                 if masked:
-                    key_pos = key_iota + (base + (j * 2 + (core if half == 0 else 1 - core)) * rows)
+                    chip = start + 2 * i + c // 2
+                    key_pos = key_iota + (base + (chip * 2 + (core if c % 2 == 0 else 1 - core)) * rows)
                     s = jnp.where((key_pos >= firsts) & (key_pos <= lasts), s, NEG_FILL)
                 peak = jnp.maximum(peak, jnp.max(s, axis=0, keepdims=True))
                 raw[cut, cols] = s
-            factors[slot, 0:1, cols] = peak
+            factors[i, 0:1, cols] = peak
         for t in range(total // tile):
             cols = slice(t * tile, (t + 1) * tile)
-            old, peak = state[0:1, cols], factors[slot, 0:1, cols]
+            old, peak = state[0:1, cols], factors[i, 0:1, cols]
             seen = state[1:2, cols] * jnp.exp2(old - peak)
-            for half in range(2):
-                cut = slice(half * rows, (half + 1) * rows)
+            for c in range(4):
+                cut = slice(c * rows, (c + 1) * rows)
                 p = jnp.exp2(raw[cut, cols] - peak)
-                p_all[slot, cut, cols] = p
+                p_all[i, cut, cols] = p
                 seen = seen + jnp.sum(p, axis=0, keepdims=True)
             state[0:1, cols] = peak
             state[1:2, cols] = seen
-        pltpu.make_async_copy(p_all.at[slot], p_out.at[slot], sems.at[slot]).start()
-
-    def plain(j, carry):
-        visit(j, False)
+        pltpu.make_async_copy(p_all.at[i], p_out.at[i], sems.at[i]).start()
+
+    def plain(i, carry):
+        visit(i, False)
         return carry
 
     def edges(i, carry):
-        visit(jnp.where(lo + i < edge, lo + i, here), True)
-        return carry
-
-    lax.fori_loop(0, edge - lo + 1, edges, 0)
-    lax.fori_loop(edge, here, plain, 0)
+        visit(jnp.where(i < inner, i, pairs - 1), True)
+        return carry
+
+    lax.fori_loop(0, inner + 1, edges, 0)
+    lax.fori_loop(inner, pairs - 1, plain, 0)
     state[1:2, :] = 1.0 / state[1:2, :]
 
-    def second(j, carry):
-        slot = j - lo
-        dv = jnp.zeros((2 * rows, hd), F32)
+    def second(i, carry):
+        dv = None
         for g in range(total // group):
             for t in range(g * group // tile, (g + 1) * group // tile):
                 cols = slice(t * tile, (t + 1) * tile)
-                factor = jnp.exp2(factors[slot, 0:1, cols] - state[0:1, cols]) * state[1:2, cols]
-                factors[slot, 0:1, cols] = factor
-                for half in range(2):
-                    cut = slice(half * rows, (half + 1) * rows)
-                    low[cut, cols] = (p_all[slot, cut, cols] * factor).astype(BF)
+                factor = jnp.exp2(factors[i, 0:1, cols] - state[0:1, cols]) * state[1:2, cols]
+                factors[i, 0:1, cols] = factor
+                for c in range(4):
+                    cut = slice(c * rows, (c + 1) * rows)
+                    low[cut, cols] = (p_all[i, cut, cols] * factor).astype(BF)
             span = slice(g * group, (g + 1) * group)
-            dv = dv + nn(low[:, span], do_all[span, :])
-        at = out_index(j, z, zs)
-        dv_own[at] = dv[:rows]
-        dv_other[at] = dv[rows:]
-        return carry
-
-    lax.fori_loop(lo, here + 1, second, 0)
+            more = nn(low[:, span], do_all[span, :])
+            dv = more if dv is None else dv + more
+        store_pair(start + 2 * i, dv, dv_own, dv_other, z, lambda j: out_index(j, z, zs))
+        return carry
+
+    lax.fori_loop(0, pairs, second, 0)
 
     def clear(j, carry):
         at = out_index(j, z, zs)
@@ -191,12 +214,11 @@
 
     lax.fori_loop(z, lo, clear, 0)
 
-    def finish(j, carry):
-        slot = j - lo
-        pltpu.make_async_copy(p_all.at[slot], p_out.at[slot], sems.at[slot]).wait()
-        return carry
-
-    lax.fori_loop(lo, here + 1, finish, 0)
+    def finish(i, carry):
+        pltpu.make_async_copy(p_all.at[i], p_out.at[i], sems.at[i]).wait()
+        return carry
+
+    lax.fori_loop(0, pairs, finish, 0)
 
 
 def score_kernel(
@@ -211,8 +233,6 @@
     far_other,
     v_own,
     v_other,
-    far_v_own,
-    far_v_other,
     factors,
     owner_ref,
     p_in,
@@ -245,15 +265,18 @@
     def copy_in(slot):
         return pltpu.make_async_copy(p_in.at[slot], p_all.at[slot], sems.at[slot])
 
-    def begin(j, carry):
-        copy_in(j - lo).start()
-        return carry
-
-    lax.fori_loop(lo, here + 1, begin, 0)
+    pairs = (here - lo + 2) // 2
+    start = here + 1 - 2 * pairs
+
+    def begin(i, carry):
+        copy_in(i).start()
+        return carry
+
+    lax.fori_loop(0, pairs, begin, 0)
     stack_heads(q_all, q_ref)
     stack_heads(do_all, do_ref)
-    fill_window(k_win, k_own, k_other, far_own[:rows, :], far_other[:rows, :], z, zs)
-    fill_window(v_win, v_own, v_other, far_v_own[...], far_v_other[...], z, zs)
+    fill_window(k_win, k_own, k_other, far_own, far_other, z, zs, slice(0, hd), rows)
+    fill_window(v_win, v_own, v_other, far_own, far_other, z, zs, slice(hd, 2 * hd), rows)
     for n in range(width // hd):
         cols = slice(n * hd, (n + 1) * hd)
         prod = do_ref[:, cols].astype(F32) * o_ref[:, cols].astype(F32)
@@ -268,35 +291,40 @@
 
     lax.fori_loop(z, lo, clear, 0)
 
-    def visit(j, carry):
-        slot = j - lo
-        copy_in(slot).wait()
-        keys_t = k_win[j].T
-        dk = jnp.zeros((2 * rows, hd), F32)
+    def visit(i, carry):
+        copy_in(i).wait()
+        window = pl.ds(pl.multiple_of((start + 2 * i + 1) * 2 * rows, 2 * rows), 4 * rows)
+        keys_t = k_win[window, :].T
+        values = v_win[window, :]
+        dk = None
         for g in range(total // group):
             for t in range(g * group // tile, (g + 1) * group // tile):
                 cols = slice(t * tile, (t + 1) * tile)
                 do_t = do_all[cols, :]
-                for half in range(2):
-                    cut = slice(half * rows, (half + 1) * rows)
-                    dprob = nt(v_win[j, cut, :], do_t)
-                    probs = p_all[slot, cut, cols] * factors[slot, 0:1, cols]
+                for c in range(4):
+                    cut = slice(c * rows, (c + 1) * rows)
+                    dprob = nt(values[cut], do_t)
+                    probs = p_all[i, cut, cols] * factors[i, 0:1, cols]
                     low[cut, cols] = (probs * (dprob - delta[0:1, cols]) * scale).astype(BF)
             span = slice(g * group, (g + 1) * group)
-            dk = dk + nn(low[:, span], q_all[span, :])
+            more = nn(low[:, span], q_all[span, :])
+            dk = more if dk is None else dk + more
             dq_sum[:, span] += nn(keys_t, low[:, span])
-        at = relative_index(j, z, zs)
-        dk_own[at] = dk[:rows]
-        dk_other[at] = dk[rows:]
-        return carry
-
-    lax.fori_loop(lo, here + 1, visit, 0)
+        store_pair(start + 2 * i, dk, dk_own, dk_other, z, lambda j: relative_index(j, z, zs))
+        return carry
+
+    lax.fori_loop(0, pairs, visit, 0)
     half_width = width // 2
     half_heads = half_width // hd
     spots = packed_ref.shape[0]
     row = lax.broadcasted_iota(jnp.int32, (spots, rows), 0)
     token = lax.broadcasted_iota(jnp.int32, (spots, rows), 1)
-    goes = (row // (2 * block) == owner_ref[...]) & (row % block == token % block)
+    slots = owner_ref.shape[1]
+    spread = lax.broadcasted_iota(jnp.int32, (slots, rows), 1) // block
+    spread = spread == lax.broadcasted_iota(jnp.int32, (slots, rows), 0)
+    owners = jnp.broadcast_to(owner_ref[...].astype(F32).astype(BF), (8, slots))
+    owners = nn(owners, spread.astype(F32).astype(BF))[0:1]
+    goes = ((row // (2 * block)).astype(F32) == owners) & (row % block == token % block)
     packed = jnp.zeros((spots, half_width), F32)
     for h in range(2):
         here_half = goes & (row // block % 2 == h)
@@ -398,7 +426,7 @@
         near = near + got[0].astype(F32)
         mine = mine + jnp.where(z < k, got[1].astype(F32), 0.0)
         far = far + jnp.where(z < k, 0.0, got[1].astype(F32))
-    return mine, near, far
+    return mine, near, far, came[zs // 2]
 
 
 def program(queries, keys, values, outputs, grad_out, doc_ids, owner):
@@ -407,7 +435,7 @@
     rows, _, width = queries.shape
     total = rows * (width // hd)
     tile = min(256, total)
-    group = min(512, total)
+    group = min(1024, total)
     xs, zs = lax.axis_size("x"), lax.axis_size("z")
     x, z, core = lax.axis_index("x"), lax.axis_index("z"), lax.axis_index("core")
     peers = xs * zs * 2
@@ -415,6 +443,7 @@
     block_len = rows // per_device
     part = keys.shape[0]
     chips = 2 * zs + 1
+    steps = zs + 1
 
     extra = COUNTS + xs
     vmem = pl.BlockSpec(memory_space=pltpu.VMEM)
@@ -464,6 +493,7 @@
     o = outputs.reshape(rows, width)
     grad_shape = jax.ShapeDtypeStruct((chips, rows, hd), F32)
     params = pltpu.CompilerParams(vmem_limit_bytes=VMEM_BYTES)
+    small = pltpu.CompilerParams(vmem_limit_bytes=8 * 1024 * 1024)
     dv_own, dv_other, probs, info, factors = pl.pallas_call(
         functools.partial(softmax_kernel, zs=zs, scale=scale, tile=tile, group=group),
         in_specs=[smem] + [vmem] * 7,
@@ -471,19 +501,19 @@
         out_shape=[
             grad_shape,
             grad_shape,
-            jax.ShapeDtypeStruct((chips, 2 * rows, total), F32),
+            jax.ShapeDtypeStruct((steps, 4 * rows, total), F32),
             jax.ShapeDtypeStruct((1,), jnp.int32),
-            jax.ShapeDtypeStruct((chips, 8, total), F32),
+            jax.ShapeDtypeStruct((steps, 8, total), F32),
         ],
         scratch_shapes=[
             pltpu.VMEM((total, hd), BF),
             pltpu.VMEM((total, hd), BF),
-            pltpu.VMEM((3 * zs, 2 * rows, hd), BF),
-            pltpu.VMEM((chips, 2 * rows, total), F32),
-            pltpu.VMEM((2 * rows, total), F32),
-            pltpu.VMEM((2 * rows, total), BF),
+            pltpu.VMEM(((3 * zs + 1) * 2 * rows, hd), BF),
+            pltpu.VMEM((steps, 4 * rows, total), F32),
+            pltpu.VMEM((4 * rows, total), F32),
+            pltpu.VMEM((4 * rows, total), BF),
             pltpu.VMEM((8, total), F32),
-            pltpu.SemaphoreType.DMA((chips,)),
+            pltpu.SemaphoreType.DMA((steps,)),
         ],
         compiler_params=params,
         cost_estimate=pl.CostEstimate(
@@ -497,8 +527,8 @@
         doc_ids.reshape(1, rows),
         k_own,
         k_other,
-        far[:, :hd],
-        far_other[:, :hd],
+        far,
+        far_other,
     )
     v_other = swap(v_own)
     parts_v = reduce_at_once(dv_own, dv_other, zs, z)
@@ -506,7 +536,7 @@
         functools.partial(
             score_kernel, zs=zs, scale=scale, tile=tile, group=group, block=block_len
         ),
-        in_specs=[smem, smem] + [vmem] * 13 + [anywhere],
+        in_specs=[smem, smem] + [vmem] * 11 + [anywhere],
         out_specs=[vmem] * 3,
         out_shape=[
             jax.ShapeDtypeStruct((peers * 2 * block_len, width // 2), BF),
@@ -516,13 +546,13 @@
         scratch_shapes=[
             pltpu.VMEM((total, hd), BF),
             pltpu.VMEM((total, hd), BF),
-            pltpu.VMEM((3 * zs, 2 * rows, hd), BF),
-            pltpu.VMEM((3 * zs, 2 * rows, hd), BF),
-            pltpu.VMEM((chips, 2 * rows, total), F32),
-            pltpu.VMEM((2 * rows, total), BF),
+            pltpu.VMEM(((3 * zs + 1) * 2 * rows, hd), BF),
+            pltpu.VMEM(((3 * zs + 1) * 2 * rows, hd), BF),
+            pltpu.VMEM((steps, 4 * rows, total), F32),
+            pltpu.VMEM((4 * rows, total), BF),
             pltpu.VMEM((8, total), F32),
             pltpu.VMEM((hd, total), F32),
-            pltpu.SemaphoreType.DMA((chips,)),
+            pltpu.SemaphoreType.DMA((steps,)),
         ],
         compiler_params=params,
         cost_estimate=pl.CostEstimate(
@@ -537,17 +567,15 @@
         o,
         k_own,
         k_other,
-        far[:, :hd],
-        far_other[:, :hd],
+        far,
+        far_other,
         v_own,
         v_other,
-        far[:rows, hd:],
-        far_other[:rows, hd:],
         factors,
-        jnp.repeat(owner, block_len)[None],
+        owner[None],
         probs,
     )
-    parts_k = reduce_by_shifts(dk_own, dk_other, zs, z)
+    *parts_k, halfway = reduce_by_shifts(dk_own, dk_other, zs, z)
     grads = along_x([jnp.concatenate(pair, axis=1) for pair in zip(parts_k, parts_v)], xs)
     grad_k, grad_v = grads[:, None, :hd], grads[:, None, hd:]
 
@@ -557,8 +585,9 @@
         out_specs=vmem,
         out_shape=jax.ShapeDtypeStruct((2, rows, peers * 2 * block_len), BF),
         cost_estimate=pl.CostEstimate(flops=100_000_000, bytes_accessed=1_000_000, transcendentals=0),
+        compiler_params=small,
         name="placement_choice",
-    )(place, k_own, k_other)
+    )(lax.optimization_barrier((place, halfway))[0], k_own, k_other)
     arrived = lax.all_to_all(
         packed.reshape(peers, 2 * block_len, width // 2),
         ("x", "z", "core"),
@@ -571,7 +600,7 @@
         in_specs=[vmem, vmem],
         out_specs=vmem,
         out_shape=jax.ShapeDtypeStruct((rows, width), BF),
-        compiler_params=params,
+        compiler_params=small,
         name="query_gradient_placement",
     )(pick, arrived.reshape(packed.shape))
     return (placed.reshape(rows, 1, width), grad_k, grad_v)

time: 168 us -> 163 us (0.970)
  waiting for transfers between devices: 62.8 us -> 70.4 us
  starting transfers between devices: 63.3 us -> 55.7 us
  Pallas kernels: 27.1 us -> 22.1 us
  local copies, waits for them, and re-layouts: 6.11 us -> 3.24 us
  other arithmetic: 6.61 us -> 9.43 us
    ppermute x7, starting transfers between devices: 19.8 us -> 15.2 us  [reduce_by_shifts(): came.append(lax.ppermute(sent, 'z', [(i, (i + k) % zs) for i in range(zs)]))]
    ppermute x7, waiting for transfers between devices: 6.09 us -> 10.2 us  [reduce_by_shifts(): came.append(lax.ppermute(sent, 'z', [(i, (i + k) % zs) for i in range(zs)]))]
    all_to_all x1, waiting for transfers between devices: 13.1 us -> 15.5 us  [program(): lax.all_to_all(packed.reshape(peers, 2 * block_len, width // 2), ('x', 'z...]
    all_to_all x2, waiting for transfers between devices: 28.4 us -> 30.4 us  [along_z(): return lax.all_to_all(pair, 'z', split_axis=0, concat_axis=0, tiled=True)]
  transfers between devices with their start and end apart: 19 -> 19, of which waited for: 8 -> 8; matrix products, arithmetic and copies ran while one was open for 5% -> 5% of each run, Pallas kernels for 15% -> 13%
where the time goes in v5:
time: 163 us; the launch traced here: 162 us
  waiting for transfers between devices  70.4 us (43%)
  starting transfers between devices  55.7 us (34%)
  Pallas kernels  22.1 us (14%)
  other arithmetic  9.43 us (6%)
  local copies, waits for them, and re-layouts  3.24 us (2%)
    all_to_all x2, waiting for transfers between devices, along_z(): return lax.all_to_all(pair, 'z', split_axis=0, concat_axis=0, tiled=True)  30.4 us
    all_to_all x1, waiting for transfers between devices, program(): lax.all_to_all(packed.reshape(peers, 2 * block_len, width // 2), ('x', 'z...  15.5 us
    ppermute x7, starting transfers between devices, reduce_by_shifts(): came.append(lax.ppermute(sent, 'z', [(i, (i + k) % zs) for i in range(zs)]))  15.2 us
    all_to_all x2, starting transfers between devices, along_z(): return lax.all_to_all(pair, 'z', split_axis=0, concat_axis=0, tiled=True)  12 us
    all_to_all x1, starting transfers between devices, program(): lax.all_to_all(packed.reshape(peers, 2 * block_len, width // 2), ('x', 'z...  11.8 us
    ppermute x7, waiting for transfers between devices, reduce_by_shifts(): came.append(lax.ppermute(sent, 'z', [(i, (i + k) % zs) for i in range(zs)]))  10.2 us
    pallas_call x1, Pallas kernels, program(): pl.pallas_call(functools.partial(score_kernel, zs=zs, scale=scale, tile=t...  10 us
    pallas_call x1, Pallas kernels, program(): pl.pallas_call(functools.partial(softmax_kernel, zs=zs, scale=scale, tile...  8.49 us
  transfers between devices with their start and end apart: 19, of which 8 were waited for; matrix products, arithmetic and copies ran while one was open for 5% of the time, Pallas kernels for 13%

profile of v5, /device:TPU:2, one launch (start us, length us, event | category | flops | bytes accessed | tf_op | source)
XLA Modules:
  0.0 161.9 jit_solution(3598300280940524857)
XLA Ops:
  0.6 1.7 %first_payload.1 = bf16[16,40,256]{2,1,0:T(8,128)(2,1)} custom-call(bf16[32,4,128]{2,1,0:T(4,128)(2,1)} %keys_ref.1, bf16[32,4,128]{2,1,0:T(4,128)(2,1)} %values_ref.1, s32[1,128]{1,0:T(1,128)} %bitcast.79, s32[1,32]{1,0:T(1,128)} %bitcast.81), custom_call_target="tpu_custom_call" | custom-call | tf_op jit(solution)/shard_map/first_payload/pallas_call | solution.py:452
  2.3 7.5 %all-to-all-start = ((bf16[16,40,256]{2,1,0:T(8,128)(2,1)}), bf16[16,40,256]{2,1,0:T(8,128)(2,1)S(1)}, u32[]{:S(2)}, u32[]{:S(2)}) async-start(bf16[16,40,256]{2,1,0:T(8,128)(2,1)} %first_payload.1), calls=%async_computation | async-start | bytes 655360 | tf_op jit(solution)/shard_map/all_to_all | solution.py:460
  9.8 8.0 %all-to-all-done = bf16[16,40,256]{2,1,0:T(8,128)(2,1)S(1)} async-done(((bf16[16,40,256]{2,1,0:T(8,128)(2,1)}), bf16[16,40,256]{2,1,0:T(8,128)(2,1)S(1)}, u32[]{:S(2)}, u32[]{:S(2)}) %all-to-all-start) | async-done | bytes 327712 | tf_op jit(solution)/shard_map/all_to_all | solution.py:460
  18.1 0.9 pad_maximum_fusion
  19.0 8.5 %all-to-all-start.1 = ((bf16[8,2,136,128]{3,2,1,0:T(8,128)(2,1)}), bf16[8,2,136,128]{3,2,1,0:T(8,128)(2,1)S(1)}, u32[]{:S(2)}, u32[]{:S(2)}) async-start(bf16[8,2,136,128]{3,2,1,0:T(8,128)(2,1)} %pad_maximum_fusion), calls=%async_computation.1 | async-start | bytes 1114112 | tf_op jit(solution)/shard_map/all_to_all | solution.py:480
  28.5 16.1 %all-to-all-done.1.k_own = bf16[8,2,136,128]{3,2,1,0:T(8,128)(2,1)S(1)} async-done(((bf16[8,2,136,128]{3,2,1,0:T(8,128)(2,1)}), bf16[8,2,136,128]{3,2,1,0:T(8,128)(2,1)S(1)}, u32[]{:S(2)}, u32[]{:S(2)}) %all-to-all-start.1) | async-done | bytes 557088 | tf_op jit(solution)/shard_map/all_to_all | solution.py:480
  44.6 3.5 %all-to-all-start.2 = ((bf16[8,2,128,128]{3,2,1,0:T(8,128)(2,1)}), bf16[8,2,128,128]{3,2,1,0:T(8,128)(2,1)S(1)}, u32[]{:S(2)}, u32[]{:S(2)}) async-start(bf16[8,2,128,128]{3,2,1,0:T(8,128)(2,1)} %pad_maximum_fusion.1), calls=%async_computation.2 | async-start | bytes 1048576 | tf_op jit(solution)/shard_map/all_to_all | solution.py:480
  49.4 14.4 %all-to-all-done.2.v_own = bf16[8,2,128,128]{3,2,1,0:T(8,128)(2,1)S(1)} async-done(((bf16[8,2,128,128]{3,2,1,0:T(8,128)(2,1)}), bf16[8,2,128,128]{3,2,1,0:T(8,128)(2,1)S(1)}, u32[]{:S(2)}, u32[]{:S(2)}) %all-to-all-start.2) | async-done | bytes 524320 | tf_op jit(solution)/shard_map/all_to_all | solution.py:480
  64.7 8.5 %softmax_and_value_gradient.1 = (f32[17,128,128]{2,1,0:T(8,128)}, f32[17,128,128]{2,1,0:T(8,128)}, f32[9,512,1024]{2,1,0:T(8,128)}, s32[1]{0:T(128)}, f32[9,8,1024]{2,1,0:T(8,128)}) custom-call(s32[6]{0:T(128)} %stack.35.place_ref, bf16[128,1024]{1,0:T(8,128)(2,1)} %bitcast.83, bf16[128,1024]{1,0:T(8,128)(2,1)} %bitcast.85, s32[1,128]{1,0:T(1,128)} %bitcast.80, ...), custom_call_target="tpu_custom_call" | custom-call | flops 12000000000 | bytes 20000000 | tf_op jit(solution)/shard_map/softmax_and_value_gradient/pallas_call | solution.py:497
  74.6 10.0 %score_gradient.1 = (bf16[512,512]{1,0:T(8,128)(2,1)}, f32[17,128,128]{2,1,0:T(8,128)}, f32[17,128,128]{2,1,0:T(8,128)}) custom-call(s32[6]{0:T(128)} %stack.35.place_ref, s32[1]{0:T(128)} %get-tuple-element.12.info_ref, bf16[128,1024]{1,0:T(8,128)(2,1)} %bitcast.84, bf16[128,1024]{1,0:T(8,128)(2,1)} %bitcast.86, bf16[128,1024]{1,0:T(8,128)(2,1)} %bitcast.87, ...), custom_call_target="tpu_custom_call" | custom-call | flops 12000000000 | bytes 20000000 | tf_op jit(solution)/shard_map/score_gradient/pallas_call | solution.py:535
  84.8 11.8 %all-to-all-start.3 = ((bf16[64,8,512]{2,1,0:T(8,128)(2,1)}), bf16[64,8,512]{2,1,0:T(8,128)(2,1)S(1)}, u32[]{:S(2)}, u32[]{:S(2)}) async-start(bf16[64,8,512]{2,1,0:T(8,128)(2,1)} %bitcast.72), calls=%async_computation.3 | async-start | bytes 1048576 | tf_op jit(solution)/shard_map/all_to_all | solution.py:591
  96.6 1.1 fusion
  97.8 15.5 %all-to-all-done.3 = bf16[64,8,512]{2,1,0:T(8,128)(2,1)S(1)} async-done(((bf16[64,8,512]{2,1,0:T(8,128)(2,1)}), bf16[64,8,512]{2,1,0:T(8,128)(2,1)S(1)}, u32[]{:S(2)}, u32[]{:S(2)}) %all-to-all-start.3) | async-done | bytes 524320 | tf_op jit(solution)/shard_map/all_to_all | solution.py:591
  113.3 3.6 %all-to-all-start.4 = ((bf16[8,2,128,128]{3,2,1,0:T(8,128)(2,1)}), bf16[8,2,128,128]{3,2,1,0:T(8,128)(2,1)S(1)}, u32[]{:S(2)}, u32[]{:S(2)}) async-start(bf16[8,2,128,128]{3,2,1,0:T(8,128)(2,1)} %bitcast.29), calls=%async_computation.4 | async-start | bytes 1048576 | tf_op jit(solution)/shard_map/all_to_all | solution.py:407
  116.9 2.4 %fusion.6 = (bf16[2,128,128]{2,1,0:T(8,128)(2,1)}, bf16[2,128,128]{2,1,0:T(8,128)(2,1)S(1)}, bf16[2,128,128]{2,1,0:T(8,128)(2,1)}, bf16[2,128,128]{2,1,0:T(8,128...) fusion(f32[17,128,128]{2,1,0:T(8,128)} %collective-permute-done.3, ...), kind=kLoop, calls=%fused_computation.21 | loop fusion | flops 458752 | bytes 2293760 | tf_op jit(solution)/shard_map/convert_element_type | solution.py:420
  119.3 3.2 %collective-permute-start.10 = (bf16[2,128,128]{2,1,0:T(8,128)(2,1)S(1)}, bf16[2,128,128]{2,1,0:T(8,128)(2,1)S(1)}, u32[]{:S(2)}, u32[]{:S(2)}) collective-permute-start(bf16[2,128,128]{2,1,0:T(8,128)(2,1)S(1)} %get-tuple-element.24), channel_id=1, source_target_pairs={{0,28},{4,0},{8,4},{12,8},{16,12},{20,16},{24,20},{28,24},{1,29},{... | collective-permute-start | bytes 196616 | tf_op jit(solution)/shard_map/ppermute | solution.py:421
  122.5 3.3 %collective-permute-start.4 = (bf16[2,128,128]{2,1,0:T(8,128)(2,1)S(1)}, bf16[2,128,128]{2,1,0:T(8,128)(2,1)S(1)}, u32[]{:S(2)}, u32[]{:S(2)}) collective-permute-start(bf16[2,128,128]{2,1,0:T(8,128)(2,1)S(1)} %get-tuple-element.29), channel_id=1, source_target_pairs={{0,20},{4,24},{8,28},{12,0},{16,4},{20,8},{24,12},{28,16},{1,21},{... | collective-permute-start | bytes 196616 | tf_op jit(solution)/shard_map/ppermute | solution.py:421
  126.9 2.4 %collective-permute-start.7 = (bf16[2,128,128]{2,1,0:T(8,128)(2,1)}, bf16[2,128,128]{2,1,0:T(8,128)(2,1)}, u32[]{:S(2)}, u32[]{:S(2)}) collective-permute-start(bf16[2,128,128]{2,1,0:T(8,128)(2,1)} %get-tuple-element.27), channel_id=1, source_target_pairs={{0,12},{4,16},{8,20},{12,24},{16,28},{20,0},{24,4},{28,8},{1,13},{... | collective-permute-start | bytes 196616 | tf_op jit(solution)/shard_map/ppermute | solution.py:421
  129.2 6.0 %collective-permute-done.10 = bf16[2,128,128]{2,1,0:T(8,128)(2,1)S(1)} collective-permute-done((bf16[2,128,128]{2,1,0:T(8,128)(2,1)S(1)}, bf16[2,128,128]{2,1,0:T(8,128)(2,1)S(1)}, u32[]{:S(2)}, u32[]{:S(2)}) %collective-permute-start.10) | collective-permute-done | bytes 65568 | tf_op jit(solution)/shard_map/ppermute | solution.py:421
  135.2 3.0 %collective-permute-start.8 = (bf16[2,128,128]{2,1,0:T(8,128)(2,1)}, bf16[2,128,128]{2,1,0:T(8,128)(2,1)}, u32[]{:S(2)}, u32[]{:S(2)}) collective-permute-start(bf16[2,128,128]{2,1,0:T(8,128)(2,1)} %get-tuple-element.26), channel_id=1, source_target_pairs={{0,16},{4,20},{8,24},{12,28},{16,0},{20,4},{24,8},{28,12},{1,17},{... | collective-permute-start | bytes 196616 | tf_op jit(solution)/shard_map/ppermute | solution.py:421
  138.3 2.2 %collective-permute-start.9 = (bf16[2,128,128]{2,1,0:T(8,128)(2,1)}, bf16[2,128,128]{2,1,0:T(8,128)(2,1)}, u32[]{:S(2)}, u32[]{:S(2)}) collective-permute-start(bf16[2,128,128]{2,1,0:T(8,128)(2,1)} %get-tuple-element.25), channel_id=1, source_target_pairs={{0,24},{4,28},{8,0},{12,4},{16,8},{20,12},{24,16},{28,20},{1,25},{... | collective-permute-start | bytes 196616 | tf_op jit(solution)/shard_map/ppermute | solution.py:421
  140.5 0.9 placement_choice.1.pick_ref
  141.4 1.0 query_gradient_placement.1
  142.4 4.2 %collective-permute-done.8 = bf16[2,128,128]{2,1,0:T(8,128)(2,1)} collective-permute-done((bf16[2,128,128]{2,1,0:T(8,128)(2,1)}, bf16[2,128,128]{2,1,0:T(8,128)(2,1)}, u32[]{:S(2)}, u32[]{:S(2)}) %collective-permute-start.8) | collective-permute-done | bytes 65568 | tf_op jit(solution)/shard_map/ppermute | solution.py:421
  146.6 0.9 fusion.35
  147.6 1.0 fusion.26
  148.8 3.0 %collective-permute-start.12 = (f32[128,256]{1,0:T(8,128)S(1)}, f32[128,256]{1,0:T(8,128)S(1)}, u32[]{:S(2)}, u32[]{:S(2)}) collective-permute-start(f32[128,256]{1,0:T(8,128)S(1)} %pad_maximum_fusion.2), channel_id=1, source_target_pairs={{32,0},{64,32},{96,64},{33,1},{65,33},{97,65},{34,2},{66,34},{98,6... | collective-permute-start | bytes 393224 | tf_op jit(solution)/shard_map/ppermute | solution.py:398
  151.8 0.9 fusion.27
  152.7 1.3 collective-permute-start.13
  154.0 1.0 fusion.18
  155.0 1.2 collective-permute-done.12
  156.2 5.0 %collective-permute-done.13 = f32[128,256]{1,0:T(8,128)S(1)} collective-permute-done((f32[128,256]{1,0:T(8,128)S(1)}, f32[128,256]{1,0:T(8,128)S(1)}, u32[]{:S(2)}, u32[]{:S(2)}) %collective-permute-start.13) | collective-permute-done | bytes 131104 | tf_op jit(solution)/shard_map/ppermute | solution.py:399
  (71 shorter events, 7.1 us)
Async XLA Ops:
  2.3 15.5 %all-to-all-start = ((bf16[16,40,256]{2,1,0:T(8,128)(2,1)}), bf16[16,40,256]{2,1,0:T(8,128)(2,1)S(1)}, u32[]{:S(2)}, u32[]{:S(2)}) async-start(bf16[16,40,256]{2,1,0:T(8,128)(2,1)} %first_payload.1), calls=%async_computation | async-start | bytes 655360 | tf_op jit(solution)/shard_map/all_to_all | solution.py:460
  19.0 25.6 %all-to-all-start.1 = ((bf16[8,2,136,128]{3,2,1,0:T(8,128)(2,1)}), bf16[8,2,136,128]{3,2,1,0:T(8,128)(2,1)S(1)}, u32[]{:S(2)}, u32[]{:S(2)}) async-start(bf16[8,2,136,128]{3,2,1,0:T(8,128)(2,1)} %pad_maximum_fusion), calls=%async_computation.1 | async-start | bytes 1114112 | tf_op jit(solution)/shard_map/all_to_all | solution.py:480
  44.6 19.3 %copy-start = (bf16[8,2,136,128]{3,2,1,0:T(8,128)(2,1)}, bf16[8,2,136,128]{3,2,1,0:T(8,128)(2,1)S(1)}, u32[]{:S(2)}) copy-start(bf16[8,2,136,128]{3,2,1,0:T(8,128)(2,1)S(1)} %all-to-all-done.1.k_own) | copy-start | bytes 1671172
  44.6 19.2 %all-to-all-start.2 = ((bf16[8,2,128,128]{3,2,1,0:T(8,128)(2,1)}), bf16[8,2,128,128]{3,2,1,0:T(8,128)(2,1)S(1)}, u32[]{:S(2)}, u32[]{:S(2)}) async-start(bf16[8,2,128,128]{3,2,1,0:T(8,128)(2,1)} %pad_maximum_fusion.1), calls=%async_computation.2 | async-start | bytes 1048576 | tf_op jit(solution)/shard_map/all_to_all | solution.py:480
  48.1 15.8 %collective-permute-start = (bf16[8,2,136,128]{3,2,1,0:T(8,128)(2,1)S(1)}, bf16[8,2,136,128]{3,2,1,0:T(8,128)(2,1)S(1)}, u32[]{:S(2)}, u32[]{:S(2)}) collective-permute-start(bf16[8,2,136,128]{3,2,1,0:T(8,128)(2,1)S(1)} %all-to-all-done.1.k_own), channel_id=1, source_target_pairs={{0,2},{2,0},{1,3},{3,1},{4,6},{6,4},{5,7},{7,5},{8,10},{10,8},{9,1... | collective-permute-start | bytes 1671176 | tf_op jit(solution)/shard_map/ppermute | solution.py:340
  48.2 15.7 %copy-start.8 = (bf16[136,256]{1,0:T(8,128)(2,1)}, bf16[136,256]{1,0:T(8,128)(2,1)S(1)}, u32[]{:S(2)}) copy-start(bf16[136,256]{1,0:T(8,128)(2,1)S(1)} %pad_maximum_fusion.4.far_own) | copy-start | bytes 208900
  48.2 15.6 %collective-permute-start.1 = (bf16[136,256]{1,0:T(8,128)(2,1)S(1)}, bf16[136,256]{1,0:T(8,128)(2,1)S(1)}, u32[]{:S(2)}, u32[]{:S(2)}) collective-permute-start(bf16[136,256]{1,0:T(8,128)(2,1)S(1)} %pad_maximum_fusion.4.far_own), channel_id=1, source_target_pairs={{0,2},{2,0},{1,3},{3,1},{4,6},{6,4},{5,7},{7,5},{8,10},{10,8},{9,1... | collective-permute-start | bytes 208904 | tf_op jit(solution)/shard_map/ppermute | solution.py:340
  63.8 9.4 %copy-start.7 = (bf16[8,2,128,128]{3,2,1,0:T(8,128)(2,1)}, bf16[8,2,128,128]{3,2,1,0:T(8,128)(2,1)S(1)}, u32[]{:S(2)}) copy-start(bf16[8,2,128,128]{3,2,1,0:T(8,128)(2,1)S(1)} %all-to-all-done.2.v_own) | copy-start | bytes 1572868
  63.8 9.9 %collective-permute-start.2 = (bf16[8,2,128,128]{3,2,1,0:T(8,128)(2,1)S(1)}, bf16[8,2,128,128]{3,2,1,0:T(8,128)(2,1)S(1)}, u32[]{:S(2)}, u32[]{:S(2)}) collective-permute-start(bf16[8,2,128,128]{3,2,1,0:T(8,128)(2,1)S(1)} %all-to-all-done.2.v_own), channel_id=1, source_target_pairs={{0,2},{2,0},{1,3},{3,1},{4,6},{6,4},{5,7},{7,5},{8,10},{10,8},{9,1... | collective-permute-start | bytes 1572872 | tf_op jit(solution)/shard_map/ppermute | solution.py:340
  63.8 0.7 copy-start.10
  63.8 0.9 copy-start.2
  73.2 23.4 %collective-permute-start.11 = (f32[17,128,128]{2,1,0:T(8,128)}, f32[17,128,128]{2,1,0:T(8,128)S(1)}, u32[]{:S(2)}, u32[]{:S(2)}) collective-permute-start(f32[17,128,128]{2,1,0:T(8,128)} %get-tuple-element.20), channel_id=1, source_target_pairs={{0,2},{2,0},{1,3},{3,1},{4,6},{6,4},{5,7},{7,5},{8,10},{10,8},{9,1... | collective-permute-start | bytes 3342344 | tf_op jit(solution)/shard_map/ppermute | solution.py:340
  73.8 0.8 copy-start.9
  74.6 22.1 %copy-start.5 = (f32[17,128,128]{2,1,0:T(8,128)S(1)}, f32[17,128,128]{2,1,0:T(8,128)}, u32[]{:S(2)}) copy-start(f32[17,128,128]{2,1,0:T(8,128)} %get-tuple-element.19) | copy-start | bytes 3342340
  84.6 32.2 %collective-permute-start.3 = (f32[17,128,128]{2,1,0:T(8,128)}, f32[17,128,128]{2,1,0:T(8,128)}, u32[]{:S(2)}, u32[]{:S(2)}) collective-permute-start(f32[17,128,128]{2,1,0:T(8,128)} %get-tuple-element.16), channel_id=1, source_target_pairs={{0,2},{2,0},{1,3},{3,1},{4,6},{6,4},{5,7},{7,5},{8,10},{10,8},{9,1... | collective-permute-start | bytes 3342344 | tf_op jit(solution)/shard_map/ppermute | solution.py:340
  84.8 28.5 %all-to-all-start.3 = ((bf16[64,8,512]{2,1,0:T(8,128)(2,1)}), bf16[64,8,512]{2,1,0:T(8,128)(2,1)S(1)}, u32[]{:S(2)}, u32[]{:S(2)}) async-start(bf16[64,8,512]{2,1,0:T(8,128)(2,1)} %bitcast.72), calls=%async_computation.3 | async-start | bytes 1048576 | tf_op jit(solution)/shard_map/all_to_all | solution.py:591
  96.6 1.2 copy-start.6
  113.3 35.3 %all-to-all-start.4 = ((bf16[8,2,128,128]{3,2,1,0:T(8,128)(2,1)}), bf16[8,2,128,128]{3,2,1,0:T(8,128)(2,1)S(1)}, u32[]{:S(2)}, u32[]{:S(2)}) async-start(bf16[8,2,128,128]{3,2,1,0:T(8,128)(2,1)} %bitcast.29), calls=%async_computation.4 | async-start | bytes 1048576 | tf_op jit(solution)/shard_map/all_to_all | solution.py:407
  116.8 23.7 %copy-start.1 = (bf16[8,2,136,128]{3,2,1,0:T(8,128)(2,1)S(1)}, bf16[8,2,136,128]{3,2,1,0:T(8,128)(2,1)}, u32[]{:S(2)}) copy-start(bf16[8,2,136,128]{3,2,1,0:T(8,128)(2,1)} %copy-done) | copy-start | bytes 1671172
  116.9 23.7 %copy-start.3 = (bf16[8,2,136,128]{3,2,1,0:T(8,128)(2,1)S(1)}, bf16[8,2,136,128]{3,2,1,0:T(8,128)(2,1)}, u32[]{:S(2)}) copy-start(bf16[8,2,136,128]{3,2,1,0:T(8,128)(2,1)} %copy-done.2) | copy-start | bytes 1671172
  116.9 23.6 %copy-start.4 = (s32[6]{0:T(128)S(1)}, s32[6]{0:T(128)}, u32[]{:S(2)}) copy-start(s32[6]{0:T(128)} %stack.35.place_ref) | copy-start | bytes 76
  119.3 16.0 %collective-permute-start.10 = (bf16[2,128,128]{2,1,0:T(8,128)(2,1)S(1)}, bf16[2,128,128]{2,1,0:T(8,128)(2,1)S(1)}, u32[]{:S(2)}, u32[]{:S(2)}) collective-permute-start(bf16[2,128,128]{2,1,0:T(8,128)(2,1)S(1)} %get-tuple-element.24), channel_id=1, source_target_pairs={{0,28},{4,0},{8,4},{12,8},{16,12},{20,16},{24,20},{28,24},{1,29},{... | collective-permute-start | bytes 196616 | tf_op jit(solution)/shard_map/ppermute | solution.py:421
  122.5 15.8 %collective-permute-start.4 = (bf16[2,128,128]{2,1,0:T(8,128)(2,1)S(1)}, bf16[2,128,128]{2,1,0:T(8,128)(2,1)S(1)}, u32[]{:S(2)}, u32[]{:S(2)}) collective-permute-start(bf16[2,128,128]{2,1,0:T(8,128)(2,1)S(1)} %get-tuple-element.29), channel_id=1, source_target_pairs={{0,20},{4,24},{8,28},{12,0},{16,4},{20,8},{24,12},{28,16},{1,21},{... | collective-permute-start | bytes 196616 | tf_op jit(solution)/shard_map/ppermute | solution.py:421
  125.7 16.7 %collective-permute-start.5 = (bf16[2,128,128]{2,1,0:T(8,128)(2,1)}, bf16[2,128,128]{2,1,0:T(8,128)(2,1)S(1)}, u32[]{:S(2)}, u32[]{:S(2)}) collective-permute-start(bf16[2,128,128]{2,1,0:T(8,128)(2,1)} %get-tuple-element.23), channel_id=1, source_target_pairs={{0,4},{4,8},{8,12},{12,16},{16,20},{20,24},{24,28},{28,0},{1,5},{5... | collective-permute-start | bytes 196616 | tf_op jit(solution)/shard_map/ppermute | solution.py:421
  126.3 16.1 %collective-permute-start.6 = (bf16[2,128,128]{2,1,0:T(8,128)(2,1)}, bf16[2,128,128]{2,1,0:T(8,128)(2,1)S(1)}, u32[]{:S(2)}, u32[]{:S(2)}) collective-permute-start(bf16[2,128,128]{2,1,0:T(8,128)(2,1)} %get-tuple-element.28), channel_id=1, source_target_pairs={{0,8},{4,12},{8,16},{12,20},{16,24},{20,28},{24,0},{28,4},{1,9},{5... | collective-permute-start | bytes 196616 | tf_op jit(solution)/shard_map/ppermute | solution.py:421
  126.9 15.5 %collective-permute-start.7 = (bf16[2,128,128]{2,1,0:T(8,128)(2,1)}, bf16[2,128,128]{2,1,0:T(8,128)(2,1)}, u32[]{:S(2)}, u32[]{:S(2)}) collective-permute-start(bf16[2,128,128]{2,1,0:T(8,128)(2,1)} %get-tuple-element.27), channel_id=1, source_target_pairs={{0,12},{4,16},{8,20},{12,24},{16,28},{20,0},{24,4},{28,8},{1,13},{... | collective-permute-start | bytes 196616 | tf_op jit(solution)/shard_map/ppermute | solution.py:421
  135.2 11.4 %collective-permute-start.8 = (bf16[2,128,128]{2,1,0:T(8,128)(2,1)}, bf16[2,128,128]{2,1,0:T(8,128)(2,1)}, u32[]{:S(2)}, u32[]{:S(2)}) collective-permute-start(bf16[2,128,128]{2,1,0:T(8,128)(2,1)} %get-tuple-element.26), channel_id=1, source_target_pairs={{0,16},{4,20},{8,24},{12,28},{16,0},{20,4},{24,8},{28,12},{1,17},{... | collective-permute-start | bytes 196616 | tf_op jit(solution)/shard_map/ppermute | solution.py:421
  138.3 8.4 %collective-permute-start.9 = (bf16[2,128,128]{2,1,0:T(8,128)(2,1)}, bf16[2,128,128]{2,1,0:T(8,128)(2,1)}, u32[]{:S(2)}, u32[]{:S(2)}) collective-permute-start(bf16[2,128,128]{2,1,0:T(8,128)(2,1)} %get-tuple-element.25), channel_id=1, source_target_pairs={{0,24},{4,28},{8,0},{12,4},{16,8},{20,12},{24,16},{28,20},{1,25},{... | collective-permute-start | bytes 196616 | tf_op jit(solution)/shard_map/ppermute | solution.py:421
  148.8 7.4 %collective-permute-start.12 = (f32[128,256]{1,0:T(8,128)S(1)}, f32[128,256]{1,0:T(8,128)S(1)}, u32[]{:S(2)}, u32[]{:S(2)}) collective-permute-start(f32[128,256]{1,0:T(8,128)S(1)} %pad_maximum_fusion.2), channel_id=1, source_target_pairs={{32,0},{64,32},{96,64},{33,1},{65,33},{97,65},{34,2},{66,34},{98,6... | collective-permute-start | bytes 393224 | tf_op jit(solution)/shard_map/ppermute | solution.py:398
  152.7 8.5 %collective-permute-start.13 = (f32[128,256]{1,0:T(8,128)S(1)}, f32[128,256]{1,0:T(8,128)S(1)}, u32[]{:S(2)}, u32[]{:S(2)}) collective-permute-start(f32[128,256]{1,0:T(8,128)S(1)} %pad_maximum_fusion.3), channel_id=1, source_target_pairs={{64,0},{96,32},{65,1},{97,33},{66,2},{98,34},{67,3},{99,35},{68,4}... | collective-permute-start | bytes 393224 | tf_op jit(solution)/shard_map/ppermute | solution.py:399

commit v6 on v5

--- a/solution.py
+++ b/solution.py
@@ -400,16 +400,20 @@
     return (mine + from_next + from_last).astype(BF)
 
 
-def reduce_at_once(own, other, zs, z):
+def reduce_at_once(own, other, zs):
     rows, hd = own.shape[1:]
     swapped = swap(other)
     sent = (own[: 2 * zs] + swapped[: 2 * zs]).astype(BF).reshape(zs, 2, rows, hd)
     came = lax.all_to_all(sent, "z", split_axis=0, concat_axis=0, tiled=True)
+    return came, own[2 * zs] + swapped[2 * zs]
+
+
+def sum_arrived(came, far, zs, z):
     came = came.astype(F32)
     later = (jnp.arange(zs) >= z)[:, None, None]
     mine = jnp.sum(jnp.where(later, came[:, 1], 0.0), axis=0)
     near = jnp.sum(came[:, 0], axis=0)
-    far = jnp.sum(jnp.where(later, 0.0, came[:, 1]), axis=0) + own[2 * zs] + swapped[2 * zs]
+    far = jnp.sum(jnp.where(later, 0.0, came[:, 1]), axis=0) + far
     return mine, near, far
 
 
@@ -531,7 +535,7 @@
         far_other,
     )
     v_other = swap(v_own)
-    parts_v = reduce_at_once(dv_own, dv_other, zs, z)
+    came_v, far_v = reduce_at_once(dv_own, dv_other, zs)
     packed, dk_own, dk_other = pl.pallas_call(
         functools.partial(
             score_kernel, zs=zs, scale=scale, tile=tile, group=group, block=block_len
@@ -576,6 +580,7 @@
         probs,
     )
     *parts_k, halfway = reduce_by_shifts(dk_own, dk_other, zs, z)
+    parts_v = sum_arrived(lax.optimization_barrier((came_v, halfway))[0], far_v, zs, z)
     grads = along_x([jnp.concatenate(pair, axis=1) for pair in zip(parts_k, parts_v)], xs)
     grad_k, grad_v = grads[:, None, :hd], grads[:, None, hd:]
 

time: 163 us -> 163 us (level)
  no operation moved by 1% of the time
where the time goes in v6:
time: 163 us; the launch traced here: 162 us
  waiting for transfers between devices  70.4 us (43%)
  starting transfers between devices  55.7 us (34%)
  Pallas kernels  22.1 us (14%)
  other arithmetic  9.43 us (6%)
  local copies, waits for them, and re-layouts  3.24 us (2%)
    all_to_all x2, waiting for transfers between devices, along_z(): return lax.all_to_all(pair, 'z', split_axis=0, concat_axis=0, tiled=True)  30.4 us
    all_to_all x1, waiting for transfers between devices, program(): lax.all_to_all(packed.reshape(peers, 2 * block_len, width // 2), ('x', 'z...  15.5 us
    ppermute x7, starting transfers between devices, reduce_by_shifts(): came.append(lax.ppermute(sent, 'z', [(i, (i + k) % zs) for i in range(zs)]))  15.2 us
    all_to_all x2, starting transfers between devices, along_z(): return lax.all_to_all(pair, 'z', split_axis=0, concat_axis=0, tiled=True)  12 us
    all_to_all x1, starting transfers between devices, program(): lax.all_to_all(packed.reshape(peers, 2 * block_len, width // 2), ('x', 'z...  11.8 us
    ppermute x7, waiting for transfers between devices, reduce_by_shifts(): came.append(lax.ppermute(sent, 'z', [(i, (i + k) % zs) for i in range(zs)]))  10.2 us
    pallas_call x1, Pallas kernels, program(): pl.pallas_call(functools.partial(score_kernel, zs=zs, scale=scale, tile=t...  10 us
    pallas_call x1, Pallas kernels, program(): pl.pallas_call(functools.partial(softmax_kernel, zs=zs, scale=scale, tile...  8.49 us
  transfers between devices with their start and end apart: 19, of which 8 were waited for; matrix products, arithmetic and copies ran while one was open for 5% of the time, Pallas kernels for 13%

profile of v6, /device:TPU:2, one launch (start us, length us, event | category | flops | bytes accessed | tf_op | source)
XLA Modules:
  0.0 161.9 jit_solution(3164578041210724408)
XLA Ops:
  0.6 1.7 %first_payload.1 = bf16[16,40,256]{2,1,0:T(8,128)(2,1)} custom-call(bf16[32,4,128]{2,1,0:T(4,128)(2,1)} %keys_ref.1, bf16[32,4,128]{2,1,0:T(4,128)(2,1)} %values_ref.1, s32[1,128]{1,0:T(1,128)} %bitcast.75, s32[1,32]{1,0:T(1,128)} %bitcast.77), custom_call_target="tpu_custom_call" | custom-call | tf_op jit(solution)/shard_map/first_payload/pallas_call | solution.py:456
  2.3 7.5 %all-to-all-start = ((bf16[16,40,256]{2,1,0:T(8,128)(2,1)}), bf16[16,40,256]{2,1,0:T(8,128)(2,1)S(1)}, u32[]{:S(2)}, u32[]{:S(2)}) async-start(bf16[16,40,256]{2,1,0:T(8,128)(2,1)} %first_payload.1), calls=%async_computation | async-start | bytes 655360 | tf_op jit(solution)/shard_map/all_to_all | solution.py:464
  9.8 8.0 %all-to-all-done = bf16[16,40,256]{2,1,0:T(8,128)(2,1)S(1)} async-done(((bf16[16,40,256]{2,1,0:T(8,128)(2,1)}), bf16[16,40,256]{2,1,0:T(8,128)(2,1)S(1)}, u32[]{:S(2)}, u32[]{:S(2)}) %all-to-all-start) | async-done | bytes 327712 | tf_op jit(solution)/shard_map/all_to_all | solution.py:464
  18.1 0.9 pad_maximum_fusion
  19.0 8.5 %all-to-all-start.1 = ((bf16[8,2,136,128]{3,2,1,0:T(8,128)(2,1)}), bf16[8,2,136,128]{3,2,1,0:T(8,128)(2,1)S(1)}, u32[]{:S(2)}, u32[]{:S(2)}) async-start(bf16[8,2,136,128]{3,2,1,0:T(8,128)(2,1)} %pad_maximum_fusion), calls=%async_computation.1 | async-start | bytes 1114112 | tf_op jit(solution)/shard_map/all_to_all | solution.py:484
  28.5 16.1 %all-to-all-done.1.k_own = bf16[8,2,136,128]{3,2,1,0:T(8,128)(2,1)S(1)} async-done(((bf16[8,2,136,128]{3,2,1,0:T(8,128)(2,1)}), bf16[8,2,136,128]{3,2,1,0:T(8,128)(2,1)S(1)}, u32[]{:S(2)}, u32[]{:S(2)}) %all-to-all-start.1) | async-done | bytes 557088 | tf_op jit(solution)/shard_map/all_to_all | solution.py:484
  44.6 3.5 %all-to-all-start.2 = ((bf16[8,2,128,128]{3,2,1,0:T(8,128)(2,1)}), bf16[8,2,128,128]{3,2,1,0:T(8,128)(2,1)S(1)}, u32[]{:S(2)}, u32[]{:S(2)}) async-start(bf16[8,2,128,128]{3,2,1,0:T(8,128)(2,1)} %pad_maximum_fusion.1), calls=%async_computation.2 | async-start | bytes 1048576 | tf_op jit(solution)/shard_map/all_to_all | solution.py:484
  49.4 14.4 %all-to-all-done.2.v_own = bf16[8,2,128,128]{3,2,1,0:T(8,128)(2,1)S(1)} async-done(((bf16[8,2,128,128]{3,2,1,0:T(8,128)(2,1)}), bf16[8,2,128,128]{3,2,1,0:T(8,128)(2,1)S(1)}, u32[]{:S(2)}, u32[]{:S(2)}) %all-to-all-start.2) | async-done | bytes 524320 | tf_op jit(solution)/shard_map/all_to_all | solution.py:484
  64.7 8.5 %softmax_and_value_gradient.1 = (f32[17,128,128]{2,1,0:T(8,128)}, f32[17,128,128]{2,1,0:T(8,128)}, f32[9,512,1024]{2,1,0:T(8,128)}, s32[1]{0:T(128)}, f32[9,8,1024]{2,1,0:T(8,128)}) custom-call(s32[6]{0:T(128)} %stack.35.place_ref, bf16[128,1024]{1,0:T(8,128)(2,1)} %bitcast.79, bf16[128,1024]{1,0:T(8,128)(2,1)} %bitcast.81, s32[1,128]{1,0:T(1,128)} %bitcast.76, ...), custom_call_target="tpu_custom_call" | custom-call | flops 12000000000 | bytes 20000000 | tf_op jit(solution)/shard_map/softmax_and_value_gradient/pallas_call | solution.py:501
  74.6 10.0 %score_gradient.1 = (bf16[512,512]{1,0:T(8,128)(2,1)}, f32[17,128,128]{2,1,0:T(8,128)}, f32[17,128,128]{2,1,0:T(8,128)}) custom-call(s32[6]{0:T(128)} %stack.35.place_ref, s32[1]{0:T(128)} %get-tuple-element.13.info_ref, bf16[128,1024]{1,0:T(8,128)(2,1)} %bitcast.80, bf16[128,1024]{1,0:T(8,128)(2,1)} %bitcast.82, bf16[128,1024]{1,0:T(8,128)(2,1)} %bitcast.83, ...), custom_call_target="tpu_custom_call" | custom-call | flops 12000000000 | bytes 20000000 | tf_op jit(solution)/shard_map/score_gradient/pallas_call | solution.py:539
  84.8 11.8 %all-to-all-start.3 = ((bf16[64,8,512]{2,1,0:T(8,128)(2,1)}), bf16[64,8,512]{2,1,0:T(8,128)(2,1)S(1)}, u32[]{:S(2)}, u32[]{:S(2)}) async-start(bf16[64,8,512]{2,1,0:T(8,128)(2,1)} %bitcast.68), calls=%async_computation.3 | async-start | bytes 1048576 | tf_op jit(solution)/shard_map/all_to_all | solution.py:596
  96.6 1.1 fusion
  97.8 15.5 %all-to-all-done.3 = bf16[64,8,512]{2,1,0:T(8,128)(2,1)S(1)} async-done(((bf16[64,8,512]{2,1,0:T(8,128)(2,1)}), bf16[64,8,512]{2,1,0:T(8,128)(2,1)S(1)}, u32[]{:S(2)}, u32[]{:S(2)}) %all-to-all-start.3) | async-done | bytes 524320 | tf_op jit(solution)/shard_map/all_to_all | solution.py:596
  113.3 3.6 %all-to-all-start.4 = ((bf16[8,2,128,128]{3,2,1,0:T(8,128)(2,1)}), bf16[8,2,128,128]{3,2,1,0:T(8,128)(2,1)S(1)}, u32[]{:S(2)}, u32[]{:S(2)}) async-start(bf16[8,2,128,128]{3,2,1,0:T(8,128)(2,1)} %bitcast.29), calls=%async_computation.4 | async-start | bytes 1048576 | tf_op jit(solution)/shard_map/all_to_all | solution.py:407
  116.9 2.4 %fusion.6 = (bf16[2,128,128]{2,1,0:T(8,128)(2,1)}, bf16[2,128,128]{2,1,0:T(8,128)(2,1)S(1)}, bf16[2,128,128]{2,1,0:T(8,128)(2,1)}, bf16[2,128,128]{2,1,0:T(8,128...) fusion(f32[17,128,128]{2,1,0:T(8,128)} %collective-permute-done.3, ...), kind=kLoop, calls=%fused_computation.21 | loop fusion | flops 458752 | bytes 2293760 | tf_op jit(solution)/shard_map/convert_element_type | solution.py:424
  119.3 3.2 %collective-permute-start.10 = (bf16[2,128,128]{2,1,0:T(8,128)(2,1)S(1)}, bf16[2,128,128]{2,1,0:T(8,128)(2,1)S(1)}, u32[]{:S(2)}, u32[]{:S(2)}) collective-permute-start(bf16[2,128,128]{2,1,0:T(8,128)(2,1)S(1)} %get-tuple-element.26), channel_id=1, source_target_pairs={{0,28},{4,0},{8,4},{12,8},{16,12},{20,16},{24,20},{28,24},{1,29},{... | collective-permute-start | bytes 196616 | tf_op jit(solution)/shard_map/ppermute | solution.py:425
  122.5 3.3 %collective-permute-start.4 = (bf16[2,128,128]{2,1,0:T(8,128)(2,1)S(1)}, bf16[2,128,128]{2,1,0:T(8,128)(2,1)S(1)}, u32[]{:S(2)}, u32[]{:S(2)}) collective-permute-start(bf16[2,128,128]{2,1,0:T(8,128)(2,1)S(1)} %get-tuple-element.31), channel_id=1, source_target_pairs={{0,20},{4,24},{8,28},{12,0},{16,4},{20,8},{24,12},{28,16},{1,21},{... | collective-permute-start | bytes 196616 | tf_op jit(solution)/shard_map/ppermute | solution.py:425
  126.9 2.4 %collective-permute-start.7 = (bf16[2,128,128]{2,1,0:T(8,128)(2,1)}, bf16[2,128,128]{2,1,0:T(8,128)(2,1)}, u32[]{:S(2)}, u32[]{:S(2)}) collective-permute-start(bf16[2,128,128]{2,1,0:T(8,128)(2,1)} %get-tuple-element.29), channel_id=1, source_target_pairs={{0,12},{4,16},{8,20},{12,24},{16,28},{20,0},{24,4},{28,8},{1,13},{... | collective-permute-start | bytes 196616 | tf_op jit(solution)/shard_map/ppermute | solution.py:425
  129.2 6.0 %collective-permute-done.10 = bf16[2,128,128]{2,1,0:T(8,128)(2,1)S(1)} collective-permute-done((bf16[2,128,128]{2,1,0:T(8,128)(2,1)S(1)}, bf16[2,128,128]{2,1,0:T(8,128)(2,1)S(1)}, u32[]{:S(2)}, u32[]{:S(2)}) %collective-permute-start.10) | collective-permute-done | bytes 65568 | tf_op jit(solution)/shard_map/ppermute | solution.py:425
  135.2 3.0 %collective-permute-start.8 = (bf16[2,128,128]{2,1,0:T(8,128)(2,1)}, bf16[2,128,128]{2,1,0:T(8,128)(2,1)}, u32[]{:S(2)}, u32[]{:S(2)}) collective-permute-start(bf16[2,128,128]{2,1,0:T(8,128)(2,1)} %get-tuple-element.28), channel_id=1, source_target_pairs={{0,16},{4,20},{8,24},{12,28},{16,0},{20,4},{24,8},{28,12},{1,17},{... | collective-permute-start | bytes 196616 | tf_op jit(solution)/shard_map/ppermute | solution.py:425
  138.3 2.2 %collective-permute-start.9 = (bf16[2,128,128]{2,1,0:T(8,128)(2,1)}, bf16[2,128,128]{2,1,0:T(8,128)(2,1)}, u32[]{:S(2)}, u32[]{:S(2)}) collective-permute-start(bf16[2,128,128]{2,1,0:T(8,128)(2,1)} %get-tuple-element.27), channel_id=1, source_target_pairs={{0,24},{4,28},{8,0},{12,4},{16,8},{20,12},{24,16},{28,20},{1,25},{... | collective-permute-start | bytes 196616 | tf_op jit(solution)/shard_map/ppermute | solution.py:425
  140.5 0.9 placement_choice.1.pick_ref
  141.4 1.0 query_gradient_placement.1
  142.4 4.2 %collective-permute-done.8 = bf16[2,128,128]{2,1,0:T(8,128)(2,1)} collective-permute-done((bf16[2,128,128]{2,1,0:T(8,128)(2,1)}, bf16[2,128,128]{2,1,0:T(8,128)(2,1)}, u32[]{:S(2)}, u32[]{:S(2)}) %collective-permute-start.8) | collective-permute-done | bytes 65568 | tf_op jit(solution)/shard_map/ppermute | solution.py:425
  146.6 0.9 fusion.36
  147.6 1.0 fusion.26
  148.8 3.0 %collective-permute-start.12 = (f32[128,256]{1,0:T(8,128)S(1)}, f32[128,256]{1,0:T(8,128)S(1)}, u32[]{:S(2)}, u32[]{:S(2)}) collective-permute-start(f32[128,256]{1,0:T(8,128)S(1)} %pad_maximum_fusion.2), channel_id=1, source_target_pairs={{32,0},{64,32},{96,64},{33,1},{65,33},{97,65},{34,2},{66,34},{98,6... | collective-permute-start | bytes 393224 | tf_op jit(solution)/shard_map/ppermute | solution.py:398
  151.8 0.9 fusion.28
  152.7 1.3 collective-permute-start.13
  154.0 1.0 fusion.18
  155.0 1.2 collective-permute-done.12
  156.2 5.0 %collective-permute-done.13 = f32[128,256]{1,0:T(8,128)S(1)} collective-permute-done((f32[128,256]{1,0:T(8,128)S(1)}, f32[128,256]{1,0:T(8,128)S(1)}, u32[]{:S(2)}, u32[]{:S(2)}) %collective-permute-start.13) | collective-permute-done | bytes 131104 | tf_op jit(solution)/shard_map/ppermute | solution.py:399
  (71 shorter events, 7.1 us)
Async XLA Ops:
  2.3 15.5 %all-to-all-start = ((bf16[16,40,256]{2,1,0:T(8,128)(2,1)}), bf16[16,40,256]{2,1,0:T(8,128)(2,1)S(1)}, u32[]{:S(2)}, u32[]{:S(2)}) async-start(bf16[16,40,256]{2,1,0:T(8,128)(2,1)} %first_payload.1), calls=%async_computation | async-start | bytes 655360 | tf_op jit(solution)/shard_map/all_to_all | solution.py:464
  19.0 25.6 %all-to-all-start.1 = ((bf16[8,2,136,128]{3,2,1,0:T(8,128)(2,1)}), bf16[8,2,136,128]{3,2,1,0:T(8,128)(2,1)S(1)}, u32[]{:S(2)}, u32[]{:S(2)}) async-start(bf16[8,2,136,128]{3,2,1,0:T(8,128)(2,1)} %pad_maximum_fusion), calls=%async_computation.1 | async-start | bytes 1114112 | tf_op jit(solution)/shard_map/all_to_all | solution.py:484
  44.6 19.3 %copy-start = (bf16[8,2,136,128]{3,2,1,0:T(8,128)(2,1)}, bf16[8,2,136,128]{3,2,1,0:T(8,128)(2,1)S(1)}, u32[]{:S(2)}) copy-start(bf16[8,2,136,128]{3,2,1,0:T(8,128)(2,1)S(1)} %all-to-all-done.1.k_own) | copy-start | bytes 1671172
  44.6 19.2 %all-to-all-start.2 = ((bf16[8,2,128,128]{3,2,1,0:T(8,128)(2,1)}), bf16[8,2,128,128]{3,2,1,0:T(8,128)(2,1)S(1)}, u32[]{:S(2)}, u32[]{:S(2)}) async-start(bf16[8,2,128,128]{3,2,1,0:T(8,128)(2,1)} %pad_maximum_fusion.1), calls=%async_computation.2 | async-start | bytes 1048576 | tf_op jit(solution)/shard_map/all_to_all | solution.py:484
  48.1 15.8 %collective-permute-start = (bf16[8,2,136,128]{3,2,1,0:T(8,128)(2,1)S(1)}, bf16[8,2,136,128]{3,2,1,0:T(8,128)(2,1)S(1)}, u32[]{:S(2)}, u32[]{:S(2)}) collective-permute-start(bf16[8,2,136,128]{3,2,1,0:T(8,128)(2,1)S(1)} %all-to-all-done.1.k_own), channel_id=1, source_target_pairs={{0,2},{2,0},{1,3},{3,1},{4,6},{6,4},{5,7},{7,5},{8,10},{10,8},{9,1... | collective-permute-start | bytes 1671176 | tf_op jit(solution)/shard_map/ppermute | solution.py:340
  48.2 15.7 %copy-start.8 = (bf16[136,256]{1,0:T(8,128)(2,1)}, bf16[136,256]{1,0:T(8,128)(2,1)S(1)}, u32[]{:S(2)}) copy-start(bf16[136,256]{1,0:T(8,128)(2,1)S(1)} %pad_maximum_fusion.4.far_own) | copy-start | bytes 208900
  48.2 15.6 %collective-permute-start.1 = (bf16[136,256]{1,0:T(8,128)(2,1)S(1)}, bf16[136,256]{1,0:T(8,128)(2,1)S(1)}, u32[]{:S(2)}, u32[]{:S(2)}) collective-permute-start(bf16[136,256]{1,0:T(8,128)(2,1)S(1)} %pad_maximum_fusion.4.far_own), channel_id=1, source_target_pairs={{0,2},{2,0},{1,3},{3,1},{4,6},{6,4},{5,7},{7,5},{8,10},{10,8},{9,1... | collective-permute-start | bytes 208904 | tf_op jit(solution)/shard_map/ppermute | solution.py:340
  63.8 9.4 %copy-start.7 = (bf16[8,2,128,128]{3,2,1,0:T(8,128)(2,1)}, bf16[8,2,128,128]{3,2,1,0:T(8,128)(2,1)S(1)}, u32[]{:S(2)}) copy-start(bf16[8,2,128,128]{3,2,1,0:T(8,128)(2,1)S(1)} %all-to-all-done.2.v_own) | copy-start | bytes 1572868
  63.8 9.9 %collective-permute-start.2 = (bf16[8,2,128,128]{3,2,1,0:T(8,128)(2,1)S(1)}, bf16[8,2,128,128]{3,2,1,0:T(8,128)(2,1)S(1)}, u32[]{:S(2)}, u32[]{:S(2)}) collective-permute-start(bf16[8,2,128,128]{3,2,1,0:T(8,128)(2,1)S(1)} %all-to-all-done.2.v_own), channel_id=1, source_target_pairs={{0,2},{2,0},{1,3},{3,1},{4,6},{6,4},{5,7},{7,5},{8,10},{10,8},{9,1... | collective-permute-start | bytes 1572872 | tf_op jit(solution)/shard_map/ppermute | solution.py:340
  63.8 0.7 copy-start.10
  63.8 0.9 copy-start.2
  73.2 23.4 %collective-permute-start.11 = (f32[17,128,128]{2,1,0:T(8,128)}, f32[17,128,128]{2,1,0:T(8,128)S(1)}, u32[]{:S(2)}, u32[]{:S(2)}) collective-permute-start(f32[17,128,128]{2,1,0:T(8,128)} %get-tuple-element.21), channel_id=1, source_target_pairs={{0,2},{2,0},{1,3},{3,1},{4,6},{6,4},{5,7},{7,5},{8,10},{10,8},{9,1... | collective-permute-start | bytes 3342344 | tf_op jit(solution)/shard_map/ppermute | solution.py:340
  73.8 0.8 copy-start.9
  74.6 22.1 %copy-start.5 = (f32[17,128,128]{2,1,0:T(8,128)S(1)}, f32[17,128,128]{2,1,0:T(8,128)}, u32[]{:S(2)}) copy-start(f32[17,128,128]{2,1,0:T(8,128)} %get-tuple-element.20) | copy-start | bytes 3342340
  84.6 32.2 %collective-permute-start.3 = (f32[17,128,128]{2,1,0:T(8,128)}, f32[17,128,128]{2,1,0:T(8,128)}, u32[]{:S(2)}, u32[]{:S(2)}) collective-permute-start(f32[17,128,128]{2,1,0:T(8,128)} %get-tuple-element.17), channel_id=1, source_target_pairs={{0,2},{2,0},{1,3},{3,1},{4,6},{6,4},{5,7},{7,5},{8,10},{10,8},{9,1... | collective-permute-start | bytes 3342344 | tf_op jit(solution)/shard_map/ppermute | solution.py:340
  84.8 28.5 %all-to-all-start.3 = ((bf16[64,8,512]{2,1,0:T(8,128)(2,1)}), bf16[64,8,512]{2,1,0:T(8,128)(2,1)S(1)}, u32[]{:S(2)}, u32[]{:S(2)}) async-start(bf16[64,8,512]{2,1,0:T(8,128)(2,1)} %bitcast.68), calls=%async_computation.3 | async-start | bytes 1048576 | tf_op jit(solution)/shard_map/all_to_all | solution.py:596
  96.6 1.2 copy-start.6
  113.3 35.3 %all-to-all-start.4 = ((bf16[8,2,128,128]{3,2,1,0:T(8,128)(2,1)}), bf16[8,2,128,128]{3,2,1,0:T(8,128)(2,1)S(1)}, u32[]{:S(2)}, u32[]{:S(2)}) async-start(bf16[8,2,128,128]{3,2,1,0:T(8,128)(2,1)} %bitcast.29), calls=%async_computation.4 | async-start | bytes 1048576 | tf_op jit(solution)/shard_map/all_to_all | solution.py:407
  116.8 23.7 %copy-start.1 = (bf16[8,2,136,128]{3,2,1,0:T(8,128)(2,1)S(1)}, bf16[8,2,136,128]{3,2,1,0:T(8,128)(2,1)}, u32[]{:S(2)}) copy-start(bf16[8,2,136,128]{3,2,1,0:T(8,128)(2,1)} %copy-done) | copy-start | bytes 1671172
  116.9 23.7 %copy-start.3 = (bf16[8,2,136,128]{3,2,1,0:T(8,128)(2,1)S(1)}, bf16[8,2,136,128]{3,2,1,0:T(8,128)(2,1)}, u32[]{:S(2)}) copy-start(bf16[8,2,136,128]{3,2,1,0:T(8,128)(2,1)} %copy-done.2) | copy-start | bytes 1671172
  116.9 23.6 %copy-start.4 = (s32[6]{0:T(128)S(1)}, s32[6]{0:T(128)}, u32[]{:S(2)}) copy-start(s32[6]{0:T(128)} %stack.35.place_ref) | copy-start | bytes 76
  119.3 16.0 %collective-permute-start.10 = (bf16[2,128,128]{2,1,0:T(8,128)(2,1)S(1)}, bf16[2,128,128]{2,1,0:T(8,128)(2,1)S(1)}, u32[]{:S(2)}, u32[]{:S(2)}) collective-permute-start(bf16[2,128,128]{2,1,0:T(8,128)(2,1)S(1)} %get-tuple-element.26), channel_id=1, source_target_pairs={{0,28},{4,0},{8,4},{12,8},{16,12},{20,16},{24,20},{28,24},{1,29},{... | collective-permute-start | bytes 196616 | tf_op jit(solution)/shard_map/ppermute | solution.py:425
  122.5 15.8 %collective-permute-start.4 = (bf16[2,128,128]{2,1,0:T(8,128)(2,1)S(1)}, bf16[2,128,128]{2,1,0:T(8,128)(2,1)S(1)}, u32[]{:S(2)}, u32[]{:S(2)}) collective-permute-start(bf16[2,128,128]{2,1,0:T(8,128)(2,1)S(1)} %get-tuple-element.31), channel_id=1, source_target_pairs={{0,20},{4,24},{8,28},{12,0},{16,4},{20,8},{24,12},{28,16},{1,21},{... | collective-permute-start | bytes 196616 | tf_op jit(solution)/shard_map/ppermute | solution.py:425
  125.7 16.7 %collective-permute-start.5 = (bf16[2,128,128]{2,1,0:T(8,128)(2,1)}, bf16[2,128,128]{2,1,0:T(8,128)(2,1)S(1)}, u32[]{:S(2)}, u32[]{:S(2)}) collective-permute-start(bf16[2,128,128]{2,1,0:T(8,128)(2,1)} %get-tuple-element.25), channel_id=1, source_target_pairs={{0,4},{4,8},{8,12},{12,16},{16,20},{20,24},{24,28},{28,0},{1,5},{5... | collective-permute-start | bytes 196616 | tf_op jit(solution)/shard_map/ppermute | solution.py:425
  126.3 16.1 %collective-permute-start.6 = (bf16[2,128,128]{2,1,0:T(8,128)(2,1)}, bf16[2,128,128]{2,1,0:T(8,128)(2,1)S(1)}, u32[]{:S(2)}, u32[]{:S(2)}) collective-permute-start(bf16[2,128,128]{2,1,0:T(8,128)(2,1)} %get-tuple-element.30), channel_id=1, source_target_pairs={{0,8},{4,12},{8,16},{12,20},{16,24},{20,28},{24,0},{28,4},{1,9},{5... | collective-permute-start | bytes 196616 | tf_op jit(solution)/shard_map/ppermute | solution.py:425
  126.9 15.5 %collective-permute-start.7 = (bf16[2,128,128]{2,1,0:T(8,128)(2,1)}, bf16[2,128,128]{2,1,0:T(8,128)(2,1)}, u32[]{:S(2)}, u32[]{:S(2)}) collective-permute-start(bf16[2,128,128]{2,1,0:T(8,128)(2,1)} %get-tuple-element.29), channel_id=1, source_target_pairs={{0,12},{4,16},{8,20},{12,24},{16,28},{20,0},{24,4},{28,8},{1,13},{... | collective-permute-start | bytes 196616 | tf_op jit(solution)/shard_map/ppermute | solution.py:425
  135.2 11.4 %collective-permute-start.8 = (bf16[2,128,128]{2,1,0:T(8,128)(2,1)}, bf16[2,128,128]{2,1,0:T(8,128)(2,1)}, u32[]{:S(2)}, u32[]{:S(2)}) collective-permute-start(bf16[2,128,128]{2,1,0:T(8,128)(2,1)} %get-tuple-element.28), channel_id=1, source_target_pairs={{0,16},{4,20},{8,24},{12,28},{16,0},{20,4},{24,8},{28,12},{1,17},{... | collective-permute-start | bytes 196616 | tf_op jit(solution)/shard_map/ppermute | solution.py:425
  138.3 8.4 %collective-permute-start.9 = (bf16[2,128,128]{2,1,0:T(8,128)(2,1)}, bf16[2,128,128]{2,1,0:T(8,128)(2,1)}, u32[]{:S(2)}, u32[]{:S(2)}) collective-permute-start(bf16[2,128,128]{2,1,0:T(8,128)(2,1)} %get-tuple-element.27), channel_id=1, source_target_pairs={{0,24},{4,28},{8,0},{12,4},{16,8},{20,12},{24,16},{28,20},{1,25},{... | collective-permute-start | bytes 196616 | tf_op jit(solution)/shard_map/ppermute | solution.py:425
  148.8 7.4 %collective-permute-start.12 = (f32[128,256]{1,0:T(8,128)S(1)}, f32[128,256]{1,0:T(8,128)S(1)}, u32[]{:S(2)}, u32[]{:S(2)}) collective-permute-start(f32[128,256]{1,0:T(8,128)S(1)} %pad_maximum_fusion.2), channel_id=1, source_target_pairs={{32,0},{64,32},{96,64},{33,1},{65,33},{97,65},{34,2},{66,34},{98,6... | collective-permute-start | bytes 393224 | tf_op jit(solution)/shard_map/ppermute | solution.py:398
  152.7 8.5 %collective-permute-start.13 = (f32[128,256]{1,0:T(8,128)S(1)}, f32[128,256]{1,0:T(8,128)S(1)}, u32[]{:S(2)}, u32[]{:S(2)}) collective-permute-start(f32[128,256]{1,0:T(8,128)S(1)} %pad_maximum_fusion.3), channel_id=1, source_target_pairs={{64,0},{96,32},{65,1},{97,33},{66,2},{98,34},{67,3},{99,35},{68,4}... | collective-permute-start | bytes 393224 | tf_op jit(solution)/shard_map/ppermute | solution.py:399

commit v7 on v6

--- a/solution.py
+++ b/solution.py
@@ -64,10 +64,10 @@
     @pl.when(j >= z)
     def _():
         own[index(j)] = value[:rows]
-        other[index(j)] = value[rows : 2 * rows]
+        other[index(j)] = value[rows : 2 * rows].astype(other.dtype)
 
     own[index(j + 1)] = value[2 * rows : 3 * rows]
-    other[index(j + 1)] = value[3 * rows :]
+    other[index(j + 1)] = value[3 * rows :].astype(other.dtype)
 
 
 def softmax_kernel(
@@ -209,7 +209,7 @@
     def clear(j, carry):
         at = out_index(j, z, zs)
         dv_own[at] = jnp.zeros((rows, hd), F32)
-        dv_other[at] = jnp.zeros((rows, hd), F32)
+        dv_other[at] = jnp.zeros((rows, hd), BF)
         return carry
 
     lax.fori_loop(z, lo, clear, 0)
@@ -286,7 +286,7 @@
     def clear(j, carry):
         at = relative_index(j, z, zs)
         dk_own[at] = jnp.zeros((rows, hd), F32)
-        dk_other[at] = jnp.zeros((rows, hd), F32)
+        dk_other[at] = jnp.zeros((rows, hd), BF)
         return carry
 
     lax.fori_loop(z, lo, clear, 0)
@@ -403,9 +403,9 @@
 def reduce_at_once(own, other, zs):
     rows, hd = own.shape[1:]
     swapped = swap(other)
-    sent = (own[: 2 * zs] + swapped[: 2 * zs]).astype(BF).reshape(zs, 2, rows, hd)
+    sent = (own[: 2 * zs] + swapped[: 2 * zs].astype(F32)).astype(BF).reshape(zs, 2, rows, hd)
     came = lax.all_to_all(sent, "z", split_axis=0, concat_axis=0, tiled=True)
-    return came, own[2 * zs] + swapped[2 * zs]
+    return came, own[2 * zs] + swapped[2 * zs].astype(F32)
 
 
 def sum_arrived(came, far, zs, z):
@@ -419,13 +419,15 @@
 
 def reduce_by_shifts(own, other, zs, z):
     swapped = swap(other)
+
+    def both(at):
+        return own[at] + swapped[at].astype(F32)
+
     came = []
     for k in range(1, zs):
-        sent = (own[2 * k : 2 * k + 2] + swapped[2 * k : 2 * k + 2]).astype(BF)
+        sent = both(slice(2 * k, 2 * k + 2)).astype(BF)
         came.append(lax.ppermute(sent, "z", [(i, (i + k) % zs) for i in range(zs)]))
-    mine = own[1] + swapped[1]
-    near = own[0] + swapped[0]
-    far = own[2 * zs] + swapped[2 * zs]
+    mine, near, far = both(1), both(0), both(2 * zs)
     for k, got in enumerate(came, 1):
         near = near + got[0].astype(F32)
         mine = mine + jnp.where(z < k, got[1].astype(F32), 0.0)
@@ -495,7 +497,8 @@
     q = queries.reshape(rows, width)
     do = grad_out.reshape(rows, width)
     o = outputs.reshape(rows, width)
-    grad_shape = jax.ShapeDtypeStruct((chips, rows, hd), F32)
+    own_shape = jax.ShapeDtypeStruct((chips, rows, hd), F32)
+    other_shape = jax.ShapeDtypeStruct((chips, rows, hd), BF)
     params = pltpu.CompilerParams(vmem_limit_bytes=VMEM_BYTES)
     small = pltpu.CompilerParams(vmem_limit_bytes=8 * 1024 * 1024)
     dv_own, dv_other, probs, info, factors = pl.pallas_call(
@@ -503,8 +506,8 @@
         in_specs=[smem] + [vmem] * 7,
         out_specs=[vmem, vmem, anywhere, smem, vmem],
         out_shape=[
-            grad_shape,
-            grad_shape,
+            own_shape,
+            other_shape,
             jax.ShapeDtypeStruct((steps, 4 * rows, total), F32),
             jax.ShapeDtypeStruct((1,), jnp.int32),
             jax.ShapeDtypeStruct((steps, 8, total), F32),
@@ -544,8 +547,8 @@
         out_specs=[vmem] * 3,
         out_shape=[
             jax.ShapeDtypeStruct((peers * 2 * block_len, width // 2), BF),
-            grad_shape,
-            grad_shape,
+            own_shape,
+            other_shape,
         ],
         scratch_shapes=[
             pltpu.VMEM((total, hd), BF),
@@ -592,7 +595,7 @@
         cost_estimate=pl.CostEstimate(flops=100_000_000, bytes_accessed=1_000_000, transcendentals=0),
         compiler_params=small,
         name="placement_choice",
-    )(lax.optimization_barrier((place, halfway))[0], k_own, k_other)
+    )(place, k_own, k_other)
     arrived = lax.all_to_all(
         packed.reshape(peers, 2 * block_len, width // 2),
         ("x", "z", "core"),

time: 163 us -> 152 us (0.933)
  waiting for transfers between devices: 70.4 us -> 55.2 us
  starting transfers between devices: 55.7 us -> 60.4 us
    all_to_all x1, waiting for transfers between devices: 15.5 us -> 10.2 us  [program(): lax.all_to_all(packed.reshape(peers, 2 * block_len, width // 2), ('x', 'z...]
    ppermute x1, waiting for transfers between devices: 5.03 us -> 0.01 us  [along_x(): from_last = lax.ppermute(far, 'x', [(i, i - 2) for i in range(2, xs)])]
    ppermute x7, starting transfers between devices: 15.2 us -> 20.2 us  [reduce_by_shifts(): came.append(lax.ppermute(sent, 'z', [(i, (i + k) % zs) for i in range(zs)]))]
    ppermute x7, waiting for transfers between devices: 10.2 us -> 6.61 us  [reduce_by_shifts(): came.append(lax.ppermute(sent, 'z', [(i, (i + k) % zs) for i in range(zs)]))]
  transfers between devices with their start and end apart: 19 -> 19, of which waited for: 8 -> 7; matrix products, arithmetic and copies ran while one was open for 5% -> 5% of each run, Pallas kernels for 13% -> 13%
where the time goes in v7:
time: 152 us; the launch traced here: 150 us
  starting transfers between devices  60.4 us (40%)
  waiting for transfers between devices  55.2 us (36%)
  Pallas kernels  21.3 us (14%)
  other arithmetic  8.36 us (6%)
  local copies, waits for them, and re-layouts  3.24 us (2%)
    all_to_all x2, waiting for transfers between devices, along_z(): return lax.all_to_all(pair, 'z', split_axis=0, concat_axis=0, tiled=True)  30.4 us
    ppermute x7, starting transfers between devices, reduce_by_shifts(): came.append(lax.ppermute(sent, 'z', [(i, (i + k) % zs) for i in range(zs)]))  20.2 us
    all_to_all x2, starting transfers between devices, along_z(): return lax.all_to_all(pair, 'z', split_axis=0, concat_axis=0, tiled=True)  12 us
    all_to_all x1, starting transfers between devices, program(): lax.all_to_all(packed.reshape(peers, 2 * block_len, width // 2), ('x', 'z...  11.8 us
    all_to_all x1, waiting for transfers between devices, program(): lax.all_to_all(packed.reshape(peers, 2 * block_len, width // 2), ('x', 'z...  10.2 us
    pallas_call x1, Pallas kernels, program(): pl.pallas_call(functools.partial(score_kernel, zs=zs, scale=scale, tile=t...  9.37 us
    pallas_call x1, Pallas kernels, program(): pl.pallas_call(functools.partial(softmax_kernel, zs=zs, scale=scale, tile...  8.31 us
    all_to_all x1, waiting for transfers between devices, program(): lax.all_to_all(mixed, ('dp', 'head', 'x'), split_axis=0, concat_axis=0, t...  8.01 us
  transfers between devices with their start and end apart: 19, of which 7 were waited for; matrix products, arithmetic and copies ran while one was open for 5% of the time, Pallas kernels for 13%

profile of v7, /device:TPU:2, one launch (start us, length us, event | category | flops | bytes accessed | tf_op | source)
XLA Modules:
  0.0 149.6 jit_solution(9549892760814644267)
XLA Ops:
  0.6 1.7 %first_payload.1 = bf16[16,40,256]{2,1,0:T(8,128)(2,1)} custom-call(bf16[32,4,128]{2,1,0:T(4,128)(2,1)} %keys_ref.1, bf16[32,4,128]{2,1,0:T(4,128)(2,1)} %values_ref.1, s32[1,128]{1,0:T(1,128)} %bitcast.72, s32[1,32]{1,0:T(1,128)} %bitcast.74), custom_call_target="tpu_custom_call" | custom-call | tf_op jit(solution)/shard_map/first_payload/pallas_call | solution.py:458
  2.3 7.5 %all-to-all-start = ((bf16[16,40,256]{2,1,0:T(8,128)(2,1)}), bf16[16,40,256]{2,1,0:T(8,128)(2,1)S(1)}, u32[]{:S(2)}, u32[]{:S(2)}) async-start(bf16[16,40,256]{2,1,0:T(8,128)(2,1)} %first_payload.1), calls=%async_computation | async-start | bytes 655360 | tf_op jit(solution)/shard_map/all_to_all | solution.py:466
  9.8 8.0 %all-to-all-done = bf16[16,40,256]{2,1,0:T(8,128)(2,1)S(1)} async-done(((bf16[16,40,256]{2,1,0:T(8,128)(2,1)}), bf16[16,40,256]{2,1,0:T(8,128)(2,1)S(1)}, u32[]{:S(2)}, u32[]{:S(2)}) %all-to-all-start) | async-done | bytes 327712 | tf_op jit(solution)/shard_map/all_to_all | solution.py:466
  18.1 0.9 pad_maximum_fusion
  19.0 8.5 %all-to-all-start.1 = ((bf16[8,2,136,128]{3,2,1,0:T(8,128)(2,1)}), bf16[8,2,136,128]{3,2,1,0:T(8,128)(2,1)S(1)}, u32[]{:S(2)}, u32[]{:S(2)}) async-start(bf16[8,2,136,128]{3,2,1,0:T(8,128)(2,1)} %pad_maximum_fusion), calls=%async_computation.1 | async-start | bytes 1114112 | tf_op jit(solution)/shard_map/all_to_all | solution.py:486
  27.6 0.9 pad_maximum_fusion.1
  28.5 16.1 %all-to-all-done.1.k_own = bf16[8,2,136,128]{3,2,1,0:T(8,128)(2,1)S(1)} async-done(((bf16[8,2,136,128]{3,2,1,0:T(8,128)(2,1)}), bf16[8,2,136,128]{3,2,1,0:T(8,128)(2,1)S(1)}, u32[]{:S(2)}, u32[]{:S(2)}) %all-to-all-start.1) | async-done | bytes 557088 | tf_op jit(solution)/shard_map/all_to_all | solution.py:486
  44.5 3.5 %all-to-all-start.2 = ((bf16[8,2,128,128]{3,2,1,0:T(8,128)(2,1)}), bf16[8,2,128,128]{3,2,1,0:T(8,128)(2,1)S(1)}, u32[]{:S(2)}, u32[]{:S(2)}) async-start(bf16[8,2,128,128]{3,2,1,0:T(8,128)(2,1)} %pad_maximum_fusion.1), calls=%async_computation.2 | async-start | bytes 1048576 | tf_op jit(solution)/shard_map/all_to_all | solution.py:486
  49.4 14.4 %all-to-all-done.2.v_own = bf16[8,2,128,128]{3,2,1,0:T(8,128)(2,1)S(1)} async-done(((bf16[8,2,128,128]{3,2,1,0:T(8,128)(2,1)}), bf16[8,2,128,128]{3,2,1,0:T(8,128)(2,1)S(1)}, u32[]{:S(2)}, u32[]{:S(2)}) %all-to-all-start.2) | async-done | bytes 524320 | tf_op jit(solution)/shard_map/all_to_all | solution.py:486
  64.7 8.3 %softmax_and_value_gradient.1 = (f32[17,128,128]{2,1,0:T(8,128)}, bf16[17,128,128]{2,1,0:T(8,128)(2,1)}, f32[9,512,1024]{2,1,0:T(8,128)}, s32[1]{0:T(128)}, f32[9,8,1024]{2,1,0:T(8,128)}) custom-call(s32[6]{0:T(128)} %stack.35.place_ref, bf16[128,1024]{1,0:T(8,128)(2,1)} %bitcast.76, bf16[128,1024]{1,0:T(8,128)(2,1)} %bitcast.78, s32[1,128]{1,0:T(1,128)} %bitcast.73, ...), custom_call_target="tpu_custom_call" | custom-call | flops 12000000000 | bytes 20000000 | tf_op jit(solution)/shard_map/softmax_and_value_gradient/pallas_call | solution.py:504
  73.6 0.8 copy-done.10
  74.4 9.4 %score_gradient.1 = (bf16[512,512]{1,0:T(8,128)(2,1)}, f32[17,128,128]{2,1,0:T(8,128)}, bf16[17,128,128]{2,1,0:T(8,128)(2,1)}) custom-call(s32[6]{0:T(128)} %stack.35.place_ref, s32[1]{0:T(128)} %get-tuple-element.12.info_ref, bf16[128,1024]{1,0:T(8,128)(2,1)} %bitcast.77, bf16[128,1024]{1,0:T(8,128)(2,1)} %bitcast.79, bf16[128,1024]{1,0:T(8,128)(2,1)} %bitcast.80, ...), custom_call_target="tpu_custom_call" | custom-call | flops 12000000000 | bytes 20000000 | tf_op jit(solution)/shard_map/score_gradient/pallas_call | solution.py:542
  84.0 0.9 add_convert_fusion
  84.9 4.0 %all-to-all-start.4 = ((bf16[8,2,128,128]{3,2,1,0:T(8,128)(2,1)}), bf16[8,2,128,128]{3,2,1,0:T(8,128)(2,1)S(1)}, u32[]{:S(2)}, u32[]{:S(2)}) async-start(bf16[8,2,128,128]{3,2,1,0:T(8,128)(2,1)} %bitcast.29), calls=%async_computation.4 | async-start | bytes 1048576 | tf_op jit(solution)/shard_map/all_to_all | solution.py:407
  89.0 1.9 %add_convert_fusion.7 = (bf16[2,128,128]{2,1,0:T(8,128)(2,1)S(1)}, bf16[2,128,128]{2,1,0:T(8,128)(2,1)S(1)}, bf16[2,128,128]{2,1,0:T(8,128)(2,1)S(1)}, bf16[2,12...) fusion(f32[17,128,128]{2,1,0:T(8,128)S(1)} %copy-done.5, ...), kind=kLoop, calls=%fused_computation.20 | loop fusion | flops 688128 | bytes 1835008 | tf_op jit(solution)/shard_map/convert_element_type | solution.py:428
  90.9 3.2 %collective-permute-start.10 = (bf16[2,128,128]{2,1,0:T(8,128)(2,1)S(1)}, bf16[2,128,128]{2,1,0:T(8,128)(2,1)S(1)}, u32[]{:S(2)}, u32[]{:S(2)}) collective-permute-start(bf16[2,128,128]{2,1,0:T(8,128)(2,1)S(1)} %get-tuple-element.24), channel_id=1, source_target_pairs={{0,28},{4,0},{8,4},{12,8},{16,12},{20,16},{24,20},{28,24},{1,29},{... | collective-permute-start | bytes 196616 | tf_op jit(solution)/shard_map/ppermute | solution.py:429
  94.1 1.7 %collective-permute-start.5 = (bf16[2,128,128]{2,1,0:T(8,128)(2,1)}, bf16[2,128,128]{2,1,0:T(8,128)(2,1)S(1)}, u32[]{:S(2)}, u32[]{:S(2)}) collective-permute-start(bf16[2,128,128]{2,1,0:T(8,128)(2,1)} %get-tuple-element.29), channel_id=1, source_target_pairs={{0,8},{4,12},{8,16},{12,20},{16,24},{20,28},{24,0},{28,4},{1,9},{5... | collective-permute-start | bytes 196616 | tf_op jit(solution)/shard_map/ppermute | solution.py:429
  95.8 3.6 %collective-permute-start.6 = (bf16[2,128,128]{2,1,0:T(8,128)(2,1)}, bf16[2,128,128]{2,1,0:T(8,128)(2,1)S(1)}, u32[]{:S(2)}, u32[]{:S(2)}) collective-permute-start(bf16[2,128,128]{2,1,0:T(8,128)(2,1)} %get-tuple-element.28), channel_id=1, source_target_pairs={{0,12},{4,16},{8,20},{12,24},{16,28},{20,0},{24,4},{28,8},{1,13},{... | collective-permute-start | bytes 196616 | tf_op jit(solution)/shard_map/ppermute | solution.py:429
  99.4 1.6 %collective-permute-start.7 = (bf16[2,128,128]{2,1,0:T(8,128)(2,1)}, bf16[2,128,128]{2,1,0:T(8,128)(2,1)S(1)}, u32[]{:S(2)}, u32[]{:S(2)}) collective-permute-start(bf16[2,128,128]{2,1,0:T(8,128)(2,1)} %get-tuple-element.27), channel_id=1, source_target_pairs={{0,16},{4,20},{8,24},{12,28},{16,0},{20,4},{24,8},{28,12},{1,17},{... | collective-permute-start | bytes 196616 | tf_op jit(solution)/shard_map/ppermute | solution.py:429
  101.0 5.6 %collective-permute-done.10 = bf16[2,128,128]{2,1,0:T(8,128)(2,1)S(1)} collective-permute-done((bf16[2,128,128]{2,1,0:T(8,128)(2,1)S(1)}, bf16[2,128,128]{2,1,0:T(8,128)(2,1)S(1)}, u32[]{:S(2)}, u32[]{:S(2)}) %collective-permute-start.10) | collective-permute-done | bytes 65568 | tf_op jit(solution)/shard_map/ppermute | solution.py:429
  106.6 2.7 %collective-permute-start.8 = (bf16[2,128,128]{2,1,0:T(8,128)(2,1)}, bf16[2,128,128]{2,1,0:T(8,128)(2,1)S(1)}, u32[]{:S(2)}, u32[]{:S(2)}) collective-permute-start(bf16[2,128,128]{2,1,0:T(8,128)(2,1)} %get-tuple-element.26), channel_id=1, source_target_pairs={{0,20},{4,24},{8,28},{12,0},{16,4},{20,8},{24,12},{28,16},{1,21},{... | collective-permute-start | bytes 196616 | tf_op jit(solution)/shard_map/ppermute | solution.py:429
  109.3 7.4 %collective-permute-start.9 = (bf16[2,128,128]{2,1,0:T(8,128)(2,1)S(1)}, bf16[2,128,128]{2,1,0:T(8,128)(2,1)S(1)}, u32[]{:S(2)}, u32[]{:S(2)}) collective-permute-start(bf16[2,128,128]{2,1,0:T(8,128)(2,1)S(1)} %get-tuple-element.25), channel_id=1, source_target_pairs={{0,24},{4,28},{8,0},{12,4},{16,8},{20,12},{24,16},{28,20},{1,25},{... | collective-permute-start | bytes 196616 | tf_op jit(solution)/shard_map/ppermute | solution.py:429
  116.7 0.9 placement_choice.1.pick_ref
  118.6 0.8 add_bitcast_fusion
  119.4 11.8 %all-to-all-start.3 = ((bf16[64,8,512]{2,1,0:T(8,128)(2,1)}), bf16[64,8,512]{2,1,0:T(8,128)(2,1)S(1)}, u32[]{:S(2)}, u32[]{:S(2)}) async-start(bf16[64,8,512]{2,1,0:T(8,128)(2,1)} %bitcast.25), calls=%async_computation.3 | async-start | bytes 1048576 | tf_op jit(solution)/shard_map/all_to_all | solution.py:599
  131.2 0.8 fusion.18
  132.2 2.4 %collective-permute-start.12 = (f32[128,256]{1,0:T(8,128)S(1)}, f32[128,256]{1,0:T(8,128)S(1)}, u32[]{:S(2)}, u32[]{:S(2)}) collective-permute-start(f32[128,256]{1,0:T(8,128)S(1)} %pad_maximum_fusion.2), channel_id=1, source_target_pairs={{32,0},{64,32},{96,64},{33,1},{65,33},{97,65},{34,2},{66,34},{98,6... | collective-permute-start | bytes 393224 | tf_op jit(solution)/shard_map/ppermute | solution.py:398
  134.7 0.9 bitcast_add_fusion
  135.6 1.3 collective-permute-start.13
  136.9 0.8 fusion.10
  137.7 10.2 %all-to-all-done.3 = bf16[64,8,512]{2,1,0:T(8,128)(2,1)S(1)} async-done(((bf16[64,8,512]{2,1,0:T(8,128)(2,1)}), bf16[64,8,512]{2,1,0:T(8,128)(2,1)S(1)}, u32[]{:S(2)}, u32[]{:S(2)}) %all-to-all-start.3) | async-done | bytes 524320 | tf_op jit(solution)/shard_map/all_to_all | solution.py:599
  147.9 1.0 query_gradient_placement.1
  (73 shorter events, 5.3 us)
Async XLA Ops:
  2.3 15.5 %all-to-all-start = ((bf16[16,40,256]{2,1,0:T(8,128)(2,1)}), bf16[16,40,256]{2,1,0:T(8,128)(2,1)S(1)}, u32[]{:S(2)}, u32[]{:S(2)}) async-start(bf16[16,40,256]{2,1,0:T(8,128)(2,1)} %first_payload.1), calls=%async_computation | async-start | bytes 655360 | tf_op jit(solution)/shard_map/all_to_all | solution.py:466
  19.0 25.6 %all-to-all-start.1 = ((bf16[8,2,136,128]{3,2,1,0:T(8,128)(2,1)}), bf16[8,2,136,128]{3,2,1,0:T(8,128)(2,1)S(1)}, u32[]{:S(2)}, u32[]{:S(2)}) async-start(bf16[8,2,136,128]{3,2,1,0:T(8,128)(2,1)} %pad_maximum_fusion), calls=%async_computation.1 | async-start | bytes 1114112 | tf_op jit(solution)/shard_map/all_to_all | solution.py:486
  44.5 19.3 %copy-start = (bf16[8,2,136,128]{3,2,1,0:T(8,128)(2,1)}, bf16[8,2,136,128]{3,2,1,0:T(8,128)(2,1)S(1)}, u32[]{:S(2)}) copy-start(bf16[8,2,136,128]{3,2,1,0:T(8,128)(2,1)S(1)} %all-to-all-done.1.k_own) | copy-start | bytes 1671172
  44.5 19.2 %all-to-all-start.2 = ((bf16[8,2,128,128]{3,2,1,0:T(8,128)(2,1)}), bf16[8,2,128,128]{3,2,1,0:T(8,128)(2,1)S(1)}, u32[]{:S(2)}, u32[]{:S(2)}) async-start(bf16[8,2,128,128]{3,2,1,0:T(8,128)(2,1)} %pad_maximum_fusion.1), calls=%async_computation.2 | async-start | bytes 1048576 | tf_op jit(solution)/shard_map/all_to_all | solution.py:486
  48.0 15.8 %collective-permute-start = (bf16[8,2,136,128]{3,2,1,0:T(8,128)(2,1)S(1)}, bf16[8,2,136,128]{3,2,1,0:T(8,128)(2,1)S(1)}, u32[]{:S(2)}, u32[]{:S(2)}) collective-permute-start(bf16[8,2,136,128]{3,2,1,0:T(8,128)(2,1)S(1)} %all-to-all-done.1.k_own), channel_id=1, source_target_pairs={{0,2},{2,0},{1,3},{3,1},{4,6},{6,4},{5,7},{7,5},{8,10},{10,8},{9,1... | collective-permute-start | bytes 1671176 | tf_op jit(solution)/shard_map/ppermute | solution.py:340
  48.2 15.7 %copy-start.9 = (bf16[136,256]{1,0:T(8,128)(2,1)}, bf16[136,256]{1,0:T(8,128)(2,1)S(1)}, u32[]{:S(2)}) copy-start(bf16[136,256]{1,0:T(8,128)(2,1)S(1)} %pad_maximum_fusion.4.far_own) | copy-start | bytes 208900
  48.2 15.6 %collective-permute-start.1 = (bf16[136,256]{1,0:T(8,128)(2,1)S(1)}, bf16[136,256]{1,0:T(8,128)(2,1)S(1)}, u32[]{:S(2)}, u32[]{:S(2)}) collective-permute-start(bf16[136,256]{1,0:T(8,128)(2,1)S(1)} %pad_maximum_fusion.4.far_own), channel_id=1, source_target_pairs={{0,2},{2,0},{1,3},{3,1},{4,6},{6,4},{5,7},{7,5},{8,10},{10,8},{9,1... | collective-permute-start | bytes 208904 | tf_op jit(solution)/shard_map/ppermute | solution.py:340
  63.8 9.2 %copy-start.8 = (bf16[8,2,128,128]{3,2,1,0:T(8,128)(2,1)}, bf16[8,2,128,128]{3,2,1,0:T(8,128)(2,1)S(1)}, u32[]{:S(2)}) copy-start(bf16[8,2,128,128]{3,2,1,0:T(8,128)(2,1)S(1)} %all-to-all-done.2.v_own) | copy-start | bytes 1572868
  63.8 9.8 %collective-permute-start.2 = (bf16[8,2,128,128]{3,2,1,0:T(8,128)(2,1)S(1)}, bf16[8,2,128,128]{3,2,1,0:T(8,128)(2,1)S(1)}, u32[]{:S(2)}, u32[]{:S(2)}) collective-permute-start(bf16[8,2,128,128]{3,2,1,0:T(8,128)(2,1)S(1)} %all-to-all-done.2.v_own), channel_id=1, source_target_pairs={{0,2},{2,0},{1,3},{3,1},{4,6},{6,4},{5,7},{7,5},{8,10},{10,8},{9,1... | collective-permute-start | bytes 1572872 | tf_op jit(solution)/shard_map/ppermute | solution.py:340
  63.8 0.7 copy-start.11
  63.8 0.9 copy-start.2
  73.0 10.9 %collective-permute-start.11 = (bf16[17,128,128]{2,1,0:T(8,128)(2,1)}, bf16[17,128,128]{2,1,0:T(8,128)(2,1)S(1)}, u32[]{:S(2)}, u32[]{:S(2)}) collective-permute-start(bf16[17,128,128]{2,1,0:T(8,128)(2,1)} %get-tuple-element.19), channel_id=1, source_target_pairs={{0,2},{2,0},{1,3},{3,1},{4,6},{6,4},{5,7},{7,5},{8,10},{10,8},{9,1... | collective-permute-start | bytes 1671176 | tf_op jit(solution)/shard_map/ppermute | solution.py:340
  73.6 0.8 copy-start.10
  74.4 9.5 %copy-start.6 = (f32[17,128,128]{2,1,0:T(8,128)S(1)}, f32[17,128,128]{2,1,0:T(8,128)}, u32[]{:S(2)}) copy-start(f32[17,128,128]{2,1,0:T(8,128)} %get-tuple-element.18) | copy-start | bytes 3342340
  83.8 5.2 %collective-permute-start.3 = (bf16[17,128,128]{2,1,0:T(8,128)(2,1)}, bf16[17,128,128]{2,1,0:T(8,128)(2,1)}, u32[]{:S(2)}, u32[]{:S(2)}) collective-permute-start(bf16[17,128,128]{2,1,0:T(8,128)(2,1)} %get-tuple-element.17), channel_id=1, source_target_pairs={{0,2},{2,0},{1,3},{3,1},{4,6},{6,4},{5,7},{7,5},{8,10},{10,8},{9,1... | collective-permute-start | bytes 1671176 | tf_op jit(solution)/shard_map/ppermute | solution.py:340
  83.9 1.0 copy-start.7
  84.0 5.0 %copy-start.5 = (f32[17,128,128]{2,1,0:T(8,128)S(1)}, f32[17,128,128]{2,1,0:T(8,128)}, u32[]{:S(2)}) copy-start(f32[17,128,128]{2,1,0:T(8,128)} %get-tuple-element.16) | copy-start | bytes 3342340
  84.9 34.4 %all-to-all-start.4 = ((bf16[8,2,128,128]{3,2,1,0:T(8,128)(2,1)}), bf16[8,2,128,128]{3,2,1,0:T(8,128)(2,1)S(1)}, u32[]{:S(2)}, u32[]{:S(2)}) async-start(bf16[8,2,128,128]{3,2,1,0:T(8,128)(2,1)} %bitcast.29), calls=%async_computation.4 | async-start | bytes 1048576 | tf_op jit(solution)/shard_map/all_to_all | solution.py:407
  88.9 27.8 %copy-start.1 = (bf16[8,2,136,128]{3,2,1,0:T(8,128)(2,1)S(1)}, bf16[8,2,136,128]{3,2,1,0:T(8,128)(2,1)}, u32[]{:S(2)}) copy-start(bf16[8,2,136,128]{3,2,1,0:T(8,128)(2,1)} %copy-done) | copy-start | bytes 1671172
  88.9 27.8 %copy-start.3 = (bf16[8,2,136,128]{3,2,1,0:T(8,128)(2,1)S(1)}, bf16[8,2,136,128]{3,2,1,0:T(8,128)(2,1)}, u32[]{:S(2)}) copy-start(bf16[8,2,136,128]{3,2,1,0:T(8,128)(2,1)} %copy-done.2) | copy-start | bytes 1671172
  88.9 27.7 %copy-start.4 = (s32[6]{0:T(128)S(1)}, s32[6]{0:T(128)}, u32[]{:S(2)}) copy-start(s32[6]{0:T(128)} %stack.35.place_ref) | copy-start | bytes 76
  90.9 15.8 %collective-permute-start.10 = (bf16[2,128,128]{2,1,0:T(8,128)(2,1)S(1)}, bf16[2,128,128]{2,1,0:T(8,128)(2,1)S(1)}, u32[]{:S(2)}, u32[]{:S(2)}) collective-permute-start(bf16[2,128,128]{2,1,0:T(8,128)(2,1)S(1)} %get-tuple-element.24), channel_id=1, source_target_pairs={{0,28},{4,0},{8,4},{12,8},{16,12},{20,16},{24,20},{28,24},{1,29},{... | collective-permute-start | bytes 196616 | tf_op jit(solution)/shard_map/ppermute | solution.py:429
  94.1 15.2 %collective-permute-start.4 = (bf16[2,128,128]{2,1,0:T(8,128)(2,1)S(1)}, bf16[2,128,128]{2,1,0:T(8,128)(2,1)S(1)}, u32[]{:S(2)}, u32[]{:S(2)}) collective-permute-start(bf16[2,128,128]{2,1,0:T(8,128)(2,1)S(1)} %get-tuple-element.23), channel_id=1, source_target_pairs={{0,4},{4,8},{8,12},{12,16},{16,20},{20,24},{24,28},{28,0},{1,5},{5... | collective-permute-start | bytes 196616 | tf_op jit(solution)/shard_map/ppermute | solution.py:429
  94.1 23.5 %collective-permute-start.5 = (bf16[2,128,128]{2,1,0:T(8,128)(2,1)}, bf16[2,128,128]{2,1,0:T(8,128)(2,1)S(1)}, u32[]{:S(2)}, u32[]{:S(2)}) collective-permute-start(bf16[2,128,128]{2,1,0:T(8,128)(2,1)} %get-tuple-element.29), channel_id=1, source_target_pairs={{0,8},{4,12},{8,16},{12,20},{16,24},{20,28},{24,0},{28,4},{1,9},{5... | collective-permute-start | bytes 196616 | tf_op jit(solution)/shard_map/ppermute | solution.py:429
  95.8 21.8 %collective-permute-start.6 = (bf16[2,128,128]{2,1,0:T(8,128)(2,1)}, bf16[2,128,128]{2,1,0:T(8,128)(2,1)S(1)}, u32[]{:S(2)}, u32[]{:S(2)}) collective-permute-start(bf16[2,128,128]{2,1,0:T(8,128)(2,1)} %get-tuple-element.28), channel_id=1, source_target_pairs={{0,12},{4,16},{8,20},{12,24},{16,28},{20,0},{24,4},{28,8},{1,13},{... | collective-permute-start | bytes 196616 | tf_op jit(solution)/shard_map/ppermute | solution.py:429
  99.4 18.9 %collective-permute-start.7 = (bf16[2,128,128]{2,1,0:T(8,128)(2,1)}, bf16[2,128,128]{2,1,0:T(8,128)(2,1)S(1)}, u32[]{:S(2)}, u32[]{:S(2)}) collective-permute-start(bf16[2,128,128]{2,1,0:T(8,128)(2,1)} %get-tuple-element.27), channel_id=1, source_target_pairs={{0,16},{4,20},{8,24},{12,28},{16,0},{20,4},{24,8},{28,12},{1,17},{... | collective-permute-start | bytes 196616 | tf_op jit(solution)/shard_map/ppermute | solution.py:429
  106.6 11.7 %collective-permute-start.8 = (bf16[2,128,128]{2,1,0:T(8,128)(2,1)}, bf16[2,128,128]{2,1,0:T(8,128)(2,1)S(1)}, u32[]{:S(2)}, u32[]{:S(2)}) collective-permute-start(bf16[2,128,128]{2,1,0:T(8,128)(2,1)} %get-tuple-element.26), channel_id=1, source_target_pairs={{0,20},{4,24},{8,28},{12,0},{16,4},{20,8},{24,12},{28,16},{1,21},{... | collective-permute-start | bytes 196616 | tf_op jit(solution)/shard_map/ppermute | solution.py:429
  109.3 9.3 %collective-permute-start.9 = (bf16[2,128,128]{2,1,0:T(8,128)(2,1)S(1)}, bf16[2,128,128]{2,1,0:T(8,128)(2,1)S(1)}, u32[]{:S(2)}, u32[]{:S(2)}) collective-permute-start(bf16[2,128,128]{2,1,0:T(8,128)(2,1)S(1)} %get-tuple-element.25), channel_id=1, source_target_pairs={{0,24},{4,28},{8,0},{12,4},{16,8},{20,12},{24,16},{28,20},{1,25},{... | collective-permute-start | bytes 196616 | tf_op jit(solution)/shard_map/ppermute | solution.py:429
  119.4 28.5 %all-to-all-start.3 = ((bf16[64,8,512]{2,1,0:T(8,128)(2,1)}), bf16[64,8,512]{2,1,0:T(8,128)(2,1)S(1)}, u32[]{:S(2)}, u32[]{:S(2)}) async-start(bf16[64,8,512]{2,1,0:T(8,128)(2,1)} %bitcast.25), calls=%async_computation.3 | async-start | bytes 1048576 | tf_op jit(solution)/shard_map/all_to_all | solution.py:599
  132.2 16.7 %collective-permute-start.12 = (f32[128,256]{1,0:T(8,128)S(1)}, f32[128,256]{1,0:T(8,128)S(1)}, u32[]{:S(2)}, u32[]{:S(2)}) collective-permute-start(f32[128,256]{1,0:T(8,128)S(1)} %pad_maximum_fusion.2), channel_id=1, source_target_pairs={{32,0},{64,32},{96,64},{33,1},{65,33},{97,65},{34,2},{66,34},{98,6... | collective-permute-start | bytes 393224 | tf_op jit(solution)/shard_map/ppermute | solution.py:398
  135.6 13.3 %collective-permute-start.13 = (f32[128,256]{1,0:T(8,128)S(1)}, f32[128,256]{1,0:T(8,128)S(1)}, u32[]{:S(2)}, u32[]{:S(2)}) collective-permute-start(f32[128,256]{1,0:T(8,128)S(1)} %pad_maximum_fusion.3), channel_id=1, source_target_pairs={{64,0},{96,32},{65,1},{97,33},{66,2},{98,34},{67,3},{99,35},{68,4}... | collective-permute-start | bytes 393224 | tf_op jit(solution)/shard_map/ppermute | solution.py:399

commit v8 on v7

--- a/solution.py
+++ b/solution.py
@@ -432,7 +432,7 @@
         near = near + got[0].astype(F32)
         mine = mine + jnp.where(z < k, got[1].astype(F32), 0.0)
         far = far + jnp.where(z < k, 0.0, got[1].astype(F32))
-    return mine, near, far, came[zs // 2]
+    return mine, near, far
 
 
 def program(queries, keys, values, outputs, grad_out, doc_ids, owner):
@@ -582,8 +582,8 @@
         owner[None],
         probs,
     )
-    *parts_k, halfway = reduce_by_shifts(dk_own, dk_other, zs, z)
-    parts_v = sum_arrived(lax.optimization_barrier((came_v, halfway))[0], far_v, zs, z)
+    parts_k = reduce_by_shifts(dk_own, dk_other, zs, z)
+    parts_v = sum_arrived(came_v, far_v, zs, z)
     grads = along_x([jnp.concatenate(pair, axis=1) for pair in zip(parts_k, parts_v)], xs)
     grad_k, grad_v = grads[:, None, :hd], grads[:, None, hd:]
 

time: 152 us -> 152 us (level)
  no operation moved by 1% of the time
where the time goes in v8:
time: 152 us; the launch traced here: 150 us
  starting transfers between devices  60.4 us (40%)
  waiting for transfers between devices  55.2 us (36%)
  Pallas kernels  21.3 us (14%)
  other arithmetic  8.36 us (6%)
  local copies, waits for them, and re-layouts  3.24 us (2%)
    all_to_all x2, waiting for transfers between devices, along_z(): return lax.all_to_all(pair, 'z', split_axis=0, concat_axis=0, tiled=True)  30.4 us
    ppermute x7, starting transfers between devices, reduce_by_shifts(): came.append(lax.ppermute(sent, 'z', [(i, (i + k) % zs) for i in range(zs)]))  20.2 us
    all_to_all x2, starting transfers between devices, along_z(): return lax.all_to_all(pair, 'z', split_axis=0, concat_axis=0, tiled=True)  12 us
    all_to_all x1, starting transfers between devices, program(): lax.all_to_all(packed.reshape(peers, 2 * block_len, width // 2), ('x', 'z...  11.8 us
    all_to_all x1, waiting for transfers between devices, program(): lax.all_to_all(packed.reshape(peers, 2 * block_len, width // 2), ('x', 'z...  10.2 us
    pallas_call x1, Pallas kernels, program(): pl.pallas_call(functools.partial(score_kernel, zs=zs, scale=scale, tile=t...  9.37 us
    pallas_call x1, Pallas kernels, program(): pl.pallas_call(functools.partial(softmax_kernel, zs=zs, scale=scale, tile...  8.31 us
    all_to_all x1, waiting for transfers between devices, program(): lax.all_to_all(mixed, ('dp', 'head', 'x'), split_axis=0, concat_axis=0, t...  8.01 us
  transfers between devices with their start and end apart: 19, of which 7 were waited for; matrix products, arithmetic and copies ran while one was open for 5% of the time, Pallas kernels for 13%

profile of v8, /device:TPU:2, one launch (start us, length us, event | category | flops | bytes accessed | tf_op | source)
XLA Modules:
  0.0 149.6 jit_solution(9549892760814644267)
XLA Ops:
  0.6 1.7 %first_payload.1 = bf16[16,40,256]{2,1,0:T(8,128)(2,1)} custom-call(bf16[32,4,128]{2,1,0:T(4,128)(2,1)} %keys_ref.1, bf16[32,4,128]{2,1,0:T(4,128)(2,1)} %values_ref.1, s32[1,128]{1,0:T(1,128)} %bitcast.72, s32[1,32]{1,0:T(1,128)} %bitcast.74), custom_call_target="tpu_custom_call" | custom-call | tf_op jit(solution)/shard_map/first_payload/pallas_call | solution.py:458
  2.3 7.5 %all-to-all-start = ((bf16[16,40,256]{2,1,0:T(8,128)(2,1)}), bf16[16,40,256]{2,1,0:T(8,128)(2,1)S(1)}, u32[]{:S(2)}, u32[]{:S(2)}) async-start(bf16[16,40,256]{2,1,0:T(8,128)(2,1)} %first_payload.1), calls=%async_computation | async-start | bytes 655360 | tf_op jit(solution)/shard_map/all_to_all | solution.py:466
  9.8 8.0 %all-to-all-done = bf16[16,40,256]{2,1,0:T(8,128)(2,1)S(1)} async-done(((bf16[16,40,256]{2,1,0:T(8,128)(2,1)}), bf16[16,40,256]{2,1,0:T(8,128)(2,1)S(1)}, u32[]{:S(2)}, u32[]{:S(2)}) %all-to-all-start) | async-done | bytes 327712 | tf_op jit(solution)/shard_map/all_to_all | solution.py:466
  18.1 0.9 pad_maximum_fusion
  19.0 8.5 %all-to-all-start.1 = ((bf16[8,2,136,128]{3,2,1,0:T(8,128)(2,1)}), bf16[8,2,136,128]{3,2,1,0:T(8,128)(2,1)S(1)}, u32[]{:S(2)}, u32[]{:S(2)}) async-start(bf16[8,2,136,128]{3,2,1,0:T(8,128)(2,1)} %pad_maximum_fusion), calls=%async_computation.1 | async-start | bytes 1114112 | tf_op jit(solution)/shard_map/all_to_all | solution.py:486
  27.6 0.9 pad_maximum_fusion.1
  28.5 16.1 %all-to-all-done.1.k_own = bf16[8,2,136,128]{3,2,1,0:T(8,128)(2,1)S(1)} async-done(((bf16[8,2,136,128]{3,2,1,0:T(8,128)(2,1)}), bf16[8,2,136,128]{3,2,1,0:T(8,128)(2,1)S(1)}, u32[]{:S(2)}, u32[]{:S(2)}) %all-to-all-start.1) | async-done | bytes 557088 | tf_op jit(solution)/shard_map/all_to_all | solution.py:486
  44.5 3.5 %all-to-all-start.2 = ((bf16[8,2,128,128]{3,2,1,0:T(8,128)(2,1)}), bf16[8,2,128,128]{3,2,1,0:T(8,128)(2,1)S(1)}, u32[]{:S(2)}, u32[]{:S(2)}) async-start(bf16[8,2,128,128]{3,2,1,0:T(8,128)(2,1)} %pad_maximum_fusion.1), calls=%async_computation.2 | async-start | bytes 1048576 | tf_op jit(solution)/shard_map/all_to_all | solution.py:486
  49.4 14.4 %all-to-all-done.2.v_own = bf16[8,2,128,128]{3,2,1,0:T(8,128)(2,1)S(1)} async-done(((bf16[8,2,128,128]{3,2,1,0:T(8,128)(2,1)}), bf16[8,2,128,128]{3,2,1,0:T(8,128)(2,1)S(1)}, u32[]{:S(2)}, u32[]{:S(2)}) %all-to-all-start.2) | async-done | bytes 524320 | tf_op jit(solution)/shard_map/all_to_all | solution.py:486
  64.7 8.3 %softmax_and_value_gradient.1 = (f32[17,128,128]{2,1,0:T(8,128)}, bf16[17,128,128]{2,1,0:T(8,128)(2,1)}, f32[9,512,1024]{2,1,0:T(8,128)}, s32[1]{0:T(128)}, f32[9,8,1024]{2,1,0:T(8,128)}) custom-call(s32[6]{0:T(128)} %stack.35.place_ref, bf16[128,1024]{1,0:T(8,128)(2,1)} %bitcast.76, bf16[128,1024]{1,0:T(8,128)(2,1)} %bitcast.78, s32[1,128]{1,0:T(1,128)} %bitcast.73, ...), custom_call_target="tpu_custom_call" | custom-call | flops 12000000000 | bytes 20000000 | tf_op jit(solution)/shard_map/softmax_and_value_gradient/pallas_call | solution.py:504
  73.6 0.8 copy-done.10
  74.4 9.4 %score_gradient.1 = (bf16[512,512]{1,0:T(8,128)(2,1)}, f32[17,128,128]{2,1,0:T(8,128)}, bf16[17,128,128]{2,1,0:T(8,128)(2,1)}) custom-call(s32[6]{0:T(128)} %stack.35.place_ref, s32[1]{0:T(128)} %get-tuple-element.11.info_ref, bf16[128,1024]{1,0:T(8,128)(2,1)} %bitcast.77, bf16[128,1024]{1,0:T(8,128)(2,1)} %bitcast.79, bf16[128,1024]{1,0:T(8,128)(2,1)} %bitcast.80, ...), custom_call_target="tpu_custom_call" | custom-call | flops 12000000000 | bytes 20000000 | tf_op jit(solution)/shard_map/score_gradient/pallas_call | solution.py:542
  84.0 0.9 add_convert_fusion
  84.9 4.0 %all-to-all-start.4 = ((bf16[8,2,128,128]{3,2,1,0:T(8,128)(2,1)}), bf16[8,2,128,128]{3,2,1,0:T(8,128)(2,1)S(1)}, u32[]{:S(2)}, u32[]{:S(2)}) async-start(bf16[8,2,128,128]{3,2,1,0:T(8,128)(2,1)} %bitcast.29), calls=%async_computation.4 | async-start | bytes 1048576 | tf_op jit(solution)/shard_map/all_to_all | solution.py:407
  89.0 1.9 %add_convert_fusion.7 = (bf16[2,128,128]{2,1,0:T(8,128)(2,1)S(1)}, bf16[2,128,128]{2,1,0:T(8,128)(2,1)S(1)}, bf16[2,128,128]{2,1,0:T(8,128)(2,1)S(1)}, bf16[2,12...) fusion(f32[17,128,128]{2,1,0:T(8,128)S(1)} %copy-done.5, ...), kind=kLoop, calls=%fused_computation.20 | loop fusion | flops 688128 | bytes 1835008 | tf_op jit(solution)/shard_map/convert_element_type | solution.py:428
  90.9 3.2 %collective-permute-start.10 = (bf16[2,128,128]{2,1,0:T(8,128)(2,1)S(1)}, bf16[2,128,128]{2,1,0:T(8,128)(2,1)S(1)}, u32[]{:S(2)}, u32[]{:S(2)}) collective-permute-start(bf16[2,128,128]{2,1,0:T(8,128)(2,1)S(1)} %get-tuple-element.22), channel_id=1, source_target_pairs={{0,28},{4,0},{8,4},{12,8},{16,12},{20,16},{24,20},{28,24},{1,29},{... | collective-permute-start | bytes 196616 | tf_op jit(solution)/shard_map/ppermute | solution.py:429
  94.1 1.7 %collective-permute-start.5 = (bf16[2,128,128]{2,1,0:T(8,128)(2,1)}, bf16[2,128,128]{2,1,0:T(8,128)(2,1)S(1)}, u32[]{:S(2)}, u32[]{:S(2)}) collective-permute-start(bf16[2,128,128]{2,1,0:T(8,128)(2,1)} %get-tuple-element.27), channel_id=1, source_target_pairs={{0,8},{4,12},{8,16},{12,20},{16,24},{20,28},{24,0},{28,4},{1,9},{5... | collective-permute-start | bytes 196616 | tf_op jit(solution)/shard_map/ppermute | solution.py:429
  95.8 3.6 %collective-permute-start.6 = (bf16[2,128,128]{2,1,0:T(8,128)(2,1)}, bf16[2,128,128]{2,1,0:T(8,128)(2,1)S(1)}, u32[]{:S(2)}, u32[]{:S(2)}) collective-permute-start(bf16[2,128,128]{2,1,0:T(8,128)(2,1)} %get-tuple-element.26), channel_id=1, source_target_pairs={{0,12},{4,16},{8,20},{12,24},{16,28},{20,0},{24,4},{28,8},{1,13},{... | collective-permute-start | bytes 196616 | tf_op jit(solution)/shard_map/ppermute | solution.py:429
  99.4 1.6 %collective-permute-start.7 = (bf16[2,128,128]{2,1,0:T(8,128)(2,1)}, bf16[2,128,128]{2,1,0:T(8,128)(2,1)S(1)}, u32[]{:S(2)}, u32[]{:S(2)}) collective-permute-start(bf16[2,128,128]{2,1,0:T(8,128)(2,1)} %get-tuple-element.25), channel_id=1, source_target_pairs={{0,16},{4,20},{8,24},{12,28},{16,0},{20,4},{24,8},{28,12},{1,17},{... | collective-permute-start | bytes 196616 | tf_op jit(solution)/shard_map/ppermute | solution.py:429
  101.0 5.6 %collective-permute-done.10 = bf16[2,128,128]{2,1,0:T(8,128)(2,1)S(1)} collective-permute-done((bf16[2,128,128]{2,1,0:T(8,128)(2,1)S(1)}, bf16[2,128,128]{2,1,0:T(8,128)(2,1)S(1)}, u32[]{:S(2)}, u32[]{:S(2)}) %collective-permute-start.10) | collective-permute-done | bytes 65568 | tf_op jit(solution)/shard_map/ppermute | solution.py:429
  106.6 2.7 %collective-permute-start.8 = (bf16[2,128,128]{2,1,0:T(8,128)(2,1)}, bf16[2,128,128]{2,1,0:T(8,128)(2,1)S(1)}, u32[]{:S(2)}, u32[]{:S(2)}) collective-permute-start(bf16[2,128,128]{2,1,0:T(8,128)(2,1)} %get-tuple-element.24), channel_id=1, source_target_pairs={{0,20},{4,24},{8,28},{12,0},{16,4},{20,8},{24,12},{28,16},{1,21},{... | collective-permute-start | bytes 196616 | tf_op jit(solution)/shard_map/ppermute | solution.py:429
  109.3 7.4 %collective-permute-start.9 = (bf16[2,128,128]{2,1,0:T(8,128)(2,1)S(1)}, bf16[2,128,128]{2,1,0:T(8,128)(2,1)S(1)}, u32[]{:S(2)}, u32[]{:S(2)}) collective-permute-start(bf16[2,128,128]{2,1,0:T(8,128)(2,1)S(1)} %get-tuple-element.23), channel_id=1, source_target_pairs={{0,24},{4,28},{8,0},{12,4},{16,8},{20,12},{24,16},{28,20},{1,25},{... | collective-permute-start | bytes 196616 | tf_op jit(solution)/shard_map/ppermute | solution.py:429
  116.7 0.9 placement_choice.1.pick_ref
  118.6 0.8 add_bitcast_fusion
  119.4 11.8 %all-to-all-start.3 = ((bf16[64,8,512]{2,1,0:T(8,128)(2,1)}), bf16[64,8,512]{2,1,0:T(8,128)(2,1)S(1)}, u32[]{:S(2)}, u32[]{:S(2)}) async-start(bf16[64,8,512]{2,1,0:T(8,128)(2,1)} %bitcast.25), calls=%async_computation.3 | async-start | bytes 1048576 | tf_op jit(solution)/shard_map/all_to_all | solution.py:599
  131.2 0.8 fusion.18
  132.2 2.4 %collective-permute-start.12 = (f32[128,256]{1,0:T(8,128)S(1)}, f32[128,256]{1,0:T(8,128)S(1)}, u32[]{:S(2)}, u32[]{:S(2)}) collective-permute-start(f32[128,256]{1,0:T(8,128)S(1)} %pad_maximum_fusion.2), channel_id=1, source_target_pairs={{32,0},{64,32},{96,64},{33,1},{65,33},{97,65},{34,2},{66,34},{98,6... | collective-permute-start | bytes 393224 | tf_op jit(solution)/shard_map/ppermute | solution.py:398
  134.7 0.9 bitcast_add_fusion
  135.6 1.3 collective-permute-start.13
  136.9 0.8 fusion.10
  137.7 10.2 %all-to-all-done.3 = bf16[64,8,512]{2,1,0:T(8,128)(2,1)S(1)} async-done(((bf16[64,8,512]{2,1,0:T(8,128)(2,1)}), bf16[64,8,512]{2,1,0:T(8,128)(2,1)S(1)}, u32[]{:S(2)}, u32[]{:S(2)}) %all-to-all-start.3) | async-done | bytes 524320 | tf_op jit(solution)/shard_map/all_to_all | solution.py:599
  147.9 1.0 query_gradient_placement.1
  (73 shorter events, 5.3 us)
Async XLA Ops:
  2.3 15.5 %all-to-all-start = ((bf16[16,40,256]{2,1,0:T(8,128)(2,1)}), bf16[16,40,256]{2,1,0:T(8,128)(2,1)S(1)}, u32[]{:S(2)}, u32[]{:S(2)}) async-start(bf16[16,40,256]{2,1,0:T(8,128)(2,1)} %first_payload.1), calls=%async_computation | async-start | bytes 655360 | tf_op jit(solution)/shard_map/all_to_all | solution.py:466
  19.0 25.6 %all-to-all-start.1 = ((bf16[8,2,136,128]{3,2,1,0:T(8,128)(2,1)}), bf16[8,2,136,128]{3,2,1,0:T(8,128)(2,1)S(1)}, u32[]{:S(2)}, u32[]{:S(2)}) async-start(bf16[8,2,136,128]{3,2,1,0:T(8,128)(2,1)} %pad_maximum_fusion), calls=%async_computation.1 | async-start | bytes 1114112 | tf_op jit(solution)/shard_map/all_to_all | solution.py:486
  44.5 19.3 %copy-start = (bf16[8,2,136,128]{3,2,1,0:T(8,128)(2,1)}, bf16[8,2,136,128]{3,2,1,0:T(8,128)(2,1)S(1)}, u32[]{:S(2)}) copy-start(bf16[8,2,136,128]{3,2,1,0:T(8,128)(2,1)S(1)} %all-to-all-done.1.k_own) | copy-start | bytes 1671172
  44.5 19.2 %all-to-all-start.2 = ((bf16[8,2,128,128]{3,2,1,0:T(8,128)(2,1)}), bf16[8,2,128,128]{3,2,1,0:T(8,128)(2,1)S(1)}, u32[]{:S(2)}, u32[]{:S(2)}) async-start(bf16[8,2,128,128]{3,2,1,0:T(8,128)(2,1)} %pad_maximum_fusion.1), calls=%async_computation.2 | async-start | bytes 1048576 | tf_op jit(solution)/shard_map/all_to_all | solution.py:486
  48.0 15.8 %collective-permute-start = (bf16[8,2,136,128]{3,2,1,0:T(8,128)(2,1)S(1)}, bf16[8,2,136,128]{3,2,1,0:T(8,128)(2,1)S(1)}, u32[]{:S(2)}, u32[]{:S(2)}) collective-permute-start(bf16[8,2,136,128]{3,2,1,0:T(8,128)(2,1)S(1)} %all-to-all-done.1.k_own), channel_id=1, source_target_pairs={{0,2},{2,0},{1,3},{3,1},{4,6},{6,4},{5,7},{7,5},{8,10},{10,8},{9,1... | collective-permute-start | bytes 1671176 | tf_op jit(solution)/shard_map/ppermute | solution.py:340
  48.2 15.7 %copy-start.9 = (bf16[136,256]{1,0:T(8,128)(2,1)}, bf16[136,256]{1,0:T(8,128)(2,1)S(1)}, u32[]{:S(2)}) copy-start(bf16[136,256]{1,0:T(8,128)(2,1)S(1)} %pad_maximum_fusion.4.far_own) | copy-start | bytes 208900
  48.2 15.6 %collective-permute-start.1 = (bf16[136,256]{1,0:T(8,128)(2,1)S(1)}, bf16[136,256]{1,0:T(8,128)(2,1)S(1)}, u32[]{:S(2)}, u32[]{:S(2)}) collective-permute-start(bf16[136,256]{1,0:T(8,128)(2,1)S(1)} %pad_maximum_fusion.4.far_own), channel_id=1, source_target_pairs={{0,2},{2,0},{1,3},{3,1},{4,6},{6,4},{5,7},{7,5},{8,10},{10,8},{9,1... | collective-permute-start | bytes 208904 | tf_op jit(solution)/shard_map/ppermute | solution.py:340
  63.8 9.2 %copy-start.8 = (bf16[8,2,128,128]{3,2,1,0:T(8,128)(2,1)}, bf16[8,2,128,128]{3,2,1,0:T(8,128)(2,1)S(1)}, u32[]{:S(2)}) copy-start(bf16[8,2,128,128]{3,2,1,0:T(8,128)(2,1)S(1)} %all-to-all-done.2.v_own) | copy-start | bytes 1572868
  63.8 9.8 %collective-permute-start.2 = (bf16[8,2,128,128]{3,2,1,0:T(8,128)(2,1)S(1)}, bf16[8,2,128,128]{3,2,1,0:T(8,128)(2,1)S(1)}, u32[]{:S(2)}, u32[]{:S(2)}) collective-permute-start(bf16[8,2,128,128]{3,2,1,0:T(8,128)(2,1)S(1)} %all-to-all-done.2.v_own), channel_id=1, source_target_pairs={{0,2},{2,0},{1,3},{3,1},{4,6},{6,4},{5,7},{7,5},{8,10},{10,8},{9,1... | collective-permute-start | bytes 1572872 | tf_op jit(solution)/shard_map/ppermute | solution.py:340
  63.8 0.7 copy-start.11
  63.8 0.9 copy-start.2
  73.0 10.9 %collective-permute-start.11 = (bf16[17,128,128]{2,1,0:T(8,128)(2,1)}, bf16[17,128,128]{2,1,0:T(8,128)(2,1)S(1)}, u32[]{:S(2)}, u32[]{:S(2)}) collective-permute-start(bf16[17,128,128]{2,1,0:T(8,128)(2,1)} %get-tuple-element.18), channel_id=1, source_target_pairs={{0,2},{2,0},{1,3},{3,1},{4,6},{6,4},{5,7},{7,5},{8,10},{10,8},{9,1... | collective-permute-start | bytes 1671176 | tf_op jit(solution)/shard_map/ppermute | solution.py:340
  73.6 0.8 copy-start.10
  74.4 9.5 %copy-start.6 = (f32[17,128,128]{2,1,0:T(8,128)S(1)}, f32[17,128,128]{2,1,0:T(8,128)}, u32[]{:S(2)}) copy-start(f32[17,128,128]{2,1,0:T(8,128)} %get-tuple-element.17) | copy-start | bytes 3342340
  83.8 5.2 %collective-permute-start.3 = (bf16[17,128,128]{2,1,0:T(8,128)(2,1)}, bf16[17,128,128]{2,1,0:T(8,128)(2,1)}, u32[]{:S(2)}, u32[]{:S(2)}) collective-permute-start(bf16[17,128,128]{2,1,0:T(8,128)(2,1)} %get-tuple-element.16), channel_id=1, source_target_pairs={{0,2},{2,0},{1,3},{3,1},{4,6},{6,4},{5,7},{7,5},{8,10},{10,8},{9,1... | collective-permute-start | bytes 1671176 | tf_op jit(solution)/shard_map/ppermute | solution.py:340
  83.9 1.0 copy-start.7
  84.0 5.0 %copy-start.5 = (f32[17,128,128]{2,1,0:T(8,128)S(1)}, f32[17,128,128]{2,1,0:T(8,128)}, u32[]{:S(2)}) copy-start(f32[17,128,128]{2,1,0:T(8,128)} %get-tuple-element.15) | copy-start | bytes 3342340
  84.9 34.4 %all-to-all-start.4 = ((bf16[8,2,128,128]{3,2,1,0:T(8,128)(2,1)}), bf16[8,2,128,128]{3,2,1,0:T(8,128)(2,1)S(1)}, u32[]{:S(2)}, u32[]{:S(2)}) async-start(bf16[8,2,128,128]{3,2,1,0:T(8,128)(2,1)} %bitcast.29), calls=%async_computation.4 | async-start | bytes 1048576 | tf_op jit(solution)/shard_map/all_to_all | solution.py:407
  88.9 27.8 %copy-start.1 = (bf16[8,2,136,128]{3,2,1,0:T(8,128)(2,1)S(1)}, bf16[8,2,136,128]{3,2,1,0:T(8,128)(2,1)}, u32[]{:S(2)}) copy-start(bf16[8,2,136,128]{3,2,1,0:T(8,128)(2,1)} %copy-done) | copy-start | bytes 1671172
  88.9 27.8 %copy-start.3 = (bf16[8,2,136,128]{3,2,1,0:T(8,128)(2,1)S(1)}, bf16[8,2,136,128]{3,2,1,0:T(8,128)(2,1)}, u32[]{:S(2)}) copy-start(bf16[8,2,136,128]{3,2,1,0:T(8,128)(2,1)} %copy-done.2) | copy-start | bytes 1671172
  88.9 27.7 %copy-start.4 = (s32[6]{0:T(128)S(1)}, s32[6]{0:T(128)}, u32[]{:S(2)}) copy-start(s32[6]{0:T(128)} %stack.35.place_ref) | copy-start | bytes 76
  90.9 15.8 %collective-permute-start.10 = (bf16[2,128,128]{2,1,0:T(8,128)(2,1)S(1)}, bf16[2,128,128]{2,1,0:T(8,128)(2,1)S(1)}, u32[]{:S(2)}, u32[]{:S(2)}) collective-permute-start(bf16[2,128,128]{2,1,0:T(8,128)(2,1)S(1)} %get-tuple-element.22), channel_id=1, source_target_pairs={{0,28},{4,0},{8,4},{12,8},{16,12},{20,16},{24,20},{28,24},{1,29},{... | collective-permute-start | bytes 196616 | tf_op jit(solution)/shard_map/ppermute | solution.py:429
  94.1 15.2 %collective-permute-start.4 = (bf16[2,128,128]{2,1,0:T(8,128)(2,1)S(1)}, bf16[2,128,128]{2,1,0:T(8,128)(2,1)S(1)}, u32[]{:S(2)}, u32[]{:S(2)}) collective-permute-start(bf16[2,128,128]{2,1,0:T(8,128)(2,1)S(1)} %get-tuple-element.21), channel_id=1, source_target_pairs={{0,4},{4,8},{8,12},{12,16},{16,20},{20,24},{24,28},{28,0},{1,5},{5... | collective-permute-start | bytes 196616 | tf_op jit(solution)/shard_map/ppermute | solution.py:429
  94.1 23.5 %collective-permute-start.5 = (bf16[2,128,128]{2,1,0:T(8,128)(2,1)}, bf16[2,128,128]{2,1,0:T(8,128)(2,1)S(1)}, u32[]{:S(2)}, u32[]{:S(2)}) collective-permute-start(bf16[2,128,128]{2,1,0:T(8,128)(2,1)} %get-tuple-element.27), channel_id=1, source_target_pairs={{0,8},{4,12},{8,16},{12,20},{16,24},{20,28},{24,0},{28,4},{1,9},{5... | collective-permute-start | bytes 196616 | tf_op jit(solution)/shard_map/ppermute | solution.py:429
  95.8 21.8 %collective-permute-start.6 = (bf16[2,128,128]{2,1,0:T(8,128)(2,1)}, bf16[2,128,128]{2,1,0:T(8,128)(2,1)S(1)}, u32[]{:S(2)}, u32[]{:S(2)}) collective-permute-start(bf16[2,128,128]{2,1,0:T(8,128)(2,1)} %get-tuple-element.26), channel_id=1, source_target_pairs={{0,12},{4,16},{8,20},{12,24},{16,28},{20,0},{24,4},{28,8},{1,13},{... | collective-permute-start | bytes 196616 | tf_op jit(solution)/shard_map/ppermute | solution.py:429
  99.4 18.9 %collective-permute-start.7 = (bf16[2,128,128]{2,1,0:T(8,128)(2,1)}, bf16[2,128,128]{2,1,0:T(8,128)(2,1)S(1)}, u32[]{:S(2)}, u32[]{:S(2)}) collective-permute-start(bf16[2,128,128]{2,1,0:T(8,128)(2,1)} %get-tuple-element.25), channel_id=1, source_target_pairs={{0,16},{4,20},{8,24},{12,28},{16,0},{20,4},{24,8},{28,12},{1,17},{... | collective-permute-start | bytes 196616 | tf_op jit(solution)/shard_map/ppermute | solution.py:429
  106.6 11.7 %collective-permute-start.8 = (bf16[2,128,128]{2,1,0:T(8,128)(2,1)}, bf16[2,128,128]{2,1,0:T(8,128)(2,1)S(1)}, u32[]{:S(2)}, u32[]{:S(2)}) collective-permute-start(bf16[2,128,128]{2,1,0:T(8,128)(2,1)} %get-tuple-element.24), channel_id=1, source_target_pairs={{0,20},{4,24},{8,28},{12,0},{16,4},{20,8},{24,12},{28,16},{1,21},{... | collective-permute-start | bytes 196616 | tf_op jit(solution)/shard_map/ppermute | solution.py:429
  109.3 9.3 %collective-permute-start.9 = (bf16[2,128,128]{2,1,0:T(8,128)(2,1)S(1)}, bf16[2,128,128]{2,1,0:T(8,128)(2,1)S(1)}, u32[]{:S(2)}, u32[]{:S(2)}) collective-permute-start(bf16[2,128,128]{2,1,0:T(8,128)(2,1)S(1)} %get-tuple-element.23), channel_id=1, source_target_pairs={{0,24},{4,28},{8,0},{12,4},{16,8},{20,12},{24,16},{28,20},{1,25},{... | collective-permute-start | bytes 196616 | tf_op jit(solution)/shard_map/ppermute | solution.py:429
  119.4 28.5 %all-to-all-start.3 = ((bf16[64,8,512]{2,1,0:T(8,128)(2,1)}), bf16[64,8,512]{2,1,0:T(8,128)(2,1)S(1)}, u32[]{:S(2)}, u32[]{:S(2)}) async-start(bf16[64,8,512]{2,1,0:T(8,128)(2,1)} %bitcast.25), calls=%async_computation.3 | async-start | bytes 1048576 | tf_op jit(solution)/shard_map/all_to_all | solution.py:599
  132.2 16.7 %collective-permute-start.12 = (f32[128,256]{1,0:T(8,128)S(1)}, f32[128,256]{1,0:T(8,128)S(1)}, u32[]{:S(2)}, u32[]{:S(2)}) collective-permute-start(f32[128,256]{1,0:T(8,128)S(1)} %pad_maximum_fusion.2), channel_id=1, source_target_pairs={{32,0},{64,32},{96,64},{33,1},{65,33},{97,65},{34,2},{66,34},{98,6... | collective-permute-start | bytes 393224 | tf_op jit(solution)/shard_map/ppermute | solution.py:398
  135.6 13.3 %collective-permute-start.13 = (f32[128,256]{1,0:T(8,128)S(1)}, f32[128,256]{1,0:T(8,128)S(1)}, u32[]{:S(2)}, u32[]{:S(2)}) collective-permute-start(f32[128,256]{1,0:T(8,128)S(1)} %pad_maximum_fusion.3), channel_id=1, source_target_pairs={{64,0},{96,32},{65,1},{97,33},{66,2},{98,34},{67,3},{99,35},{68,4}... | collective-permute-start | bytes 393224 | tf_op jit(solution)/shard_map/ppermute | solution.py:399
